TPU v7x, 32 devices: a whole 2x2x4 slice. The times are simulated.
32 devices in a mesh: port: 4 (over x, core), fac: 4 (over z), scen: 2 (over y).
Axes of the slice: x: 2, y: 2, z: 4, core: 2. Of those that a mesh axis runs over, the one named last changes fastest.
Arguments:
- shocks: bfloat16 [4096, 16384], P(('port', 'scen'), 'fac'), may hold values from -6 to 6
- loading: bfloat16 [16384, 8192], P('fac', 'port'), may hold values from -0.046875 to 0.046875
- thresholds: float32 [64, 8192], P(None, 'port'), may hold values from -1 to 3.5
- weights: bfloat16 [4096], P(('port', 'scen')), may hold values from 0.5 to 5, as said below
Outputs:
- mean_excess: float32 [64, 8192], P(None, 'port')
- tail_prob: float32 [64, 8192], P(None, 'port')
Inputs may be any that keep to these rules, and one draw needn't show every extreme that they name: Positive weights.
All inputs are finite; a program needn't handle non-finite values.
Results may differ from a plain program's by a relative error of at most 0.008.
Values may be sent and summed in bfloat16 or wider, within the bound.
No kernel may reach another device: no remote copies, remote signals or barrier semaphores. Data moves between devices by JAX's collectives and lax.ppermute only.
A program may use at most 128 MiB of HBM per device.

v0:
```python
import jax
import jax.numpy as jnp
from jax import lax
from jax.sharding import PartitionSpec as P

smooth_width = 0.05


def sums_rows(losses, levels, scen_weights):
    width = levels.shape[1]

    def block(limits):
        diff = losses[None, :, :] - limits[:, None, :]
        weighted = scen_weights[None, :, None] * jax.nn.sigmoid(diff / smooth_width)
        return (jnp.sum(weighted, axis=1), jnp.sum(weighted * diff, axis=1))

    count, excess = lax.map(block, levels.reshape(-1, 8, width))
    return (count.reshape(-1, width), excess.reshape(-1, width))


def per_device(shocks, loading, thresholds, weights):
    fac_count = lax.axis_size("fac")
    fac_index = lax.axis_index("fac")
    gathered, group_weights = (
        lax.all_gather(shocks, "port", axis=0, tiled=True),
        lax.all_gather(weights, "port", axis=0, tiled=True),
    )
    group_rows = gathered.shape[0]
    local_rows = group_rows // fac_count
    losses = lax.psum_scatter(
        jnp.dot(gathered, loading, preferred_element_type=jnp.float32),
        "fac",
        scatter_dimension=0,
        tiled=True,
    )
    own_weights = lax.dynamic_slice_in_dim(
        group_weights, fac_index * local_rows, local_rows, 0
    ).astype(jnp.float32)
    count, excess = sums_rows(losses, thresholds, own_weights)
    count, excess, total = lax.psum((count, excess, jnp.sum(own_weights)), ("fac", "scen"))
    return (excess / jnp.maximum(count, 1.0), count / total)


def solution(mesh):
    placed = (P(("port", "scen"), "fac"), P("fac", "port"), P(None, "port"), P(("port", "scen")))
    return jax.shard_map(
        per_device,
        mesh=mesh,
        in_specs=placed,
        out_specs=(P(None, "port"), P(None, "port")),
        check_vma=False,
    )
```

profile of v0, /device:TPU:8, one launch (start us, length us, event | category | flops | bytes accessed | tf_op | source)
XLA Modules:
  0.0 653.6 jit_solution(9818000232970721348)
XLA Ops:
  7.2 0.7 all-gather.3.cloned.1.call-update
  7.9 108.7 %all-gather.3.cloned.1.call-done = bf16[2048,4096]{1,0:T(8,128)(2,1)} async-done(((bf16[512,4096]{1,0:T(8,128)(2,1)}), bf16[2048,4096]{1,0:T(8,128)(2,1)}) %all-gather.3.cloned.1.call-update) | async-done | bytes 16777232 | tf_op jit(solution)/shard_map/all_gather | solution.py:25
  116.7 43.0 %fusion.8 = f32[2048,2048]{1,0:T(8,128)} fusion(bf16[2048,4096]{1,0:T(8,128)(2,1)} %all-gather.3.cloned.1.call-done, bf16[4096,2048]{1,0:T(8,128)(2,1)} %param.7), kind=kOutput, calls=%fused_computation.16 | convolution fusion | flops 34359738368 | bytes 50331648 | tf_op jit(solution)/shard_map/dot_general | solution.py:31
  160.3 5.1 all-gather
  165.6 271.4 %reduce-scatter.2.cloned.1.call-done = f32[512,2048]{1,0:T(8,128)} async-done(((f32[2048,2048]{1,0:T(8,128)}), f32[512,2048]{1,0:T(8,128)}) %reduce-scatter.2.cloned.1.call-update) | async-done | bytes 4194320 | tf_op jit(solution)/shard_map/reduce_scatter | solution.py:30
  436.9 124.2 %while.12 = (s32[]{:T(128)}, f32[8,8,2048]{2,1,0:T(8,128)S(1)}, f32[8,8,2048]{2,1,0:T(8,128)}, f32[512]{0:T(512)S(1)}, f32[512,2048]{1,0:T(8,128)}, /*index=5*/f32[8,8,2048]{2,1,0:T(8,128)}, s32[]{:T(128)}) while((s32[]{:T(128)}, f32[8,8,2048]{2,1,0:T(8,128)S(1)}, f32[8,8,2048]{2,1,0:T(8,128)}, f32[512]{0:T(512)S(1)}, f32[512,2048]{1,0:T(8,128)}, ...), condition=%wide.region_4.5_spmd, body=%wide.region_1.4_spmd.sunk | while | flops 75464704 | bytes 4786269 | solution.py:17
  436.9 0.8 dynamic-slice_bitcast_fusion.2
  437.8 14.0 %fusion.12 = (f32[8,2048]{1,0:T(8,128)S(1)}, f32[8,2048]{1,0:T(8,128)S(1)}) fusion(f32[8,2048]{1,0:T(8,128)S(1)} %dynamic-slice_bitcast_fusion.2, f32[512,2048]{1,0:T(8,128)} %get-tuple-element.120, f32[512]{0:T(512)S(1)} %get-tuple-element.119), kind=kLoop, calls=%fused_computation.7.clone.1 | loop fusion | flops 75464704 | bytes 4392960 | tf_op jit(solution)/shard_map/while/body/eval_jaxpr/reduce_sum | solution.py:15
  451.8 0.6 bitcast_dynamic-update-slice_fusion.3
  452.5 0.8 dynamic-slice_bitcast_fusion.2
  453.3 14.0 %fusion.12 = (f32[8,2048]{1,0:T(8,128)S(1)}, f32[8,2048]{1,0:T(8,128)S(1)}) fusion(f32[8,2048]{1,0:T(8,128)S(1)} %dynamic-slice_bitcast_fusion.2, f32[512,2048]{1,0:T(8,128)} %get-tuple-element.120, f32[512]{0:T(512)S(1)} %get-tuple-element.119), kind=kLoop, calls=%fused_computation.7.clone.1 | loop fusion | flops 75464704 | bytes 4392960 | tf_op jit(solution)/shard_map/while/body/eval_jaxpr/reduce_sum | solution.py:15
  467.3 0.6 bitcast_dynamic-update-slice_fusion.3
  468.0 0.8 dynamic-slice_bitcast_fusion.2
  468.8 14.0 %fusion.12 = (f32[8,2048]{1,0:T(8,128)S(1)}, f32[8,2048]{1,0:T(8,128)S(1)}) fusion(f32[8,2048]{1,0:T(8,128)S(1)} %dynamic-slice_bitcast_fusion.2, f32[512,2048]{1,0:T(8,128)} %get-tuple-element.120, f32[512]{0:T(512)S(1)} %get-tuple-element.119), kind=kLoop, calls=%fused_computation.7.clone.1 | loop fusion | flops 75464704 | bytes 4392960 | tf_op jit(solution)/shard_map/while/body/eval_jaxpr/reduce_sum | solution.py:15
  482.9 0.6 bitcast_dynamic-update-slice_fusion.3
  483.5 0.8 dynamic-slice_bitcast_fusion.2
  484.4 14.0 %fusion.12 = (f32[8,2048]{1,0:T(8,128)S(1)}, f32[8,2048]{1,0:T(8,128)S(1)}) fusion(f32[8,2048]{1,0:T(8,128)S(1)} %dynamic-slice_bitcast_fusion.2, f32[512,2048]{1,0:T(8,128)} %get-tuple-element.120, f32[512]{0:T(512)S(1)} %get-tuple-element.119), kind=kLoop, calls=%fused_computation.7.clone.1 | loop fusion | flops 75464704 | bytes 4392960 | tf_op jit(solution)/shard_map/while/body/eval_jaxpr/reduce_sum | solution.py:15
  498.4 0.6 bitcast_dynamic-update-slice_fusion.3
  499.0 0.8 dynamic-slice_bitcast_fusion.2
  499.9 14.0 %fusion.12 = (f32[8,2048]{1,0:T(8,128)S(1)}, f32[8,2048]{1,0:T(8,128)S(1)}) fusion(f32[8,2048]{1,0:T(8,128)S(1)} %dynamic-slice_bitcast_fusion.2, f32[512,2048]{1,0:T(8,128)} %get-tuple-element.120, f32[512]{0:T(512)S(1)} %get-tuple-element.119), kind=kLoop, calls=%fused_computation.7.clone.1 | loop fusion | flops 75464704 | bytes 4392960 | tf_op jit(solution)/shard_map/while/body/eval_jaxpr/reduce_sum | solution.py:15
  513.9 0.6 bitcast_dynamic-update-slice_fusion.3
  514.5 0.8 dynamic-slice_bitcast_fusion.2
  515.4 14.0 %fusion.12 = (f32[8,2048]{1,0:T(8,128)S(1)}, f32[8,2048]{1,0:T(8,128)S(1)}) fusion(f32[8,2048]{1,0:T(8,128)S(1)} %dynamic-slice_bitcast_fusion.2, f32[512,2048]{1,0:T(8,128)} %get-tuple-element.120, f32[512]{0:T(512)S(1)} %get-tuple-element.119), kind=kLoop, calls=%fused_computation.7.clone.1 | loop fusion | flops 75464704 | bytes 4392960 | tf_op jit(solution)/shard_map/while/body/eval_jaxpr/reduce_sum | solution.py:15
  530.1 0.8 dynamic-slice_bitcast_fusion.2
  530.9 14.0 %fusion.12 = (f32[8,2048]{1,0:T(8,128)S(1)}, f32[8,2048]{1,0:T(8,128)S(1)}) fusion(f32[8,2048]{1,0:T(8,128)S(1)} %dynamic-slice_bitcast_fusion.2, f32[512,2048]{1,0:T(8,128)} %get-tuple-element.120, f32[512]{0:T(512)S(1)} %get-tuple-element.119), kind=kLoop, calls=%fused_computation.7.clone.1 | loop fusion | flops 75464704 | bytes 4392960 | tf_op jit(solution)/shard_map/while/body/eval_jaxpr/reduce_sum | solution.py:15
  545.6 0.8 dynamic-slice_bitcast_fusion.2
  546.4 14.0 %fusion.12 = (f32[8,2048]{1,0:T(8,128)S(1)}, f32[8,2048]{1,0:T(8,128)S(1)}) fusion(f32[8,2048]{1,0:T(8,128)S(1)} %dynamic-slice_bitcast_fusion.2, f32[512,2048]{1,0:T(8,128)} %get-tuple-element.120, f32[512]{0:T(512)S(1)} %get-tuple-element.119), kind=kLoop, calls=%fused_computation.7.clone.1 | loop fusion | flops 75464704 | bytes 4392960 | tf_op jit(solution)/shard_map/while/body/eval_jaxpr/reduce_sum | solution.py:15
  561.1 0.8 copy-done
  561.9 0.8 fusion.7
  562.7 22.6 %psum.23 = f32[]{:T(128)} all-reduce(f32[]{:T(128)} %fusion.7), channel_id=1, replica_groups=mesh['port'=4,'fac'=4,'scen'=2] {'fac','scen'}, use_global_device_ids=true, to_apply=%region_8.9 | all-reduce | flops 1 | bytes 8 | tf_op jit(solution)/shard_map/psum | solution.py:40
  585.2 58.8 %all-reduce.3.cloned.1.call-done = (f32[64,2048]{1,0:T(8,128)}, f32[64,2048]{1,0:T(8,128)}) async-done(((f32[64,2048]{1,0:T(8,128)}, f32[64,2048]{1,0:T(8,128)}), (f32[64,2048]{1,0:T(8,128)}, f32[64,2048]{1,0:T(8,128)})) %all-reduce.3.cloned.1.call-update) | async-done | bytes 1048592 | tf_op jit(solution)/shard_map/psum | solution.py:40
  644.1 2.9 broadcast_divide_fusion
  (17 shorter events, 2.8 us)
Async XLA Ops:
  7.2 109.5 %all-gather.3.cloned.1.call-start = ((), (), s32[]{:S(2)}) async-start(), calls=%async_computation.1 | async-start | bytes 20971520 | tf_op jit(solution)/shard_map/all_gather | solution.py:25
  7.9 429.1 %reduce-scatter.2.cloned.1.call-start = ((), (), s32[]{:S(2)}) async-start(), calls=%async_computation.2 | async-start | bytes 20971520 | tf_op jit(solution)/shard_map/reduce_scatter | solution.py:30
  159.6 0.7 copy-start.1
  159.7 484.4 %all-reduce.3.cloned.1.call-start = ((), (), s32[]{:S(2)}) async-start(), calls=%async_computation.3 | async-start | bytes 2097152 | tf_op jit(solution)/shard_map/psum | solution.py:40
  561.1 0.8 copy-start
Sparse Core Ops, SparseCore 0:
  9.6 107.0 all-gather.2
  159.8 277.1 reduce-scatter.1
  562.0 82.0 all-reduce.2
where the time goes:
time: 656 us; the launch traced here: 654 us
  waiting for transfers between devices  440 us (67%)
  other arithmetic  116 us (18%)
  matrix products  43 us (7%)
  blocking collectives  27.7 us (4%)
  between operations  13.8 us (2%)
  local copies, waits for them, and re-layouts  13.3 us (2%)
    reduce_scatter x1, waiting for transfers between devices, per_device(): lax.psum_scatter(jnp.dot(gathered, loading, preferred_element_type=jnp.fl...  271 us
    reduce_sum x8, other arithmetic, block(): return (jnp.sum(weighted, axis=1), jnp.sum(weighted * diff, axis=1))  112 us
    all_gather x1, waiting for transfers between devices, per_device(): lax.all_gather(shocks, 'port', axis=0, tiled=True)  109 us
    psum x1, waiting for transfers between devices, per_device(): lax.psum((count, excess, jnp.sum(own_weights)), ('fac', 'scen'))  58.8 us
    dot_general x1, matrix products, per_device(): jnp.dot(gathered, loading, preferred_element_type=jnp.float32)  43 us
    psum x1, blocking collectives, per_device(): lax.psum((count, excess, jnp.sum(own_weights)), ('fac', 'scen'))  22.6 us
  transfers between devices with their start and end apart: 3, of which 3 were waited for; matrix products, arithmetic and copies ran while one was open for 0% of the time, Pallas kernels for 0%

commit v1 on v0

--- a/solution.py
+++ b/solution.py
@@ -1,9 +1,181 @@
+import functools
+
 import jax
 import jax.numpy as jnp
 from jax import lax
+from jax.experimental import pallas as pl
+from jax.experimental.pallas import tpu as pltpu
 from jax.sharding import PartitionSpec as P
 
 smooth_width = 0.05
+half_inverse = 0.5 / smooth_width
+lane_block = 256
+row_block = 256
+level_group = 8
+
+
+def tail_body(count_own, losses, levels, weights, count_in, excess_in, count_out, excess_out):
+    rows = losses.shape[0]
+    groups = levels.shape[0] // level_group
+    bf16 = jnp.bfloat16
+
+    @pl.when(pl.program_id(0) < count_own[0])
+    def _():
+        which = lax.broadcasted_iota(jnp.int32, (level_group, row_block), 0)
+
+        def group(at, carry):
+            span = pl.ds(pl.multiple_of(at * level_group, level_group), level_group)
+            limits = levels[span, :]
+            count = count_in[span, :]
+            excess = excess_in[span, :]
+            for start in range(0, rows, row_block):
+                row_weights = weights[:, pl.ds(start, row_block)]
+                for level in range(level_group):
+                    picked = jnp.where(which == level, row_weights, jnp.zeros_like(row_weights))
+                    limit = jnp.broadcast_to(limits[level : level + 1, :], (32, lane_block))
+                    smooth, products = [], []
+                    for row in range(start, start + row_block, 32):
+                        diff = (losses[pl.ds(row, 32), :] - limit).astype(bf16)
+                        twice = jnp.tanh(diff) + bf16(1)
+                        smooth.append(twice)
+                        products.append(twice * diff)
+                    count = count + jnp.dot(
+                        picked, jnp.concatenate(smooth, 0), preferred_element_type=jnp.float32
+                    )
+                    excess = excess + jnp.dot(
+                        picked, jnp.concatenate(products, 0), preferred_element_type=jnp.float32
+                    )
+            count_out[span, :] = count
+            excess_out[span, :] = excess
+            return carry
+
+        lax.fori_loop(0, groups, group, 0)
+
+
+def tail_sums(count_own, losses, levels, weights, count, excess):
+    rows, width = losses.shape
+    depth = levels.shape[0]
+    table = pl.BlockSpec((depth, lane_block), lambda i, own: (0, i))
+    return pl.pallas_call(
+        tail_body,
+        out_shape=[jax.ShapeDtypeStruct((depth, width), jnp.float32)] * 2,
+        grid_spec=pltpu.PrefetchScalarGridSpec(
+            num_scalar_prefetch=1,
+            grid=(width // lane_block,),
+            in_specs=[
+                pl.BlockSpec((rows, lane_block), lambda i, own: (0, i)),
+                table,
+                pl.BlockSpec((8, rows), lambda i, own: (0, 0)),
+                table,
+                table,
+            ],
+            out_specs=[table, table],
+        ),
+        input_output_aliases={4: 0, 5: 1},
+        cost_estimate=pl.CostEstimate(
+            flops=rows * width * depth * 8,
+            transcendentals=rows * width * depth,
+            bytes_accessed=rows * width * 4 + depth * width * 20,
+        ),
+        name="tail_sums",
+    )(count_own, losses, levels, weights, count, excess)
+
+
+def pipelined(shocks, loading, thresholds, weights):
+    rows = shocks.shape[0]
+    width = loading.shape[1]
+    half = width // 2
+    owned = 3 * half // 4
+    link, f32 = jnp.float16, jnp.float32
+    place = lax.axis_index("fac")
+    at_end = (place == 0) | (place == 3)
+    upper = (place >= 2).astype(jnp.int32)
+
+    def exchange_core(v):
+        return lax.ppermute(v, "port", [(0, 1), (1, 0), (2, 3), (3, 2)])
+
+    def exchange_chip(v):
+        return lax.ppermute(v, "port", [(0, 2), (2, 0), (1, 3), (3, 1)])
+
+    def halves(v, k):
+        return lax.dynamic_slice_in_dim(v, k * half, half, 1)
+
+    def own_part(v):
+        return jnp.where(at_end, v[:, :owned], jnp.pad(v[:, owned:], ((0, 0), (0, 2 * owned - half))))
+
+    weights_pair = jnp.stack([weights, exchange_core(weights)])
+    weights_far = exchange_chip(weights_pair)
+    group_total = jnp.sum(weights_pair.astype(f32)) + jnp.sum(weights_far.astype(f32))
+    total = group_total + lax.ppermute(group_total, "scen", [(0, 1), (1, 0)])
+
+    piece = rows // 4
+    far = []
+    for k in range(4):
+        got = exchange_chip(shocks[k * piece : (k + 1) * piece])
+        far.append((got, exchange_core(got)))
+    sibling = exchange_core(shocks)
+    blocks = [
+        (shocks, weights_pair[0]),
+        (sibling, weights_pair[1]),
+    ]
+    for k in range(4):
+        part = slice(k * piece, (k + 1) * piece)
+        blocks.append((jnp.concatenate(far[k], 0), weights_far[:, part].reshape(-1)))
+
+    limits = own_part(halves(thresholds, upper)) * half_inverse
+    count_own = jnp.where(at_end, owned // lane_block, (half - owned) // lane_block).astype(jnp.int32).reshape(1)
+    count = jnp.zeros((limits.shape[0], owned), f32)
+    excess = jnp.zeros((limits.shape[0], owned), f32)
+    for block, block_weights in blocks:
+        partial = (jnp.dot(block, loading, preferred_element_type=f32) * half_inverse).astype(link)
+        away = halves(partial, 1 - upper)
+        near = halves(partial, upper)
+        first = lax.ppermute(
+            jnp.concatenate([away, near[:, owned:]], 1), "fac", [(0, 1), (3, 2)]
+        )
+        passed = (away.astype(f32) + first[:, :half].astype(f32)).astype(link)
+        second = lax.ppermute(passed, "fac", [(1, 2), (2, 1)])
+        near = near.astype(f32) + second.astype(f32)
+        third = lax.ppermute(near[:, :owned].astype(link), "fac", [(1, 0), (2, 3)])
+        losses = own_part(near) + jnp.where(
+            at_end,
+            third,
+            jnp.pad(first[:, half:], ((0, 0), (0, 2 * owned - half))),
+        ).astype(f32)
+        spread = jnp.broadcast_to(block_weights[None], (8, block_weights.shape[0]))
+        count, excess = tail_sums(count_own, losses, limits, spread, count, excess)
+
+    sums = jnp.concatenate([count * 0.5, excess * (0.5 / half_inverse)], 0)
+    sums = sums + lax.ppermute(sums, "scen", [(0, 1), (1, 0)])
+    depth = limits.shape[0]
+    count, excess = sums[:depth], sums[depth:]
+    result = jnp.concatenate([excess / jnp.maximum(count, 1.0), count / total], 0)
+    ends = [result] + [
+        lax.ppermute(result, "fac", pairs)
+        for pairs in ([(0, 1), (3, 2)], [(0, 2), (3, 1)], [(0, 3), (3, 0)])
+    ]
+    inner = result[:, : half - owned]
+    mids = [inner] + [
+        lax.ppermute(inner, "fac", pairs)
+        for pairs in ([(1, 0), (2, 3)], [(1, 2), (2, 1)], [(1, 3), (2, 0)])
+    ]
+
+    def choose(parts, order):
+        out = parts[order[3]]
+        for k in (2, 1, 0):
+            out = jnp.where(place == k, parts[order[k]], out)
+        return out
+
+    full = jnp.concatenate(
+        [
+            choose(ends, (0, 1, 2, 3)),
+            choose(mids, (1, 0, 2, 3)),
+            choose(ends, (3, 2, 1, 0)),
+            choose(mids, (3, 2, 0, 1)),
+        ],
+        1,
+    )
+    return full[:depth], full[depth:]
 
 
 def sums_rows(losses, levels, scen_weights):
@@ -18,15 +190,14 @@
     return (count.reshape(-1, width), excess.reshape(-1, width))
 
 
-def per_device(shocks, loading, thresholds, weights):
+def plain(shocks, loading, thresholds, weights):
     fac_count = lax.axis_size("fac")
     fac_index = lax.axis_index("fac")
     gathered, group_weights = (
         lax.all_gather(shocks, "port", axis=0, tiled=True),
         lax.all_gather(weights, "port", axis=0, tiled=True),
     )
-    group_rows = gathered.shape[0]
-    local_rows = group_rows // fac_count
+    local_rows = gathered.shape[0] // fac_count
     losses = lax.psum_scatter(
         jnp.dot(gathered, loading, preferred_element_type=jnp.float32),
         "fac",
@@ -39,6 +210,19 @@
     count, excess = sums_rows(losses, thresholds, own_weights)
     count, excess, total = lax.psum((count, excess, jnp.sum(own_weights)), ("fac", "scen"))
     return (excess / jnp.maximum(count, 1.0), count / total)
+
+
+def per_device(shocks, loading, thresholds, weights):
+    sizes = tuple(lax.axis_size(name) for name in ("port", "fac", "scen"))
+    fits = (
+        sizes == (4, 4, 2)
+        and shocks.shape[0] % 512 == 0
+        and loading.shape[1] % 2048 == 0
+        and thresholds.shape[0] % level_group == 0
+    )
+    if fits:
+        return pipelined(shocks, loading, thresholds, weights)
+    return plain(shocks, loading, thresholds, weights)
 
 
 def solution(mesh):

time: 656 us -> 388 us (0.59)
  waiting for transfers between devices: 440 us -> 118 us
  starting transfers between devices: 0.12 us -> 111 us
  other arithmetic: 116 us -> 27.3 us
  Pallas kernels: 0 us -> 40.7 us
  blocking collectives: 27.7 us -> 0 us
  matrix products: 43 us -> 68.9 us
  between operations: 13.8 us -> 3.7 us
    reduce_scatter x1 -> x0, waiting for transfers between devices: 271 us -> none  [per_device(): lax.psum_scatter(jnp.dot(gathered, loading, preferred_element_type=jnp.fl...]
    ppermute x0 -> x37, waiting for transfers between devices: none -> 118 us  [the longest x5 66.1 us: exchange_chip(): return lax.ppermute(v, 'port', [(0, 2), (2, 0), (1, 3), (3, 1)])]
    reduce_sum x9 -> x2, other arithmetic: 113 us -> 1.27 us  [the longest x1 0.67 us: pipelined(): jnp.sum(weights_pair.astype(f32)) + jnp.sum(weights_far.astype(f32))]
    ppermute x0 -> x37, starting transfers between devices: none -> 111 us  [the longest x3 44.2 us: pipelined(): lax.ppermute(inner, 'fac', pairs)]
    all_gather x1 -> x0, waiting for transfers between devices: 109 us -> none  [per_device(): lax.all_gather(shocks, 'port', axis=0, tiled=True)]
    psum x1 -> x0, waiting for transfers between devices: 58.8 us -> none  [per_device(): lax.psum((count, excess, jnp.sum(own_weights)), ('fac', 'scen'))]
    pallas_call x0 -> x6, Pallas kernels: none -> 40.7 us  [tail_sums(): pl.pallas_call(tail_body, out_shape=[jax.ShapeDtypeStruct((depth, width),...]
    dot_general x1 -> x6, matrix products: 43 us -> 68.9 us  [pipelined(): jnp.dot(block, loading, preferred_element_type=f32) * half_inverse]
  transfers between devices with their start and end apart: 3 -> 37, of which waited for: 3 -> 12; matrix products, arithmetic and copies ran while one was open for 0% -> 26% of each run, Pallas kernels for 0% -> 2%
where the time goes in v1:
time: 388 us; the launch traced here: 384 us
  waiting for transfers between devices  118 us (30%)
  starting transfers between devices  111 us (29%)
  matrix products  68.9 us (18%)
  Pallas kernels  40.7 us (10%)
  other arithmetic  27.3 us (7%)
  local copies, waits for them, and re-layouts  13.7 us (4%)
    dot_general x6, matrix products, pipelined(): jnp.dot(block, loading, preferred_element_type=f32) * half_inverse  68.9 us
    ppermute x5, waiting for transfers between devices, exchange_chip(): return lax.ppermute(v, 'port', [(0, 2), (2, 0), (1, 3), (3, 1)])  66.1 us
    ppermute x3, starting transfers between devices, pipelined(): lax.ppermute(inner, 'fac', pairs)  44.2 us
    pallas_call x6, Pallas kernels, tail_sums(): pl.pallas_call(tail_body, out_shape=[jax.ShapeDtypeStruct((depth, width),...  40.7 us
    ppermute x6, starting transfers between devices, pipelined(): third = lax.ppermute(near[:, :owned].astype(link), 'fac', [(1, 0), (2, 3)])  25.9 us
    ppermute x6, starting transfers between devices, pipelined(): second = lax.ppermute(passed, 'fac', [(1, 2), (2, 1)])  17.8 us
    ppermute x6, waiting for transfers between devices, pipelined(): second = lax.ppermute(passed, 'fac', [(1, 2), (2, 1)])  15.9 us
    ppermute x3, waiting for transfers between devices, pipelined(): lax.ppermute(inner, 'fac', pairs)  14 us
  transfers between devices with their start and end apart: 37, of which 12 were waited for; matrix products, arithmetic and copies ran while one was open for 26% of the time, Pallas kernels for 2%

profile of v1, /device:TPU:8, one launch (start us, length us, event | category | flops | bytes accessed | tf_op | source)
XLA Modules:
  0.0 383.5 jit_solution(10059960696540980374)
XLA Ops:
  0.6 4.4 %fusion.23 = (bf16[128,4096]{1,0:T(8,128)(2,1)}, bf16[128,4096]{1,0:T(8,128)(2,1)}, bf16[128,4096]{1,0:T(8,128)(2,1)}, bf16[128,4096]{1,0:T(8,128)(2,1)}) fusion(bf16[512,4096]{1,0:T(8,128)(2,1)} %param.4), kind=kLoop, calls=%fused_computation.93 | loop fusion | bytes 8388608 | tf_op jit(solution)/shard_map/slice | solution.py:114
  6.5 13.6 %multiply_convert_fusion = f16[512,2048]{1,0:T(8,128)(2,1)S(1)} fusion(bf16[512,4096]{1,0:T(8,128)(2,1)} %param.4, bf16[4096,2048]{1,0:T(8,128)(2,1)} %param.5), kind=kOutput, calls=%fused_computation | convolution fusion | flops 8592031744 | bytes 23068672 | tf_op jit(solution)/shard_map/dot_general | solution.py:130
  27.6 3.8 collective-permute-done.6
  35.3 18.5 %collective-permute-done.12 = bf16[128,4096]{1,0:T(8,128)(2,1)} collective-permute-done((bf16[128,4096]{1,0:T(8,128)(2,1)}, bf16[128,4096]{1,0:T(8,128)(2,1)}, u32[]{:S(2)}, u32[]{:S(2)}) %collective-permute-start.12) | collective-permute-done | bytes 1048608 | tf_op jit(solution)/shard_map/ppermute | solution.py:98
  53.9 22.5 %collective-permute-done.7 = bf16[128,4096]{1,0:T(8,128)(2,1)} collective-permute-done((bf16[128,4096]{1,0:T(8,128)(2,1)}, bf16[128,4096]{1,0:T(8,128)(2,1)}, u32[]{:S(2)}, u32[]{:S(2)}) %collective-permute-start.7) | collective-permute-done | bytes 1048608 | tf_op jit(solution)/shard_map/ppermute | solution.py:98
  76.3 21.3 %collective-permute-done = bf16[128,4096]{1,0:T(8,128)(2,1)} collective-permute-done((bf16[128,4096]{1,0:T(8,128)(2,1)}, bf16[128,4096]{1,0:T(8,128)(2,1)}, u32[]{:S(2)}, u32[]{:S(2)}) %collective-permute-start) | collective-permute-done | bytes 1048608 | tf_op jit(solution)/shard_map/ppermute | solution.py:98
  98.5 3.5 collective-permute-start.27
  102.0 10.9 %fusion.3 = f16[256,2048]{1,0:T(8,128)(2,1)S(1)} fusion(bf16[4096,2048]{1,0:T(8,128)(2,1)} %param.5, bf16[128,4096]{1,0:T(8,128)(2,1)} %collective-permute-done.18, bf16[128,4096]{1,0:T(8,128)(2,1)} %collective-permute-done.17), kind=kOutput, calls=%fused_computation.9 | convolution fusion | flops 4300210176 | bytes 19922944 | tf_op jit(solution)/shard_map/dot_general | solution.py:130
  114.8 10.6 %fusion.2 = f16[256,2048]{1,0:T(8,128)(2,1)S(1)} fusion(bf16[4096,2048]{1,0:T(8,128)(2,1)} %param.5, bf16[128,4096]{1,0:T(8,128)(2,1)S(1)} %collective-permute-done.13, bf16[128,4096]{1,0:T(8,128)(2,1)} %collective-permute-done.12), kind=kOutput, calls=%fused_computation.8 | convolution fusion | flops 4300210176 | bytes 19922944 | tf_op jit(solution)/shard_map/dot_general | solution.py:130
  127.1 10.6 %fusion.1 = f16[256,2048]{1,0:T(8,128)(2,1)S(1)} fusion(bf16[4096,2048]{1,0:T(8,128)(2,1)} %param.5, bf16[128,4096]{1,0:T(8,128)(2,1)S(1)} %collective-permute-done.8, bf16[128,4096]{1,0:T(8,128)(2,1)} %collective-permute-done.7), kind=kOutput, calls=%fused_computation.7 | convolution fusion | flops 4300210176 | bytes 19922944 | tf_op jit(solution)/shard_map/dot_general | solution.py:130
  139.3 10.6 %fusion = f16[256,2048]{1,0:T(8,128)(2,1)S(1)} fusion(bf16[4096,2048]{1,0:T(8,128)(2,1)} %param.5, bf16[128,4096]{1,0:T(8,128)(2,1)S(1)} %collective-permute-done.1, bf16[128,4096]{1,0:T(8,128)(2,1)} %collective-permute-done), kind=kOutput, calls=%fused_computation.6 | convolution fusion | flops 4300210176 | bytes 19922944 | tf_op jit(solution)/shard_map/dot_general | solution.py:130
  152.2 4.8 %collective-permute-start.28 = (f16[512,768]{1,0:T(8,128)(2,1)S(1)}, f16[512,768]{1,0:T(8,128)(2,1)S(1)}, u32[]{:S(2)}, u32[]{:S(2)}) collective-permute-start(f16[512,768]{1,0:T(8,128)(2,1)S(1)} %slice_convert_fusion), channel_id=1, source_target_pairs={{2,0},{4,6},{3,1},{5,7},{10,8},{12,14},{11,9},{13,15},{18,16},{20,... | collective-permute-start | bytes 2359304 | tf_op jit(solution)/shard_map/ppermute | solution.py:139
  158.0 2.6 collective-permute-start.20
  161.5 3.5 collective-permute-start.15
  166.0 7.8 %collective-permute-done.2 = f16[256,1280]{1,0:T(8,128)(2,1)S(1)} collective-permute-done((f16[256,1280]{1,0:T(8,128)(2,1)S(1)}, f16[256,1280]{1,0:T(8,128)(2,1)S(1)}, u32[]{:S(2)}, u32[]{:S(2)}) %collective-permute-start.2) | collective-permute-done | bytes 655392 | tf_op jit(solution)/shard_map/ppermute | solution.py:133
  177.1 3.5 collective-permute-start.3
  180.6 12.6 %multiply_convert_fusion.1 = f16[512,2048]{1,0:T(8,128)(2,1)S(1)} fusion(bf16[512,4096]{1,0:T(8,128)(2,1)S(1)} %collective-permute-done.22, bf16[4096,2048]{1,0:T(8,128)(2,1)} %param.5), kind=kOutput, calls=%fused_computation.1 | convolution fusion | flops 8592031744 | bytes 23068672 | tf_op jit(solution)/shard_map/dot_general | solution.py:130
  199.8 8.4 %tail_sums.6 = (f32[64,768]{1,0:T(8,128)}, f32[64,768]{1,0:T(8,128)}) custom-call(s32[1]{0:T(128)} %bitcast.count_own, f32[512,768]{1,0:T(8,128)} %convert_add_fusion.2.losses, f32[64,768]{1,0:T(8,128)} %fusion.16.levels, bf16[8,512]{1,0:T(8,128)(2,1)} %broadcast_in_dim.47.weights, ...), custom_call_target="tpu_custom_call", output_to_operand_aliasing={{0}: (4, {}), {1}: (5, {})} | custom-call | flops 201326592 | bytes 2555904 | tf_op jit(solution)/shard_map/tail_sums/pallas_call | solution.py:59
  209.7 15.2 %collective-permute-start.21 = (f16[256,768]{1,0:T(8,128)(2,1)S(1)}, f16[256,768]{1,0:T(8,128)(2,1)S(1)}, u32[]{:S(2)}, u32[]{:S(2)}) collective-permute-start(f16[256,768]{1,0:T(8,128)(2,1)S(1)} %slice_convert_fusion.2), channel_id=1, source_target_pairs={{2,0},{4,6},{3,1},{5,7},{10,8},{12,14},{11,9},{13,15},{18,16},{20,... | collective-permute-start | bytes 1179656 | tf_op jit(solution)/shard_map/ppermute | solution.py:139
  229.3 2.5 collective-permute-start.24
  238.4 15.9 %collective-permute-done.24 = f16[512,1024]{1,0:T(8,128)(2,1)S(1)} collective-permute-done((f16[512,1024]{1,0:T(8,128)(2,1)S(1)}, f16[512,1024]{1,0:T(8,128)(2,1)S(1)}, u32[]{:S(2)}, u32[]{:S(2)}) %collective-permute-start.24) | collective-permute-done | bytes 1048608 | tf_op jit(solution)/shard_map/ppermute | solution.py:137
  261.8 11.9 %collective-permute-done.25 = f16[512,768]{1,0:T(8,128)(2,1)S(1)} collective-permute-done((f16[512,768]{1,0:T(8,128)(2,1)S(1)}, f16[512,768]{1,0:T(8,128)(2,1)S(1)}, u32[]{:S(2)}, u32[]{:S(2)}) %collective-permute-start.25) | collective-permute-done | bytes 786464 | tf_op jit(solution)/shard_map/ppermute | solution.py:139
  275.7 8.4 %tail_sums.7 = (f32[64,768]{1,0:T(8,128)}, f32[64,768]{1,0:T(8,128)}) custom-call(s32[1]{0:T(128)} %bitcast.count_own, f32[512,768]{1,0:T(8,128)} %convert_add_fusion.3.losses, f32[64,768]{1,0:T(8,128)} %fusion.16.levels, bf16[8,512]{1,0:T(8,128)(2,1)} %broadcast_in_dim.46.weights, ...), custom_call_target="tpu_custom_call", output_to_operand_aliasing={{0}: (4, {}), {1}: (5, {})} | custom-call | flops 201326592 | bytes 2555904 | tf_op jit(solution)/shard_map/tail_sums/pallas_call | solution.py:59
  284.7 6.0 %tail_sums.8 = (f32[64,768]{1,0:T(8,128)}, f32[64,768]{1,0:T(8,128)}) custom-call(s32[1]{0:T(128)} %bitcast.count_own, f32[256,768]{1,0:T(8,128)} %convert_add_fusion.8.losses, f32[64,768]{1,0:T(8,128)} %fusion.16.levels, bf16[8,256]{1,0:T(8,128)(2,1)} %broadcast_in_dim.45.weights, ...), custom_call_target="tpu_custom_call", output_to_operand_aliasing={{0}: (4, {}), {1}: (5, {})} | custom-call | flops 100663296 | bytes 1769472 | tf_op jit(solution)/shard_map/tail_sums/pallas_call | solution.py:59
  291.3 6.0 %tail_sums.9 = (f32[64,768]{1,0:T(8,128)}, f32[64,768]{1,0:T(8,128)}) custom-call(s32[1]{0:T(128)} %bitcast.count_own, f32[256,768]{1,0:T(8,128)} %convert_add_fusion.9.losses, f32[64,768]{1,0:T(8,128)} %fusion.16.levels, bf16[8,256]{1,0:T(8,128)(2,1)} %broadcast_in_dim.43.weights, ...), custom_call_target="tpu_custom_call", output_to_operand_aliasing={{0}: (4, {}), {1}: (5, {})} | custom-call | flops 100663296 | bytes 1769472 | tf_op jit(solution)/shard_map/tail_sums/pallas_call | solution.py:59
  297.8 6.0 %tail_sums.10 = (f32[64,768]{1,0:T(8,128)}, f32[64,768]{1,0:T(8,128)}) custom-call(s32[1]{0:T(128)} %bitcast.count_own, f32[256,768]{1,0:T(8,128)} %convert_add_fusion.10.losses, f32[64,768]{1,0:T(8,128)} %fusion.16.levels, bf16[8,256]{1,0:T(8,128)(2,1)} %broadcast_in_dim.41.weights, ...), custom_call_target="tpu_custom_call", output_to_operand_aliasing={{0}: (4, {}), {1}: (5, {})} | custom-call | flops 100663296 | bytes 1769472 | tf_op jit(solution)/shard_map/tail_sums/pallas_call | solution.py:59
  304.4 6.0 %tail_sums.11 = (f32[64,768]{1,0:T(8,128)}, f32[64,768]{1,0:T(8,128)}) custom-call(s32[1]{0:T(128)} %bitcast.count_own, f32[256,768]{1,0:T(8,128)} %convert_add_fusion.11.losses, f32[64,768]{1,0:T(8,128)} %fusion.16.levels, bf16[8,256]{1,0:T(8,128)(2,1)} %broadcast_in_dim.39.weights, ...), custom_call_target="tpu_custom_call", output_to_operand_aliasing={{0}: (4, {}), {1}: (5, {})} | custom-call | flops 100663296 | bytes 1769472 | tf_op jit(solution)/shard_map/tail_sums/pallas_call | solution.py:59
  314.9 4.0 %collective-permute-start.30 = (f32[]{:T(128)}, f32[]{:T(128)}, u32[]{:S(2)}, u32[]{:S(2)}) collective-permute-start(f32[]{:T(128)} %add.124), channel_id=1, source_target_pairs={{0,1},{1,0},{2,3},{3,2},{4,5},{5,4},{6,7},{7,6},{8,9},{9,8},{10,11... | collective-permute-start | bytes 20 | tf_op jit(solution)/shard_map/ppermute | solution.py:109
  320.6 35.3 %collective-permute-start.34 = (f32[128,256]{1,0:T(8,128)S(1)}, f32[128,256]{1,0:T(8,128)S(1)}, u32[]{:S(2)}, u32[]{:S(2)}) collective-permute-start(f32[128,256]{1,0:T(8,128)S(1)} %fusion.17), channel_id=1, source_target_pairs={{2,0},{4,6},{3,1},{5,7},{10,8},{12,14},{11,9},{13,15},{18,16},{20,... | collective-permute-start | bytes 393224 | tf_op jit(solution)/shard_map/ppermute | solution.py:159
  359.3 2.4 collective-permute-start.35
  361.7 6.5 %collective-permute-start.36 = (f32[128,256]{1,0:T(8,128)S(1)}, f32[128,256]{1,0:T(8,128)S(1)}, u32[]{:S(2)}, u32[]{:S(2)}) collective-permute-start(f32[128,256]{1,0:T(8,128)S(1)} %fusion.17), channel_id=1, source_target_pairs={{2,6},{4,0},{3,7},{5,1},{10,14},{12,8},{11,15},{13,9},{18,22},{20,... | collective-permute-start | bytes 393224 | tf_op jit(solution)/shard_map/ppermute | solution.py:159
  369.5 12.7 %collective-permute-done.36 = f32[128,256]{1,0:T(8,128)S(1)} collective-permute-done((f32[128,256]{1,0:T(8,128)S(1)}, f32[128,256]{1,0:T(8,128)S(1)}, u32[]{:S(2)}, u32[]{:S(2)}) %collective-permute-start.36) | collective-permute-done | bytes 131104 | tf_op jit(solution)/shard_map/ppermute | solution.py:159
  (186 shorter events, 68.0 us)
Async XLA Ops:
  5.0 27.9 %collective-permute-start.17 = (bf16[128,4096]{1,0:T(8,128)(2,1)}, bf16[128,4096]{1,0:T(8,128)(2,1)}, u32[]{:S(2)}, u32[]{:S(2)}) collective-permute-start(bf16[128,4096]{1,0:T(8,128)(2,1)} %get-tuple-element.28), channel_id=1, source_target_pairs={{0,16},{16,0},{8,24},{24,8},{1,17},{17,1},{9,25},{25,9},{2,18},{18... | collective-permute-start | bytes 3145736 | tf_op jit(solution)/shard_map/ppermute | solution.py:98
  21.9 75.8 %collective-permute-start.26 = (f16[512,1280]{1,0:T(8,128)(2,1)}, f16[512,1280]{1,0:T(8,128)(2,1)S(1)}, u32[]{:S(2)}, u32[]{:S(2)}) collective-permute-start(f16[512,1280]{1,0:T(8,128)(2,1)} %pad_maximum_fusion.1), channel_id=1, source_target_pairs={{0,2},{6,4},{1,3},{7,5},{8,10},{14,12},{9,11},{15,13},{16,18},{22,... | collective-permute-start | bytes 3932168 | tf_op jit(solution)/shard_map/ppermute | solution.py:133
  25.6 28.3 %collective-permute-start.12 = (bf16[128,4096]{1,0:T(8,128)(2,1)}, bf16[128,4096]{1,0:T(8,128)(2,1)}, u32[]{:S(2)}, u32[]{:S(2)}) collective-permute-start(bf16[128,4096]{1,0:T(8,128)(2,1)} %get-tuple-element.29), channel_id=1, source_target_pairs={{0,16},{16,0},{8,24},{24,8},{1,17},{17,1},{9,25},{25,9},{2,18},{18... | collective-permute-start | bytes 3145736 | tf_op jit(solution)/shard_map/ppermute | solution.py:98
  27.1 49.3 %collective-permute-start.7 = (bf16[128,4096]{1,0:T(8,128)(2,1)}, bf16[128,4096]{1,0:T(8,128)(2,1)}, u32[]{:S(2)}, u32[]{:S(2)}) collective-permute-start(bf16[128,4096]{1,0:T(8,128)(2,1)} %get-tuple-element.30), channel_id=1, source_target_pairs={{0,16},{16,0},{8,24},{24,8},{1,17},{17,1},{9,25},{25,9},{2,18},{18... | collective-permute-start | bytes 3145736 | tf_op jit(solution)/shard_map/ppermute | solution.py:98
  31.4 66.3 %collective-permute-start = (bf16[128,4096]{1,0:T(8,128)(2,1)}, bf16[128,4096]{1,0:T(8,128)(2,1)}, u32[]{:S(2)}, u32[]{:S(2)}) collective-permute-start(bf16[128,4096]{1,0:T(8,128)(2,1)} %get-tuple-element.31), channel_id=1, source_target_pairs={{0,16},{16,0},{8,24},{24,8},{1,17},{17,1},{9,25},{25,9},{2,18},{18... | collective-permute-start | bytes 3145736 | tf_op jit(solution)/shard_map/ppermute | solution.py:98
  32.9 65.7 %collective-permute-start.18 = (bf16[128,4096]{1,0:T(8,128)(2,1)}, bf16[128,4096]{1,0:T(8,128)(2,1)}, u32[]{:S(2)}, u32[]{:S(2)}) collective-permute-start(bf16[128,4096]{1,0:T(8,128)(2,1)} %collective-permute-done.17), channel_id=1, source_target_pairs={{0,8},{8,0},{16,24},{24,16},{1,9},{9,1},{17,25},{25,17},{2,10},{10... | collective-permute-start | bytes 3145736 | tf_op jit(solution)/shard_map/ppermute | solution.py:95
  53.9 123.2 %collective-permute-start.22 = (bf16[512,4096]{1,0:T(8,128)(2,1)}, bf16[512,4096]{1,0:T(8,128)(2,1)S(1)}, u32[]{:S(2)}, u32[]{:S(2)}) collective-permute-start(bf16[512,4096]{1,0:T(8,128)(2,1)} %param.4), channel_id=1, source_target_pairs={{0,8},{8,0},{16,24},{24,16},{1,9},{9,1},{17,25},{25,17},{2,10},{10... | collective-permute-start | bytes 12582920 | tf_op jit(solution)/shard_map/ppermute | solution.py:95
  76.3 37.0 %collective-permute-start.13 = (bf16[128,4096]{1,0:T(8,128)(2,1)}, bf16[128,4096]{1,0:T(8,128)(2,1)S(1)}, u32[]{:S(2)}, u32[]{:S(2)}) collective-permute-start(bf16[128,4096]{1,0:T(8,128)(2,1)} %collective-permute-done.12), channel_id=1, source_target_pairs={{0,8},{8,0},{16,24},{24,16},{1,9},{9,1},{17,25},{25,17},{2,10},{10... | collective-permute-start | bytes 3145736 | tf_op jit(solution)/shard_map/ppermute | solution.py:95
  97.7 28.1 %collective-permute-start.8 = (bf16[128,4096]{1,0:T(8,128)(2,1)}, bf16[128,4096]{1,0:T(8,128)(2,1)S(1)}, u32[]{:S(2)}, u32[]{:S(2)}) collective-permute-start(bf16[128,4096]{1,0:T(8,128)(2,1)} %collective-permute-done.7), channel_id=1, source_target_pairs={{0,8},{8,0},{16,24},{24,16},{1,9},{9,1},{17,25},{25,17},{2,10},{10... | collective-permute-start | bytes 3145736 | tf_op jit(solution)/shard_map/ppermute | solution.py:95
  97.7 40.3 %collective-permute-start.1 = (bf16[128,4096]{1,0:T(8,128)(2,1)}, bf16[128,4096]{1,0:T(8,128)(2,1)S(1)}, u32[]{:S(2)}, u32[]{:S(2)}) collective-permute-start(bf16[128,4096]{1,0:T(8,128)(2,1)} %collective-permute-done), channel_id=1, source_target_pairs={{0,8},{8,0},{16,24},{24,16},{1,9},{9,1},{17,25},{25,17},{2,10},{10... | collective-permute-start | bytes 3145736 | tf_op jit(solution)/shard_map/ppermute | solution.py:95
  98.5 51.7 %collective-permute-start.27 = (f16[512,1024]{1,0:T(8,128)(2,1)S(1)}, f16[512,1024]{1,0:T(8,128)(2,1)S(1)}, u32[]{:S(2)}, u32[]{:S(2)}) collective-permute-start(f16[512,1024]{1,0:T(8,128)(2,1)S(1)} %add_convert_fusion), channel_id=1, source_target_pairs={{2,4},{4,2},{3,5},{5,3},{10,12},{12,10},{11,13},{13,11},{18,20},{2... | collective-permute-start | bytes 3145736 | tf_op jit(solution)/shard_map/ppermute | solution.py:137
  113.3 38.9 %collective-permute-start.19 = (f16[256,1280]{1,0:T(8,128)(2,1)S(1)}, f16[256,1280]{1,0:T(8,128)(2,1)S(1)}, u32[]{:S(2)}, u32[]{:S(2)}) collective-permute-start(f16[256,1280]{1,0:T(8,128)(2,1)S(1)} %pad_maximum_fusion.6), channel_id=1, source_target_pairs={{0,2},{6,4},{1,3},{7,5},{8,10},{14,12},{9,11},{15,13},{16,18},{22,... | collective-permute-start | bytes 1966088 | tf_op jit(solution)/shard_map/ppermute | solution.py:133
  125.8 32.2 %collective-permute-start.14 = (f16[256,1280]{1,0:T(8,128)(2,1)S(1)}, f16[256,1280]{1,0:T(8,128)(2,1)S(1)}, u32[]{:S(2)}, u32[]{:S(2)}) collective-permute-start(f16[256,1280]{1,0:T(8,128)(2,1)S(1)} %pad_maximum_fusion.5), channel_id=1, source_target_pairs={{0,2},{6,4},{1,3},{7,5},{8,10},{14,12},{9,11},{15,13},{16,18},{22,... | collective-permute-start | bytes 1966088 | tf_op jit(solution)/shard_map/ppermute | solution.py:133
  138.0 23.5 %collective-permute-start.9 = (f16[256,1280]{1,0:T(8,128)(2,1)S(1)}, f16[256,1280]{1,0:T(8,128)(2,1)S(1)}, u32[]{:S(2)}, u32[]{:S(2)}) collective-permute-start(f16[256,1280]{1,0:T(8,128)(2,1)S(1)} %pad_maximum_fusion.4), channel_id=1, source_target_pairs={{0,2},{6,4},{1,3},{7,5},{8,10},{14,12},{9,11},{15,13},{16,18},{22,... | collective-permute-start | bytes 1966088 | tf_op jit(solution)/shard_map/ppermute | solution.py:133
  150.3 23.5 %collective-permute-start.2 = (f16[256,1280]{1,0:T(8,128)(2,1)S(1)}, f16[256,1280]{1,0:T(8,128)(2,1)S(1)}, u32[]{:S(2)}, u32[]{:S(2)}) collective-permute-start(f16[256,1280]{1,0:T(8,128)(2,1)S(1)} %pad_maximum_fusion.3), channel_id=1, source_target_pairs={{0,2},{6,4},{1,3},{7,5},{8,10},{14,12},{9,11},{15,13},{16,18},{22,... | collective-permute-start | bytes 1966088 | tf_op jit(solution)/shard_map/ppermute | solution.py:133
  152.2 42.8 %collective-permute-start.28 = (f16[512,768]{1,0:T(8,128)(2,1)S(1)}, f16[512,768]{1,0:T(8,128)(2,1)S(1)}, u32[]{:S(2)}, u32[]{:S(2)}) collective-permute-start(f16[512,768]{1,0:T(8,128)(2,1)S(1)} %slice_convert_fusion), channel_id=1, source_target_pairs={{2,0},{4,6},{3,1},{5,7},{10,8},{12,14},{11,9},{13,15},{18,16},{20,... | collective-permute-start | bytes 2359304 | tf_op jit(solution)/shard_map/ppermute | solution.py:139
  158.0 50.2 %collective-permute-start.20 = (f16[256,1024]{1,0:T(8,128)(2,1)}, f16[256,1024]{1,0:T(8,128)(2,1)}, u32[]{:S(2)}, u32[]{:S(2)}) collective-permute-start(f16[256,1024]{1,0:T(8,128)(2,1)} %add_convert_fusion.2), channel_id=1, source_target_pairs={{2,4},{4,2},{3,5},{5,3},{10,12},{12,10},{11,13},{13,11},{18,20},{2... | collective-permute-start | bytes 1572872 | tf_op jit(solution)/shard_map/ppermute | solution.py:137
  161.5 63.4 %collective-permute-start.15 = (f16[256,1024]{1,0:T(8,128)(2,1)}, f16[256,1024]{1,0:T(8,128)(2,1)}, u32[]{:S(2)}, u32[]{:S(2)}) collective-permute-start(f16[256,1024]{1,0:T(8,128)(2,1)} %add_convert_fusion.3), channel_id=1, source_target_pairs={{2,4},{4,2},{3,5},{5,3},{10,12},{12,10},{11,13},{13,11},{18,20},{2... | collective-permute-start | bytes 1572872 | tf_op jit(solution)/shard_map/ppermute | solution.py:137
  173.8 58.0 %collective-permute-start.10 = (f16[256,1024]{1,0:T(8,128)(2,1)}, f16[256,1024]{1,0:T(8,128)(2,1)}, u32[]{:S(2)}, u32[]{:S(2)}) collective-permute-start(f16[256,1024]{1,0:T(8,128)(2,1)} %add_convert_fusion.4), channel_id=1, source_target_pairs={{2,4},{4,2},{3,5},{5,3},{10,12},{12,10},{11,13},{13,11},{18,20},{2... | collective-permute-start | bytes 1572872 | tf_op jit(solution)/shard_map/ppermute | solution.py:137
  177.1 57.5 %collective-permute-start.3 = (f16[256,1024]{1,0:T(8,128)(2,1)}, f16[256,1024]{1,0:T(8,128)(2,1)}, u32[]{:S(2)}, u32[]{:S(2)}) collective-permute-start(f16[256,1024]{1,0:T(8,128)(2,1)} %add_convert_fusion.5), channel_id=1, source_target_pairs={{2,4},{4,2},{3,5},{5,3},{10,12},{12,10},{11,13},{13,11},{18,20},{2... | collective-permute-start | bytes 1572872 | tf_op jit(solution)/shard_map/ppermute | solution.py:137
  195.0 32.6 %collective-permute-start.23 = (f16[512,1280]{1,0:T(8,128)(2,1)}, f16[512,1280]{1,0:T(8,128)(2,1)}, u32[]{:S(2)}, u32[]{:S(2)}) collective-permute-start(f16[512,1280]{1,0:T(8,128)(2,1)} %pad_maximum_fusion), channel_id=1, source_target_pairs={{0,2},{6,4},{1,3},{7,5},{8,10},{14,12},{9,11},{15,13},{16,18},{22,... | collective-permute-start | bytes 3932168 | tf_op jit(solution)/shard_map/ppermute | solution.py:133
  209.7 27.5 %collective-permute-start.21 = (f16[256,768]{1,0:T(8,128)(2,1)S(1)}, f16[256,768]{1,0:T(8,128)(2,1)S(1)}, u32[]{:S(2)}, u32[]{:S(2)}) collective-permute-start(f16[256,768]{1,0:T(8,128)(2,1)S(1)} %slice_convert_fusion.2), channel_id=1, source_target_pairs={{2,0},{4,6},{3,1},{5,7},{10,8},{12,14},{11,9},{13,15},{18,16},{20,... | collective-permute-start | bytes 1179656 | tf_op jit(solution)/shard_map/ppermute | solution.py:139
  226.2 30.6 %collective-permute-start.16 = (f16[256,768]{1,0:T(8,128)(2,1)S(1)}, f16[256,768]{1,0:T(8,128)(2,1)S(1)}, u32[]{:S(2)}, u32[]{:S(2)}) collective-permute-start(f16[256,768]{1,0:T(8,128)(2,1)S(1)} %slice_convert_fusion.3), channel_id=1, source_target_pairs={{2,0},{4,6},{3,1},{5,7},{10,8},{12,14},{11,9},{13,15},{18,16},{20,... | collective-permute-start | bytes 1179656 | tf_op jit(solution)/shard_map/ppermute | solution.py:139
  229.3 25.0 %collective-permute-start.24 = (f16[512,1024]{1,0:T(8,128)(2,1)S(1)}, f16[512,1024]{1,0:T(8,128)(2,1)S(1)}, u32[]{:S(2)}, u32[]{:S(2)}) collective-permute-start(f16[512,1024]{1,0:T(8,128)(2,1)S(1)} %add_convert_fusion.1), channel_id=1, source_target_pairs={{2,4},{4,2},{3,5},{5,3},{10,12},{12,10},{11,13},{13,11},{18,20},{2... | collective-permute-start | bytes 3145736 | tf_op jit(solution)/shard_map/ppermute | solution.py:137
  233.1 24.8 %collective-permute-start.11 = (f16[256,768]{1,0:T(8,128)(2,1)S(1)}, f16[256,768]{1,0:T(8,128)(2,1)S(1)}, u32[]{:S(2)}, u32[]{:S(2)}) collective-permute-start(f16[256,768]{1,0:T(8,128)(2,1)S(1)} %slice_convert_fusion.4), channel_id=1, source_target_pairs={{2,0},{4,6},{3,1},{5,7},{10,8},{12,14},{11,9},{13,15},{18,16},{20,... | collective-permute-start | bytes 1179656 | tf_op jit(solution)/shard_map/ppermute | solution.py:139
  235.9 23.8 %collective-permute-start.4 = (f16[256,768]{1,0:T(8,128)(2,1)S(1)}, f16[256,768]{1,0:T(8,128)(2,1)S(1)}, u32[]{:S(2)}, u32[]{:S(2)}) collective-permute-start(f16[256,768]{1,0:T(8,128)(2,1)S(1)} %slice_convert_fusion.5), channel_id=1, source_target_pairs={{2,0},{4,6},{3,1},{5,7},{10,8},{12,14},{11,9},{13,15},{18,16},{20,... | collective-permute-start | bytes 1179656 | tf_op jit(solution)/shard_map/ppermute | solution.py:139
  255.0 18.7 %collective-permute-start.25 = (f16[512,768]{1,0:T(8,128)(2,1)S(1)}, f16[512,768]{1,0:T(8,128)(2,1)S(1)}, u32[]{:S(2)}, u32[]{:S(2)}) collective-permute-start(f16[512,768]{1,0:T(8,128)(2,1)S(1)} %slice_convert_fusion.1), channel_id=1, source_target_pairs={{2,0},{4,6},{3,1},{5,7},{10,8},{12,14},{11,9},{13,15},{18,16},{20,... | collective-permute-start | bytes 2359304 | tf_op jit(solution)/shard_map/ppermute | solution.py:139
  320.6 41.1 %collective-permute-start.34 = (f32[128,256]{1,0:T(8,128)S(1)}, f32[128,256]{1,0:T(8,128)S(1)}, u32[]{:S(2)}, u32[]{:S(2)}) collective-permute-start(f32[128,256]{1,0:T(8,128)S(1)} %fusion.17), channel_id=1, source_target_pairs={{2,0},{4,6},{3,1},{5,7},{10,8},{12,14},{11,9},{13,15},{18,16},{20,... | collective-permute-start | bytes 393224 | tf_op jit(solution)/shard_map/ppermute | solution.py:159
  356.0 26.2 %collective-permute-start.31 = (f32[128,768]{1,0:T(8,128)S(1)}, f32[128,768]{1,0:T(8,128)S(1)}, u32[]{:S(2)}, u32[]{:S(2)}) collective-permute-start(f32[128,768]{1,0:T(8,128)S(1)} %pad_maximum_fusion.7), channel_id=1, source_target_pairs={{0,2},{6,4},{1,3},{7,5},{8,10},{14,12},{9,11},{15,13},{16,18},{22,... | collective-permute-start | bytes 1179656 | tf_op jit(solution)/shard_map/ppermute | solution.py:154
  357.3 24.9 %collective-permute-start.32 = (f32[128,768]{1,0:T(8,128)S(1)}, f32[128,768]{1,0:T(8,128)S(1)}, u32[]{:S(2)}, u32[]{:S(2)}) collective-permute-start(f32[128,768]{1,0:T(8,128)S(1)} %pad_maximum_fusion.7), channel_id=1, source_target_pairs={{0,4},{6,2},{1,5},{7,3},{8,12},{14,10},{9,13},{15,11},{16,20},{22,... | collective-permute-start | bytes 1179656 | tf_op jit(solution)/shard_map/ppermute | solution.py:154
  358.6 23.6 %collective-permute-start.33 = (f32[128,768]{1,0:T(8,128)S(1)}, f32[128,768]{1,0:T(8,128)S(1)}, u32[]{:S(2)}, u32[]{:S(2)}) collective-permute-start(f32[128,768]{1,0:T(8,128)S(1)} %pad_maximum_fusion.7), channel_id=1, source_target_pairs={{0,6},{6,0},{1,7},{7,1},{8,14},{14,8},{9,15},{15,9},{16,22},{22,16... | collective-permute-start | bytes 1179656 | tf_op jit(solution)/shard_map/ppermute | solution.py:154
  361.7 20.5 %collective-permute-start.36 = (f32[128,256]{1,0:T(8,128)S(1)}, f32[128,256]{1,0:T(8,128)S(1)}, u32[]{:S(2)}, u32[]{:S(2)}) collective-permute-start(f32[128,256]{1,0:T(8,128)S(1)} %fusion.17), channel_id=1, source_target_pairs={{2,6},{4,0},{3,7},{5,1},{10,14},{12,8},{11,15},{13,9},{18,22},{20,... | collective-permute-start | bytes 393224 | tf_op jit(solution)/shard_map/ppermute | solution.py:159
  (36 other events, 360.5 us)

commit v2 on v0

--- a/solution.py
+++ b/solution.py
@@ -1,9 +1,180 @@
+import functools
+
 import jax
 import jax.numpy as jnp
 from jax import lax
+from jax.experimental import pallas as pl
+from jax.experimental.pallas import tpu as pltpu
 from jax.sharding import PartitionSpec as P
 
 smooth_width = 0.05
+half_inverse = 0.5 / smooth_width
+lane_block = 256
+row_block = 256
+level_group = 8
+
+
+def tail_body(losses, levels, weights, count_in, excess_in, count_out, excess_out):
+    rows = losses.shape[0]
+    bf16 = jnp.bfloat16
+    which = lax.broadcasted_iota(jnp.int32, (level_group, row_block), 0)
+
+    def group(at, carry):
+        span = pl.ds(pl.multiple_of(at * level_group, level_group), level_group)
+        limits = levels[span, :]
+        count = count_in[span, :]
+        excess = excess_in[span, :]
+        for start in range(0, rows, row_block):
+            row_weights = weights[:, pl.ds(start, row_block)]
+            for level in range(level_group):
+                picked = jnp.where(which == level, row_weights, jnp.zeros_like(row_weights))
+                limit = jnp.broadcast_to(limits[level : level + 1, :], (32, lane_block))
+                smooth, products = [], []
+                for row in range(start, start + row_block, 32):
+                    diff = (losses[pl.ds(row, 32), :] - limit).astype(bf16)
+                    twice = jnp.tanh(diff) + bf16(1)
+                    smooth.append(twice)
+                    products.append(twice * diff)
+                count = count + jnp.dot(
+                    picked, jnp.concatenate(smooth, 0), preferred_element_type=jnp.float32
+                )
+                excess = excess + jnp.dot(
+                    picked, jnp.concatenate(products, 0), preferred_element_type=jnp.float32
+                )
+        count_out[span, :] = count
+        excess_out[span, :] = excess
+        return carry
+
+    lax.fori_loop(0, levels.shape[0] // level_group, group, 0)
+
+
+def tail_sums(losses, levels, weights, count, excess):
+    rows, width = losses.shape
+    depth = levels.shape[0]
+    table = pl.BlockSpec((depth, lane_block), lambda i: (0, i))
+    return pl.pallas_call(
+        tail_body,
+        out_shape=[jax.ShapeDtypeStruct((depth, width), jnp.float32)] * 2,
+        grid=(width // lane_block,),
+        in_specs=[
+            pl.BlockSpec((rows, lane_block), lambda i: (0, i)),
+            table,
+            pl.BlockSpec((8, rows), lambda i: (0, 0)),
+            table,
+            table,
+        ],
+        out_specs=[table, table],
+        input_output_aliases={3: 0, 4: 1},
+        cost_estimate=pl.CostEstimate(flops=1024, transcendentals=0, bytes_accessed=1024),
+        name="tail_sums",
+    )(losses, levels, weights, count, excess)
+
+
+def together(*values):
+    return lax.optimization_barrier(values)
+
+
+def pipelined(shocks, loading, thresholds, weights):
+    rows = shocks.shape[0]
+    quarter = loading.shape[1] // 4
+    link, f32 = jnp.float16, jnp.float32
+    place = lax.axis_index("fac")
+    low, high = place % 2, place // 2
+
+    def swap(v, axis, flip):
+        return lax.ppermute(v, axis, [(i, i ^ flip) for i in range(lax.axis_size(axis))])
+
+    def columns(v, k, width):
+        return lax.dynamic_slice_in_dim(v, k * width, width, 1)
+
+    def product(block):
+        return (jnp.dot(block, loading, preferred_element_type=f32) * half_inverse).astype(link)
+
+    def send_a(partial):
+        return columns(partial, 1 - low, 2 * quarter)
+
+    def send_b(partial, got):
+        at = 2 * low + 1 - high
+        return (columns(partial, at, quarter).astype(f32) + columns(got, 1 - high, quarter).astype(f32)).astype(link)
+
+    def finish(partial, got, last):
+        at = 2 * low + high
+        return (
+            columns(partial, at, quarter).astype(f32)
+            + columns(got, high, quarter).astype(f32)
+            + last.astype(f32)
+        )
+
+    split = rows // 2
+    limits = columns(thresholds, 2 * low + high, quarter) * half_inverse
+    zero = jnp.zeros(limits.shape, f32)
+
+    weights_pair = jnp.stack([weights, swap(weights, "port", 1)])
+    weights_far = swap(weights_pair, "port", 2)
+    group_total = jnp.sum(weights_pair.astype(f32)) + jnp.sum(weights_far.astype(f32))
+    total = group_total + swap(group_total, "scen", 1)
+    block_weights = [
+        weights_pair[0],
+        weights_pair[1],
+        weights_far[:, :split].reshape(-1),
+        weights_far[:, split:].reshape(-1),
+    ]
+
+    def tails(losses, which, sums):
+        w = block_weights[which]
+        return tail_sums(losses, limits, jnp.broadcast_to(w[None], (8, w.shape[0])), *sums)
+
+    sums = (zero, zero)
+    far0 = swap(shocks[:split], "port", 2)
+    sibling = swap(shocks, "port", 1)
+    p0 = product(shocks)
+    a0, sibling, p0 = together(send_a(p0), sibling, p0)
+
+    a0 = swap(a0, "fac", 1)
+    p1 = product(sibling)
+    a0, p1, far0 = together(a0, p1, far0)
+
+    b0, a1, far0, far1 = together(send_b(p0, a0), send_a(p1), far0, shocks[split:])
+    a1 = swap(a1, "fac", 1)
+    b0 = swap(b0, "fac", 2)
+    far1 = swap(far1, "port", 2)
+    p2 = product(jnp.concatenate([far0, swap(far0, "port", 1)], 0))
+    a1, b0, p2, far1 = together(a1, b0, p2, far1)
+
+    b1, a2, far1, done = together(send_b(p1, a1), send_a(p2), far1, finish(p0, a0, b0))
+    a2 = swap(a2, "fac", 1)
+    b1 = swap(b1, "fac", 2)
+    p3 = product(jnp.concatenate([far1, swap(far1, "port", 1)], 0))
+    sums = tails(together(done, p3)[0], 0, sums)
+    a2, b1, p3, sums = together(a2, b1, p3, sums)
+
+    b2, a3, done, sums = together(send_b(p2, a2), send_a(p3), finish(p1, a1, b1), sums)
+    a3 = swap(a3, "fac", 1)
+    b2 = swap(b2, "fac", 2)
+    sums = tails(done, 1, sums)
+    a3, b2, sums = together(a3, b2, sums)
+
+    b3, done, sums = together(send_b(p3, a3), finish(p2, a2, b2), sums)
+    b3 = swap(b3, "fac", 2)
+    sums = tails(done, 2, sums)
+    b3, sums = together(b3, sums)
+    count, excess = tails(finish(p3, a3, b3), 3, sums)
+
+    sums = jnp.concatenate([count * 0.5, excess * (0.5 / half_inverse)], 0)
+    sums = sums + swap(sums, "scen", 1)
+    depth = limits.shape[0]
+    count, excess = sums[:depth], sums[depth:]
+    result = jnp.concatenate([excess / jnp.maximum(count, 1.0), count / total], 0)
+    parts = [result] + [swap(result, "fac", flip) for flip in (1, 2, 3)]
+
+    def owner(k):
+        out = parts[k ^ 3]
+        for mine in (2, 1, 0):
+            out = jnp.where(place == mine, parts[k ^ mine], out)
+        return out
+
+    full = jnp.concatenate([owner(k) for k in (0, 2, 1, 3)], 1)
+    return full[:depth], full[depth:]
 
 
 def sums_rows(losses, levels, scen_weights):
@@ -18,15 +189,14 @@
     return (count.reshape(-1, width), excess.reshape(-1, width))
 
 
-def per_device(shocks, loading, thresholds, weights):
+def plain(shocks, loading, thresholds, weights):
     fac_count = lax.axis_size("fac")
     fac_index = lax.axis_index("fac")
     gathered, group_weights = (
         lax.all_gather(shocks, "port", axis=0, tiled=True),
         lax.all_gather(weights, "port", axis=0, tiled=True),
     )
-    group_rows = gathered.shape[0]
-    local_rows = group_rows // fac_count
+    local_rows = gathered.shape[0] // fac_count
     losses = lax.psum_scatter(
         jnp.dot(gathered, loading, preferred_element_type=jnp.float32),
         "fac",
@@ -39,6 +209,19 @@
     count, excess = sums_rows(losses, thresholds, own_weights)
     count, excess, total = lax.psum((count, excess, jnp.sum(own_weights)), ("fac", "scen"))
     return (excess / jnp.maximum(count, 1.0), count / total)
+
+
+def per_device(shocks, loading, thresholds, weights):
+    sizes = tuple(lax.axis_size(name) for name in ("port", "fac", "scen"))
+    fits = (
+        sizes == (4, 4, 2)
+        and shocks.shape[0] % 512 == 0
+        and loading.shape[1] % 2048 == 0
+        and thresholds.shape[0] % level_group == 0
+    )
+    if fits:
+        return pipelined(shocks, loading, thresholds, weights)
+    return plain(shocks, loading, thresholds, weights)
 
 
 def solution(mesh):

time: 656 us -> 267 us (0.41)
  waiting for transfers between devices: 440 us -> 108 us
  other arithmetic: 116 us -> 19.6 us
  Pallas kernels: 0 us -> 50.1 us
  blocking collectives: 27.7 us -> 0 us
  starting transfers between devices: 0.12 us -> 23.5 us
  between operations: 13.8 us -> 2.82 us
  matrix products: 43 us -> 50.9 us
    reduce_scatter x1 -> x0, waiting for transfers between devices: 271 us -> none  [per_device(): lax.psum_scatter(jnp.dot(gathered, loading, preferred_element_type=jnp.fl...]
    reduce_sum x9 -> x2, other arithmetic: 113 us -> 1.23 us  [the longest x1 0.63 us: pipelined(): jnp.sum(weights_pair.astype(f32)) + jnp.sum(weights_far.astype(f32))]
    all_gather x1 -> x0, waiting for transfers between devices: 109 us -> none  [per_device(): lax.all_gather(shocks, 'port', axis=0, tiled=True)]
    ppermute x0 -> x20, waiting for transfers between devices: none -> 108 us  [swap(): lax.ppermute(v, axis, [(i, i ^ flip) for i in range(lax.axis_size(axis))])]
    psum x1 -> x0, waiting for transfers between devices: 58.8 us -> none  [per_device(): lax.psum((count, excess, jnp.sum(own_weights)), ('fac', 'scen'))]
    pallas_call x0 -> x4, Pallas kernels: none -> 50.1 us  [tail_sums(): pl.pallas_call(tail_body, out_shape=[jax.ShapeDtypeStruct((depth, width),...]
    ppermute x0 -> x20, starting transfers between devices: none -> 23.5 us  [swap(): lax.ppermute(v, axis, [(i, i ^ flip) for i in range(lax.axis_size(axis))])]
    psum x1 -> x0, blocking collectives: 22.6 us -> none  [per_device(): lax.psum((count, excess, jnp.sum(own_weights)), ('fac', 'scen'))]
  transfers between devices with their start and end apart: 3 -> 20, of which waited for: 3 -> 12; matrix products, arithmetic and copies ran while one was open for 0% -> 23% of each run, Pallas kernels for 0% -> 14%
where the time goes in v2:
time: 267 us; the launch traced here: 266 us
  waiting for transfers between devices  108 us (40%)
  matrix products  50.9 us (19%)
  Pallas kernels  50.1 us (19%)
  starting transfers between devices  23.5 us (9%)
  other arithmetic  19.6 us (7%)
  local copies, waits for them, and re-layouts  10.7 us (4%)
  between operations  2.82 us (1%)
    ppermute x20, waiting for transfers between devices, swap(): lax.ppermute(v, axis, [(i, i ^ flip) for i in range(lax.axis_size(axis))])  108 us
    dot_general x4, matrix products, product(): jnp.dot(block, loading, preferred_element_type=f32) * half_inverse  50.9 us
    pallas_call x4, Pallas kernels, tail_sums(): pl.pallas_call(tail_body, out_shape=[jax.ShapeDtypeStruct((depth, width),...  50.1 us
    ppermute x20, starting transfers between devices, swap(): lax.ppermute(v, axis, [(i, i ^ flip) for i in range(lax.axis_size(axis))])  23.5 us
    add x4, other arithmetic, finish(): columns(partial, at, quarter).astype(f32)  10.1 us
  transfers between devices with their start and end apart: 20, of which 12 were waited for; matrix products, arithmetic and copies ran while one was open for 23% of the time, Pallas kernels for 14%

profile of v2, /device:TPU:8, one launch (start us, length us, event | category | flops | bytes accessed | tf_op | source)
XLA Modules:
  0.0 266.1 jit_solution(17933376994469936540)
XLA Ops:
  0.7 4.7 %fusion.15 = (bf16[256,4096]{1,0:T(8,128)(2,1)}, bf16[256,4096]{1,0:T(8,128)(2,1)}) fusion(bf16[512,4096]{1,0:T(8,128)(2,1)} %param.4), kind=kLoop, calls=%fused_computation.44 | loop fusion | bytes 8388608 | tf_op jit(solution)/shard_map/slice | solution.py:137
  6.9 13.7 %multiply_convert_fusion.3 = f16[512,2048]{1,0:T(8,128)(2,1)S(1)} fusion(bf16[512,4096]{1,0:T(8,128)(2,1)} %param.4, bf16[4096,2048]{1,0:T(8,128)(2,1)} %param.5), kind=kOutput, calls=%fused_computation.11 | convolution fusion | flops 8592031744 | bytes 23068672 | tf_op jit(solution)/shard_map/dot_general | solution.py:91
  21.5 11.0 %multiply_convert_fusion.2 = f16[512,2048]{1,0:T(8,128)(2,1)S(1)} fusion(bf16[512,4096]{1,0:T(8,128)(2,1)} %collective-permute-done, bf16[4096,2048]{1,0:T(8,128)(2,1)S(1)} %copy-done.7), kind=kOutput, calls=%fused_computation.10 | convolution fusion | flops 8592031744 | bytes 23068672 | tf_op jit(solution)/shard_map/dot_general | solution.py:91
  32.5 21.2 %collective-permute-done.2 = bf16[256,4096]{1,0:T(8,128)(2,1)} collective-permute-done((bf16[256,4096]{1,0:T(8,128)(2,1)}, bf16[256,4096]{1,0:T(8,128)(2,1)}, u32[]{:S(2)}, u32[]{:S(2)}) %collective-permute-start.2) | collective-permute-done | bytes 2097184 | tf_op jit(solution)/shard_map/ppermute | solution.py:85
  57.2 2.6 collective-permute-start.4
  59.8 13.6 %multiply_convert_fusion.1 = f16[512,2048]{1,0:T(8,128)(2,1)S(1)} fusion(bf16[4096,2048]{1,0:T(8,128)(2,1)} %param.5, bf16[256,4096]{1,0:T(8,128)(2,1)} %collective-permute-done.5, bf16[256,4096]{1,0:T(8,128)(2,1)} %collective-permute-done.2), kind=kOutput, calls=%fused_computation.9 | convolution fusion | flops 8600420352 | bytes 23068672 | tf_op jit(solution)/shard_map/dot_general | solution.py:91
  73.4 20.8 %collective-permute-done.4 = f16[512,512]{1,0:T(8,128)(2,1)S(1)} collective-permute-done((f16[512,512]{1,0:T(8,128)(2,1)}, f16[512,512]{1,0:T(8,128)(2,1)S(1)}, u32[]{:S(2)}, u32[]{:S(2)}) %collective-permute-start.4) | collective-permute-done | bytes 524320 | tf_op jit(solution)/shard_map/ppermute | solution.py:85
  94.2 9.2 %collective-permute-done.6 = bf16[256,4096]{1,0:T(8,128)(2,1)S(1)} collective-permute-done((bf16[256,4096]{1,0:T(8,128)(2,1)}, bf16[256,4096]{1,0:T(8,128)(2,1)S(1)}, u32[]{:S(2)}, u32[]{:S(2)}) %collective-permute-start.6) | collective-permute-done | bytes 2097184 | tf_op jit(solution)/shard_map/ppermute | solution.py:85
  103.7 2.8 %convert_add_fusion.3 = (f32[512,512]{1,0:T(8,128)}, f16[512,512]{1,0:T(8,128)(2,1)}) fusion(f16[512,512]{1,0:T(8,128)(2,1)S(1)} %collective-permute-done.4, f16[512,1024]{1,0:T(8,128)(2,1)S(1)} %copy-done.5, s32[]{:T(128)S(6)} %select_n.105, f16[512,2048]{1,0:T(8,128)(2,1)} %copy-done.2, s32[]{:T(128)S(6)} %select_n.104, ...), kind=kLoop, calls=%fused_computation.18 | loop fusion | flops 2359296 | bytes 4194320 | tf_op jit(solution)/shard_map/add | solution.py:103
  106.5 1.6 dynamic-slice_multiply_fusion.levels
  108.2 2.8 %collective-permute-start.8 = (f16[512,512]{1,0:T(8,128)(2,1)}, f16[512,512]{1,0:T(8,128)(2,1)}, u32[]{:S(2)}, u32[]{:S(2)}) collective-permute-start(f16[512,512]{1,0:T(8,128)(2,1)} %get-tuple-element.65), channel_id=1, source_target_pairs={{0,4},{2,6},{4,0},{6,2},{1,5},{3,7},{5,1},{7,3},{8,12},{10,14},{12... | collective-permute-start | bytes 1572872 | tf_op jit(solution)/shard_map/ppermute | solution.py:85
  111.1 12.5 %multiply_convert_fusion = f16[512,2048]{1,0:T(8,128)(2,1)S(1)} fusion(bf16[4096,2048]{1,0:T(8,128)(2,1)} %param.5, bf16[256,4096]{1,0:T(8,128)(2,1)S(1)} %collective-permute-done.9, bf16[256,4096]{1,0:T(8,128)(2,1)S(1)} %collective-permute-done.6), kind=kOutput, calls=%fused_computation.8 | convolution fusion | flops 8600420352 | bytes 23068672 | tf_op jit(solution)/shard_map/dot_general | solution.py:91
  125.6 12.5 %tail_sums.4 = (f32[64,512]{1,0:T(8,128)}, f32[64,512]{1,0:T(8,128)}) custom-call(f32[512,512]{1,0:T(8,128)} %get-tuple-element.68.losses, f32[64,512]{1,0:T(8,128)} %dynamic-slice_multiply_fusion.levels, bf16[8,512]{1,0:T(8,128)(2,1)} %broadcast_in_dim.27.weights, ...), custom_call_target="tpu_custom_call", output_to_operand_aliasing={{0}: (3, {}), {1}: (4, {})} | custom-call | flops 1024 | bytes 1024 | tf_op jit(solution)/shard_map/tail_sums/pallas_call | solution.py:55
  138.1 7.8 %collective-permute-done.8 = f16[512,512]{1,0:T(8,128)(2,1)} collective-permute-done((f16[512,512]{1,0:T(8,128)(2,1)}, f16[512,512]{1,0:T(8,128)(2,1)}, u32[]{:S(2)}, u32[]{:S(2)}) %collective-permute-start.8) | collective-permute-done | bytes 524320 | tf_op jit(solution)/shard_map/ppermute | solution.py:85
  146.0 2.6 convert_add_fusion.2.losses
  148.8 2.2 add_convert_fusion.1
  151.0 1.9 collective-permute-start.11
  154.7 12.5 %tail_sums.5 = (f32[64,512]{1,0:T(8,128)}, f32[64,512]{1,0:T(8,128)}) custom-call(f32[512,512]{1,0:T(8,128)} %convert_add_fusion.2.losses, f32[64,512]{1,0:T(8,128)} %dynamic-slice_multiply_fusion.levels, bf16[8,512]{1,0:T(8,128)(2,1)} %broadcast_in_dim.29.weights, ...), custom_call_target="tpu_custom_call", output_to_operand_aliasing={{0}: (3, {}), {1}: (4, {})} | custom-call | flops 1024 | bytes 1024 | tf_op jit(solution)/shard_map/tail_sums/pallas_call | solution.py:55
  167.2 19.8 %collective-permute-done.11 = f16[512,512]{1,0:T(8,128)(2,1)} collective-permute-done((f16[512,512]{1,0:T(8,128)(2,1)}, f16[512,512]{1,0:T(8,128)(2,1)}, u32[]{:S(2)}, u32[]{:S(2)}) %collective-permute-start.11) | collective-permute-done | bytes 524320 | tf_op jit(solution)/shard_map/ppermute | solution.py:85
  187.0 2.5 convert_add_fusion.1.losses
  190.9 1.7 collective-permute-start.13
  194.7 2.1 collective-permute-done.14
  197.4 12.5 %tail_sums.6 = (f32[64,512]{1,0:T(8,128)}, f32[64,512]{1,0:T(8,128)}) custom-call(f32[512,512]{1,0:T(8,128)} %convert_add_fusion.1.losses, f32[64,512]{1,0:T(8,128)} %dynamic-slice_multiply_fusion.levels, bf16[8,512]{1,0:T(8,128)(2,1)} %broadcast_in_dim.31.weights, ...), custom_call_target="tpu_custom_call", output_to_operand_aliasing={{0}: (3, {}), {1}: (4, {})} | custom-call | flops 1024 | bytes 1024 | tf_op jit(solution)/shard_map/tail_sums/pallas_call | solution.py:55
  209.9 4.0 %collective-permute-done.13 = f16[512,512]{1,0:T(8,128)(2,1)S(1)} collective-permute-done((f16[512,512]{1,0:T(8,128)(2,1)S(1)}, f16[512,512]{1,0:T(8,128)(2,1)S(1)}, u32[]{:S(2)}, u32[]{:S(2)}) %collective-permute-start.13) | collective-permute-done | bytes 524320 | tf_op jit(solution)/shard_map/ppermute | solution.py:85
  214.0 2.3 convert_add_fusion.losses
  216.8 12.5 %tail_sums.7 = (f32[64,512]{1,0:T(8,128)}, f32[64,512]{1,0:T(8,128)}) custom-call(f32[512,512]{1,0:T(8,128)} %convert_add_fusion.losses, f32[64,512]{1,0:T(8,128)} %dynamic-slice_multiply_fusion.levels, bf16[8,512]{1,0:T(8,128)(2,1)} %broadcast_in_dim.33.weights, ...), custom_call_target="tpu_custom_call", output_to_operand_aliasing={{0}: (3, {}), {1}: (4, {})} | custom-call | flops 1024 | bytes 1024 | tf_op jit(solution)/shard_map/tail_sums/pallas_call | solution.py:55
  231.2 1.6 collective-permute-start.15
  234.7 3.0 %collective-permute-start.16 = (f32[]{:T(128)}, f32[]{:T(128)}, u32[]{:S(2)}, u32[]{:S(2)}) collective-permute-start(f32[]{:T(128)} %add.115), channel_id=1, source_target_pairs={{0,1},{1,0},{2,3},{3,2},{4,5},{5,4},{6,7},{7,6},{8,9},{9,8},{10,11... | collective-permute-start | bytes 20 | tf_op jit(solution)/shard_map/ppermute | solution.py:85
  239.4 2.5 collective-permute-start.17
  243.5 6.6 %collective-permute-done.17 = f32[128,512]{1,0:T(8,128)S(1)} collective-permute-done((f32[128,512]{1,0:T(8,128)S(1)}, f32[128,512]{1,0:T(8,128)S(1)}, u32[]{:S(2)}, u32[]{:S(2)}) %collective-permute-start.17) | collective-permute-done | bytes 262176 | tf_op jit(solution)/shard_map/ppermute | solution.py:85
  250.1 10.4 %collective-permute-done.18 = f32[128,512]{1,0:T(8,128)S(1)} collective-permute-done((f32[128,512]{1,0:T(8,128)S(1)}, f32[128,512]{1,0:T(8,128)S(1)}, u32[]{:S(2)}, u32[]{:S(2)}) %collective-permute-start.18) | collective-permute-done | bytes 262176 | tf_op jit(solution)/shard_map/ppermute | solution.py:85
  260.5 4.3 %collective-permute-done.19 = f32[128,512]{1,0:T(8,128)S(1)} collective-permute-done((f32[128,512]{1,0:T(8,128)S(1)}, f32[128,512]{1,0:T(8,128)S(1)}, u32[]{:S(2)}, u32[]{:S(2)}) %collective-permute-start.19) | collective-permute-done | bytes 262176 | tf_op jit(solution)/shard_map/ppermute | solution.py:85
  (67 shorter events, 21.2 us)
Async XLA Ops:
  0.6 20.4 %collective-permute-start = (bf16[512,4096]{1,0:T(8,128)(2,1)}, bf16[512,4096]{1,0:T(8,128)(2,1)}, u32[]{:S(2)}, u32[]{:S(2)}) collective-permute-start(bf16[512,4096]{1,0:T(8,128)(2,1)} %param.4), channel_id=1, source_target_pairs={{0,8},{8,0},{16,24},{24,16},{1,9},{9,1},{17,25},{25,17},{2,10},{10... | collective-permute-start | bytes 12582920 | tf_op jit(solution)/shard_map/ppermute | solution.py:85
  5.4 48.3 %collective-permute-start.2 = (bf16[256,4096]{1,0:T(8,128)(2,1)}, bf16[256,4096]{1,0:T(8,128)(2,1)}, u32[]{:S(2)}, u32[]{:S(2)}) collective-permute-start(bf16[256,4096]{1,0:T(8,128)(2,1)} %get-tuple-element.101), channel_id=1, source_target_pairs={{0,16},{8,24},{16,0},{24,8},{1,17},{9,25},{17,1},{25,9},{2,18},{10... | collective-permute-start | bytes 6291464 | tf_op jit(solution)/shard_map/ppermute | solution.py:85
  6.9 14.6 %copy-start.7 = (bf16[4096,2048]{1,0:T(8,128)(2,1)S(1)}, bf16[4096,2048]{1,0:T(8,128)(2,1)}, u32[]{:S(2)}) copy-start(bf16[4096,2048]{1,0:T(8,128)(2,1)} %param.5) | copy-start | bytes 50331652
  20.7 33.4 %copy-start.2 = (f16[512,2048]{1,0:T(8,128)(2,1)}, f16[512,2048]{1,0:T(8,128)(2,1)S(1)}, u32[]{:S(2)}) copy-start(f16[512,2048]{1,0:T(8,128)(2,1)S(1)} %multiply_convert_fusion.3) | copy-start | bytes 6291460
  21.0 32.8 %collective-permute-start.1 = (f16[512,1024]{1,0:T(8,128)(2,1)S(1)}, f16[512,1024]{1,0:T(8,128)(2,1)S(1)}, u32[]{:S(2)}, u32[]{:S(2)}) collective-permute-start(f16[512,1024]{1,0:T(8,128)(2,1)S(1)} %constant_dynamic-slice_fusion.3), channel_id=1, source_target_pairs={{0,2},{2,0},{4,6},{6,4},{1,3},{3,1},{5,7},{7,5},{8,10},{10,8},{12,... | collective-permute-start | bytes 3145736 | tf_op jit(solution)/shard_map/ppermute | solution.py:85
  32.5 71.2 %copy-start.1 = (f16[512,2048]{1,0:T(8,128)(2,1)}, f16[512,2048]{1,0:T(8,128)(2,1)S(1)}, u32[]{:S(2)}) copy-start(f16[512,2048]{1,0:T(8,128)(2,1)S(1)} %multiply_convert_fusion.2) | copy-start | bytes 6291460
  53.8 1.4 copy-start.4
  55.2 4.6 %collective-permute-start.5 = (bf16[256,4096]{1,0:T(8,128)(2,1)}, bf16[256,4096]{1,0:T(8,128)(2,1)}, u32[]{:S(2)}, u32[]{:S(2)}) collective-permute-start(bf16[256,4096]{1,0:T(8,128)(2,1)} %collective-permute-done.2), channel_id=1, source_target_pairs={{0,8},{8,0},{16,24},{24,16},{1,9},{9,1},{17,25},{25,17},{2,10},{10... | collective-permute-start | bytes 6291464 | tf_op jit(solution)/shard_map/ppermute | solution.py:85
  55.2 48.5 %copy-start.5 = (f16[512,1024]{1,0:T(8,128)(2,1)S(1)}, f16[512,1024]{1,0:T(8,128)(2,1)}, u32[]{:S(2)}) copy-start(f16[512,1024]{1,0:T(8,128)(2,1)} %copy-done.4) | copy-start | bytes 3145732
  55.2 48.3 %collective-permute-start.6 = (bf16[256,4096]{1,0:T(8,128)(2,1)}, bf16[256,4096]{1,0:T(8,128)(2,1)S(1)}, u32[]{:S(2)}, u32[]{:S(2)}) collective-permute-start(bf16[256,4096]{1,0:T(8,128)(2,1)} %get-tuple-element.59), channel_id=1, source_target_pairs={{0,16},{8,24},{16,0},{24,8},{1,17},{9,25},{17,1},{25,9},{2,18},{10... | collective-permute-start | bytes 6291464 | tf_op jit(solution)/shard_map/ppermute | solution.py:85
  56.7 37.5 %collective-permute-start.3 = (f16[512,1024]{1,0:T(8,128)(2,1)S(1)}, f16[512,1024]{1,0:T(8,128)(2,1)S(1)}, u32[]{:S(2)}, u32[]{:S(2)}) collective-permute-start(f16[512,1024]{1,0:T(8,128)(2,1)S(1)} %constant_dynamic-slice_fusion.1), channel_id=1, source_target_pairs={{0,2},{2,0},{4,6},{6,4},{1,3},{3,1},{5,7},{7,5},{8,10},{10,8},{12,... | collective-permute-start | bytes 3145736 | tf_op jit(solution)/shard_map/ppermute | solution.py:85
  57.2 37.0 %collective-permute-start.4 = (f16[512,512]{1,0:T(8,128)(2,1)}, f16[512,512]{1,0:T(8,128)(2,1)S(1)}, u32[]{:S(2)}, u32[]{:S(2)}) collective-permute-start(f16[512,512]{1,0:T(8,128)(2,1)} %add_convert_fusion.3), channel_id=1, source_target_pairs={{0,4},{2,6},{4,0},{6,2},{1,5},{3,7},{5,1},{7,3},{8,12},{10,14},{12... | collective-permute-start | bytes 1572872 | tf_op jit(solution)/shard_map/ppermute | solution.py:85
  73.4 50.3 %copy-start = (f16[512,2048]{1,0:T(8,128)(2,1)}, f16[512,2048]{1,0:T(8,128)(2,1)S(1)}, u32[]{:S(2)}) copy-start(f16[512,2048]{1,0:T(8,128)(2,1)S(1)} %multiply_convert_fusion.1) | copy-start | bytes 6291460
  94.2 29.4 %copy-start.3 = (f16[512,1024]{1,0:T(8,128)(2,1)}, f16[512,1024]{1,0:T(8,128)(2,1)S(1)}, u32[]{:S(2)}) copy-start(f16[512,1024]{1,0:T(8,128)(2,1)S(1)} %collective-permute-done.3) | copy-start | bytes 3145732
  106.5 4.6 %collective-permute-start.9 = (bf16[256,4096]{1,0:T(8,128)(2,1)S(1)}, bf16[256,4096]{1,0:T(8,128)(2,1)S(1)}, u32[]{:S(2)}, u32[]{:S(2)}) collective-permute-start(bf16[256,4096]{1,0:T(8,128)(2,1)S(1)} %collective-permute-done.6), channel_id=1, source_target_pairs={{0,8},{8,0},{16,24},{24,16},{1,9},{9,1},{17,25},{25,17},{2,10},{10... | collective-permute-start | bytes 6291464 | tf_op jit(solution)/shard_map/ppermute | solution.py:85
  108.0 15.6 %copy-start.6 = (bf16[512]{0:T(512)(128)(2,1)S(1)}, bf16[512]{0:T(512)(128)(2,1)}, u32[]{:S(2)}) copy-start(bf16[512]{0:T(512)(128)(2,1)} %param.7) | copy-start | bytes 3076
  108.0 37.9 %collective-permute-start.7 = (f16[512,1024]{1,0:T(8,128)(2,1)S(1)}, f16[512,1024]{1,0:T(8,128)(2,1)}, u32[]{:S(2)}, u32[]{:S(2)}) collective-permute-start(f16[512,1024]{1,0:T(8,128)(2,1)S(1)} %constant_dynamic-slice_fusion), channel_id=1, source_target_pairs={{0,2},{2,0},{4,6},{6,4},{1,3},{3,1},{5,7},{7,5},{8,10},{10,8},{12,... | collective-permute-start | bytes 3145736 | tf_op jit(solution)/shard_map/ppermute | solution.py:85
  108.2 37.7 %collective-permute-start.8 = (f16[512,512]{1,0:T(8,128)(2,1)}, f16[512,512]{1,0:T(8,128)(2,1)}, u32[]{:S(2)}, u32[]{:S(2)}) collective-permute-start(f16[512,512]{1,0:T(8,128)(2,1)} %get-tuple-element.65), channel_id=1, source_target_pairs={{0,4},{2,6},{4,0},{6,2},{1,5},{3,7},{5,1},{7,3},{8,12},{10,14},{12... | collective-permute-start | bytes 1572872 | tf_op jit(solution)/shard_map/ppermute | solution.py:85
  151.0 36.0 %collective-permute-start.10 = (f16[512,1024]{1,0:T(8,128)(2,1)S(1)}, f16[512,1024]{1,0:T(8,128)(2,1)}, u32[]{:S(2)}, u32[]{:S(2)}) collective-permute-start(f16[512,1024]{1,0:T(8,128)(2,1)S(1)} %constant_dynamic-slice_fusion.2), channel_id=1, source_target_pairs={{0,2},{2,0},{4,6},{6,4},{1,3},{3,1},{5,7},{7,5},{8,10},{10,8},{12,... | collective-permute-start | bytes 3145736 | tf_op jit(solution)/shard_map/ppermute | solution.py:85
  151.0 36.0 %collective-permute-start.11 = (f16[512,512]{1,0:T(8,128)(2,1)}, f16[512,512]{1,0:T(8,128)(2,1)}, u32[]{:S(2)}, u32[]{:S(2)}) collective-permute-start(f16[512,512]{1,0:T(8,128)(2,1)} %add_convert_fusion.1), channel_id=1, source_target_pairs={{0,4},{2,6},{4,0},{6,2},{1,5},{3,7},{5,1},{7,3},{8,12},{10,14},{12... | collective-permute-start | bytes 1572872 | tf_op jit(solution)/shard_map/ppermute | solution.py:85
  152.9 1.1 collective-permute-start.12
  190.9 23.1 %collective-permute-start.13 = (f16[512,512]{1,0:T(8,128)(2,1)S(1)}, f16[512,512]{1,0:T(8,128)(2,1)S(1)}, u32[]{:S(2)}, u32[]{:S(2)}) collective-permute-start(f16[512,512]{1,0:T(8,128)(2,1)S(1)} %add_convert_fusion), channel_id=1, source_target_pairs={{0,4},{2,6},{4,0},{6,2},{1,5},{3,7},{5,1},{7,3},{8,12},{10,14},{12... | collective-permute-start | bytes 1572872 | tf_op jit(solution)/shard_map/ppermute | solution.py:85
  193.2 3.6 %collective-permute-start.14 = (bf16[2,512]{1,0:T(2,128)(2,1)S(1)}, bf16[2,512]{1,0:T(2,128)(2,1)S(1)}, u32[]{:S(2)}, u32[]{:S(2)}) collective-permute-start(bf16[2,512]{1,0:T(2,128)(2,1)S(1)} %get-tuple-element.99), channel_id=1, source_target_pairs={{0,16},{8,24},{16,0},{24,8},{1,17},{9,25},{17,1},{25,9},{2,18},{10... | collective-permute-start | bytes 6152 | tf_op jit(solution)/shard_map/ppermute | solution.py:85
  231.2 8.1 %collective-permute-start.15 = (f32[128,512]{1,0:T(8,128)S(1)}, f32[128,512]{1,0:T(8,128)S(1)}, u32[]{:S(2)}, u32[]{:S(2)}) collective-permute-start(f32[128,512]{1,0:T(8,128)S(1)} %pad_maximum_fusion.1), channel_id=1, source_target_pairs={{0,1},{1,0},{2,3},{3,2},{4,5},{5,4},{6,7},{7,6},{8,9},{9,8},{10,11... | collective-permute-start | bytes 786440 | tf_op jit(solution)/shard_map/ppermute | solution.py:85
  234.7 4.0 %collective-permute-start.16 = (f32[]{:T(128)}, f32[]{:T(128)}, u32[]{:S(2)}, u32[]{:S(2)}) collective-permute-start(f32[]{:T(128)} %add.115), channel_id=1, source_target_pairs={{0,1},{1,0},{2,3},{3,2},{4,5},{5,4},{6,7},{7,6},{8,9},{9,8},{10,11... | collective-permute-start | bytes 20 | tf_op jit(solution)/shard_map/ppermute | solution.py:85
  239.4 10.7 %collective-permute-start.17 = (f32[128,512]{1,0:T(8,128)S(1)}, f32[128,512]{1,0:T(8,128)S(1)}, u32[]{:S(2)}, u32[]{:S(2)}) collective-permute-start(f32[128,512]{1,0:T(8,128)S(1)} %pad_maximum_fusion.2), channel_id=1, source_target_pairs={{0,2},{2,0},{4,6},{6,4},{1,3},{3,1},{5,7},{7,5},{8,10},{10,8},{12,... | collective-permute-start | bytes 786440 | tf_op jit(solution)/shard_map/ppermute | solution.py:85
  242.0 18.6 %collective-permute-start.18 = (f32[128,512]{1,0:T(8,128)S(1)}, f32[128,512]{1,0:T(8,128)S(1)}, u32[]{:S(2)}, u32[]{:S(2)}) collective-permute-start(f32[128,512]{1,0:T(8,128)S(1)} %pad_maximum_fusion.2), channel_id=1, source_target_pairs={{0,4},{2,6},{4,0},{6,2},{1,5},{3,7},{5,1},{7,3},{8,12},{10,14},{12... | collective-permute-start | bytes 786440 | tf_op jit(solution)/shard_map/ppermute | solution.py:85
  243.0 21.8 %collective-permute-start.19 = (f32[128,512]{1,0:T(8,128)S(1)}, f32[128,512]{1,0:T(8,128)S(1)}, u32[]{:S(2)}, u32[]{:S(2)}) collective-permute-start(f32[128,512]{1,0:T(8,128)S(1)} %pad_maximum_fusion.2), channel_id=1, source_target_pairs={{0,6},{2,4},{4,2},{6,0},{1,7},{3,5},{5,3},{7,1},{8,14},{10,12},{12... | collective-permute-start | bytes 786440 | tf_op jit(solution)/shard_map/ppermute | solution.py:85

commit v3 on v2

--- a/solution.py
+++ b/solution.py
@@ -10,20 +10,22 @@
 smooth_width = 0.05
 half_inverse = 0.5 / smooth_width
 lane_block = 256
-row_block = 256
 level_group = 8
 
 
-def tail_body(losses, levels, weights, count_in, excess_in, count_out, excess_out):
+def tail_body(losses, levels, weights, sums_in, sums_out):
     rows = losses.shape[0]
+    row_block = rows if rows <= 512 else 32
+    depth = levels.shape[0]
     bf16 = jnp.bfloat16
     which = lax.broadcasted_iota(jnp.int32, (level_group, row_block), 0)
 
     def group(at, carry):
         span = pl.ds(pl.multiple_of(at * level_group, level_group), level_group)
         limits = levels[span, :]
-        count = count_in[span, :]
-        excess = excess_in[span, :]
+        second = pl.ds(pl.multiple_of(depth + at * level_group, level_group), level_group)
+        count = sums_in[span, :]
+        excess = sums_in[second, :]
         for start in range(0, rows, row_block):
             row_weights = weights[:, pl.ds(start, row_block)]
             for level in range(level_group):
@@ -31,43 +33,42 @@
                 limit = jnp.broadcast_to(limits[level : level + 1, :], (32, lane_block))
                 smooth, products = [], []
                 for row in range(start, start + row_block, 32):
-                    diff = (losses[pl.ds(row, 32), :] - limit).astype(bf16)
-                    twice = jnp.tanh(diff) + bf16(1)
+                    diff = losses[pl.ds(row, 32), :] - limit
+                    twice = (jnp.tanh(diff) + 1.0).astype(bf16)
                     smooth.append(twice)
-                    products.append(twice * diff)
+                    products.append(twice * diff.astype(bf16))
                 count = count + jnp.dot(
                     picked, jnp.concatenate(smooth, 0), preferred_element_type=jnp.float32
                 )
                 excess = excess + jnp.dot(
                     picked, jnp.concatenate(products, 0), preferred_element_type=jnp.float32
                 )
-        count_out[span, :] = count
-        excess_out[span, :] = excess
+        sums_out[span, :] = count
+        sums_out[second, :] = excess
         return carry
 
-    lax.fori_loop(0, levels.shape[0] // level_group, group, 0)
-
-
-def tail_sums(losses, levels, weights, count, excess):
+    lax.fori_loop(0, depth // level_group, group, 0)
+
+
+def tail_sums(losses, levels, weights, sums):
     rows, width = losses.shape
     depth = levels.shape[0]
-    table = pl.BlockSpec((depth, lane_block), lambda i: (0, i))
+    both = pl.BlockSpec((2 * depth, lane_block), lambda i: (0, i))
     return pl.pallas_call(
         tail_body,
-        out_shape=[jax.ShapeDtypeStruct((depth, width), jnp.float32)] * 2,
+        out_shape=jax.ShapeDtypeStruct((2 * depth, width), jnp.float32),
         grid=(width // lane_block,),
         in_specs=[
             pl.BlockSpec((rows, lane_block), lambda i: (0, i)),
-            table,
+            pl.BlockSpec((depth, lane_block), lambda i: (0, i)),
             pl.BlockSpec((8, rows), lambda i: (0, 0)),
-            table,
-            table,
+            both,
         ],
-        out_specs=[table, table],
-        input_output_aliases={3: 0, 4: 1},
+        out_specs=both,
+        input_output_aliases={3: 0},
         cost_estimate=pl.CostEstimate(flops=1024, transcendentals=0, bytes_accessed=1024),
         name="tail_sums",
-    )(losses, levels, weights, count, excess)
+    )(losses, levels, weights, sums)
 
 
 def together(*values):
@@ -105,65 +106,77 @@
             + last.astype(f32)
         )
 
-    split = rows // 2
+    cuts = [0] + [rows * c // 32 for c in (13, 24)] + [rows]
+    pieces = [slice(i, j) for i, j in zip(cuts, cuts[1:])]
     limits = columns(thresholds, 2 * low + high, quarter) * half_inverse
-    zero = jnp.zeros(limits.shape, f32)
-
-    weights_pair = jnp.stack([weights, swap(weights, "port", 1)])
-    weights_far = swap(weights_pair, "port", 2)
-    group_total = jnp.sum(weights_pair.astype(f32)) + jnp.sum(weights_far.astype(f32))
-    total = group_total + swap(group_total, "scen", 1)
-    block_weights = [
-        weights_pair[0],
-        weights_pair[1],
-        weights_far[:, :split].reshape(-1),
-        weights_far[:, split:].reshape(-1),
-    ]
-
-    def tails(losses, which, sums):
-        w = block_weights[which]
-        return tail_sums(losses, limits, jnp.broadcast_to(w[None], (8, w.shape[0])), *sums)
-
-    sums = (zero, zero)
-    far0 = swap(shocks[:split], "port", 2)
+    depth = limits.shape[0]
+
+    blocks = 2 + len(pieces)
+    partial, got, last = {}, {}, {}
+    sums = jnp.zeros((2 * depth, quarter), f32)
+    coming = swap(shocks[pieces[0]], "port", 2)
     sibling = swap(shocks, "port", 1)
-    p0 = product(shocks)
-    a0, sibling, p0 = together(send_a(p0), sibling, p0)
-
-    a0 = swap(a0, "fac", 1)
-    p1 = product(sibling)
-    a0, p1, far0 = together(a0, p1, far0)
-
-    b0, a1, far0, far1 = together(send_b(p0, a0), send_a(p1), far0, shocks[split:])
-    a1 = swap(a1, "fac", 1)
-    b0 = swap(b0, "fac", 2)
-    far1 = swap(far1, "port", 2)
-    p2 = product(jnp.concatenate([far0, swap(far0, "port", 1)], 0))
-    a1, b0, p2, far1 = together(a1, b0, p2, far1)
-
-    b1, a2, far1, done = together(send_b(p1, a1), send_a(p2), far1, finish(p0, a0, b0))
-    a2 = swap(a2, "fac", 1)
-    b1 = swap(b1, "fac", 2)
-    p3 = product(jnp.concatenate([far1, swap(far1, "port", 1)], 0))
-    sums = tails(together(done, p3)[0], 0, sums)
-    a2, b1, p3, sums = together(a2, b1, p3, sums)
-
-    b2, a3, done, sums = together(send_b(p2, a2), send_a(p3), finish(p1, a1, b1), sums)
-    a3 = swap(a3, "fac", 1)
-    b2 = swap(b2, "fac", 2)
-    sums = tails(done, 1, sums)
-    a3, b2, sums = together(a3, b2, sums)
-
-    b3, done, sums = together(send_b(p3, a3), finish(p2, a2, b2), sums)
-    b3 = swap(b3, "fac", 2)
-    sums = tails(done, 2, sums)
-    b3, sums = together(b3, sums)
-    count, excess = tails(finish(p3, a3, b3), 3, sums)
-
-    sums = jnp.concatenate([count * 0.5, excess * (0.5 / half_inverse)], 0)
+    first = product(shocks)
+    to_a, sibling, partial[0] = together(send_a(first), sibling, first)
+
+    for step in range(blocks + 1):
+        if step < blocks:
+            got[step] = swap(to_a, "fac", 1)
+        if step > 0:
+            last[step - 1] = swap(to_b, "fac", 2)
+        nearest = None
+        if 1 <= step < len(pieces):
+            nearest = swap(to_far, "port", 2)
+        if step == 0:
+            partial[1] = product(sibling)
+            later = together(shocks, partial[1])[0]
+            to_fars = {k: later[piece] for k, piece in enumerate(pieces) if k}
+        elif step + 1 < blocks:
+            partial[step + 1] = product(jnp.concatenate([coming, swap(coming, "port", 1)], 0))
+        if step > 1:
+            if step + 1 < blocks:
+                done = together(done, partial[step + 1])[0]
+            sums = tail_sums(done, limits, block_weights[step - 2], sums)
+        if step == 0:
+            nearest = coming
+            pair = jnp.stack([weights, swap(weights, "port", 1)])
+            small = (pair, limits)
+        elif step == 1:
+            small = swap(pair, "port", 2)
+        elif step == 2:
+            small = swap(group_total, "scen", 1)
+        else:
+            small = None
+        got, last, partial, nearest, sums, to_fars, small = together(
+            got, last, partial, nearest, sums, to_fars, small
+        )
+        if step == 0:
+            pair, limits = small
+        elif step == 1:
+            group_total = jnp.sum(pair.astype(f32)) + jnp.sum(small.astype(f32))
+            block_weights = [pair[0], pair[1]]
+            block_weights += [small[:, piece].reshape(-1) for piece in pieces]
+            block_weights = [jnp.broadcast_to(w[None], (8, w.shape[0])) for w in block_weights]
+        elif step == 2:
+            total = group_total + small
+        coming = nearest
+        if step < blocks:
+            to_b = send_b(partial[step], got[step])
+        if step + 1 < blocks:
+            to_a = send_a(partial[step + 1])
+        if step + 1 < len(pieces):
+            to_far = to_fars[step + 1]
+        else:
+            to_far = None
+        if step > 0:
+            done = finish(partial[step - 1], got[step - 1], last[step - 1])
+        else:
+            done = None
+        to_a, to_b, to_far, coming, done, sums = together(to_a, to_b, to_far, coming, done, sums)
+    sums = tail_sums(done, limits, block_weights[blocks - 1], sums)
+
     sums = sums + swap(sums, "scen", 1)
-    depth = limits.shape[0]
-    count, excess = sums[:depth], sums[depth:]
+    count, excess = sums[:depth] * 0.5, sums[depth:] * (0.5 / half_inverse)
     result = jnp.concatenate([excess / jnp.maximum(count, 1.0), count / total], 0)
     parts = [result] + [swap(result, "fac", flip) for flip in (1, 2, 3)]
 

time: 267 us -> 250 us (0.936)
  waiting for transfers between devices: 108 us -> 66.1 us
  matrix products: 50.9 us -> 60.3 us
  Pallas kernels: 50.1 us -> 58.1 us
  local copies, waits for them, and re-layouts: 10.7 us -> 16.4 us
    ppermute x20 -> x24, waiting for transfers between devices: 108 us -> 66.1 us  [swap(): lax.ppermute(v, axis, [(i, i ^ flip) for i in range(lax.axis_size(axis))])]
    dot_general x4 -> x5, matrix products: 50.9 us -> 60.3 us  [product(): jnp.dot(block, loading, preferred_element_type=f32) * half_inverse]
    pallas_call x4 -> x5, Pallas kernels: 50.1 us -> 58.1 us  [tail_sums(): pl.pallas_call(tail_body, out_shape=jax.ShapeDtypeStruct((2 * depth, widt...]
    dynamic_slice x4 -> x5, local copies, waits for them, and re-layouts: 1.15 us -> 5.88 us  [columns(): return lax.dynamic_slice_in_dim(v, k * width, width, 1)]
    convert_element_type x3 -> x4, other arithmetic: 4.52 us -> 6.01 us  [send_b(): (columns(partial, at, quarter).astype(f32) + columns(got, 1 - high, quart...]
    add x4 -> x5, other arithmetic: 10.1 us -> 11.4 us  [finish(): columns(partial, at, quarter).astype(f32)]
    ppermute x20 -> x24, starting transfers between devices: 23.5 us -> 23.7 us  [swap(): lax.ppermute(v, axis, [(i, i ^ flip) for i in range(lax.axis_size(axis))])]
  transfers between devices with their start and end apart: 20 -> 24, of which waited for: 12 -> 11; matrix products, arithmetic and copies ran while one was open for 23% -> 29% of each run, Pallas kernels for 14% -> 20%
where the time goes in v3:
time: 250 us; the launch traced here: 249 us
  waiting for transfers between devices  66.1 us (26%)
  matrix products  60.3 us (24%)
  Pallas kernels  58.1 us (23%)
  starting transfers between devices  23.7 us (9%)
  other arithmetic  21.5 us (9%)
  local copies, waits for them, and re-layouts  16.4 us (7%)
  between operations  2.7 us (1%)
    ppermute x24, waiting for transfers between devices, swap(): lax.ppermute(v, axis, [(i, i ^ flip) for i in range(lax.axis_size(axis))])  66.1 us
    dot_general x5, matrix products, product(): jnp.dot(block, loading, preferred_element_type=f32) * half_inverse  60.3 us
    pallas_call x5, Pallas kernels, tail_sums(): pl.pallas_call(tail_body, out_shape=jax.ShapeDtypeStruct((2 * depth, widt...  58.1 us
    ppermute x24, starting transfers between devices, swap(): lax.ppermute(v, axis, [(i, i ^ flip) for i in range(lax.axis_size(axis))])  23.7 us
    add x5, other arithmetic, finish(): columns(partial, at, quarter).astype(f32)  11.4 us
    convert_element_type x4, other arithmetic, send_b(): (columns(partial, at, quarter).astype(f32) + columns(got, 1 - high, quart...  6.01 us
    dynamic_slice x5, local copies, waits for them, and re-layouts, columns(): return lax.dynamic_slice_in_dim(v, k * width, width, 1)  5.88 us
  transfers between devices with their start and end apart: 24, of which 11 were waited for; matrix products, arithmetic and copies ran while one was open for 29% of the time, Pallas kernels for 20%

profile of v3, /device:TPU:8, one launch (start us, length us, event | category | flops | bytes accessed | tf_op | source)
XLA Modules:
  0.0 248.7 jit_solution(12162212437557642319)
XLA Ops:
  0.7 2.9 %slice.36 = bf16[208,4096]{1,0:T(8,128)(2,1)} slice(bf16[512,4096]{1,0:T(8,128)(2,1)} %param.4), slice={[0:208], [0:4096]} | slice | bytes 3407872 | tf_op jit(solution)/shard_map/slice | solution.py:117
  5.3 13.6 %multiply_convert_fusion.1 = f16[512,2048]{1,0:T(8,128)(2,1)S(1)} fusion(bf16[512,4096]{1,0:T(8,128)(2,1)} %param.4, bf16[4096,2048]{1,0:T(8,128)(2,1)} %param.5), kind=kOutput, calls=%fused_computation.1 | convolution fusion | flops 8592031744 | bytes 23068672 | tf_op jit(solution)/shard_map/dot_general | solution.py:92
  23.6 13.9 %multiply_convert_fusion = f16[512,2048]{1,0:T(8,128)(2,1)S(1)} fusion(bf16[512,4096]{1,0:T(8,128)(2,1)} %collective-permute-done, bf16[4096,2048]{1,0:T(8,128)(2,1)} %param.5), kind=kOutput, calls=%fused_computation | convolution fusion | flops 8592031744 | bytes 23068672 | tf_op jit(solution)/shard_map/dot_general | solution.py:92
  38.7 4.8 %collective-permute-done.2 = bf16[208,4096]{1,0:T(8,128)(2,1)} collective-permute-done((bf16[208,4096]{1,0:T(8,128)(2,1)}, bf16[208,4096]{1,0:T(8,128)(2,1)}, u32[]{:S(2)}, u32[]{:S(2)}) %collective-permute-start.2) | collective-permute-done | bytes 1703968 | tf_op jit(solution)/shard_map/ppermute | solution.py:86
  43.5 5.2 %collective-permute-done.1 = f16[512,1024]{1,0:T(8,128)(2,1)S(1)} collective-permute-done((f16[512,1024]{1,0:T(8,128)(2,1)}, f16[512,1024]{1,0:T(8,128)(2,1)S(1)}, u32[]{:S(2)}, u32[]{:S(2)}) %collective-permute-start.1) | collective-permute-done | bytes 1048608 | tf_op jit(solution)/shard_map/ppermute | solution.py:86
  50.2 2.0 add_convert_fusion.1
  52.7 2.6 %collective-permute-start.5 = (f16[512,512]{1,0:T(8,128)(2,1)}, f16[512,512]{1,0:T(8,128)(2,1)S(1)}, u32[]{:S(2)}, u32[]{:S(2)}) collective-permute-start(f16[512,512]{1,0:T(8,128)(2,1)} %add_convert_fusion.1), channel_id=1, source_target_pairs={{0,4},{2,6},{4,0},{6,2},{1,5},{3,7},{5,1},{7,3},{8,12},{10,14},{12... | collective-permute-start | bytes 1572872 | tf_op jit(solution)/shard_map/ppermute | solution.py:86
  57.3 11.7 %multiply_convert_fusion.2 = f16[416,2048]{1,0:T(8,128)(2,1)S(1)} fusion(bf16[4096,2048]{1,0:T(8,128)(2,1)} %param.5, bf16[208,4096]{1,0:T(8,128)(2,1)} %collective-permute-done.6, bf16[208,4096]{1,0:T(8,128)(2,1)} %collective-permute-done.2), kind=kOutput, calls=%fused_computation.6 | convolution fusion | flops 6987841536 | bytes 21889024 | tf_op jit(solution)/shard_map/dot_general | solution.py:92
  69.0 19.8 %collective-permute-done.8 = bf16[2,512]{1,0:T(2,128)(2,1)S(1)} collective-permute-done((bf16[2,512]{1,0:T(2,128)(2,1)S(1)}, bf16[2,512]{1,0:T(2,128)(2,1)S(1)}, u32[]{:S(2)}, u32[]{:S(2)}) %collective-permute-start.8) | collective-permute-done | bytes 2080 | tf_op jit(solution)/shard_map/ppermute | solution.py:86
  91.5 2.8 %convert_add_fusion.1 = (f32[512,512]{1,0:T(8,128)}, f16[512,512]{1,0:T(8,128)(2,1)}) fusion(f16[512,512]{1,0:T(8,128)(2,1)S(1)} %collective-permute-done.5, f16[512,1024]{1,0:T(8,128)(2,1)S(1)} %copy-done.6, s32[]{:T(128)S(6)} %select_n.110, f16[512,2048]{1,0:T(8,128)(2,1)} %copy-done.1, s32[]{:T(128)S(6)} %select_n.107, ...), kind=kLoop, calls=%fused_computation.19 | loop fusion | flops 2359296 | bytes 4194320 | tf_op jit(solution)/shard_map/add | solution.py:104
  95.2 1.7 collective-permute-start.10
  99.3 2.9 %collective-permute-start.13 = (f32[]{:T(128)}, f32[]{:T(128)}, u32[]{:S(2)}, u32[]{:S(2)}) collective-permute-start(f32[]{:T(128)} %add.122), channel_id=1, source_target_pairs={{0,1},{1,0},{2,3},{3,2},{4,5},{5,4},{6,7},{7,6},{8,9},{9,8},{10,11... | collective-permute-start | bytes 20 | tf_op jit(solution)/shard_map/ppermute | solution.py:86
  102.2 10.5 %fusion.9 = f16[352,2048]{1,0:T(8,128)(2,1)S(1)} fusion(bf16[4096,2048]{1,0:T(8,128)(2,1)} %param.5, bf16[176,4096]{1,0:T(8,128)(2,1)} %collective-permute-done.11, bf16[176,4096]{1,0:T(8,128)(2,1)} %collective-permute-done.7), kind=kOutput, calls=%fused_computation.11 | convolution fusion | flops 5912788992 | bytes 21102592 | tf_op jit(solution)/shard_map/dot_general | solution.py:92
  114.0 13.6 %tail_sums.5.sums_in = f32[128,512]{1,0:T(8,128)} custom-call(f32[512,512]{1,0:T(8,128)} %get-tuple-element.109.losses, f32[64,512]{1,0:T(8,128)} %dynamic-slice_multiply_fusion.levels, bf16[8,512]{1,0:T(8,128)(2,1)} %broadcast_in_dim.40.weights, f32[128,512]{1,0:T(8,128)} %broadcast_in_dim.38.sums_in), custom_call_target="tpu_custom_call", output_to_operand_aliasing={{}: (3, {})} | custom-call | flops 1024 | bytes 1024 | tf_op jit(solution)/shard_map/tail_sums/pallas_call | solution.py:57
  128.8 2.0 add_convert_fusion.2
  130.8 2.3 convert_add_fusion.losses
  133.2 1.6 collective-permute-start.14
  134.8 1.6 collective-permute-start.15
  136.3 10.6 %fusion.12 = f16[256,2048]{1,0:T(8,128)(2,1)S(1)} fusion(bf16[4096,2048]{1,0:T(8,128)(2,1)} %param.5, bf16[128,4096]{1,0:T(8,128)(2,1)S(1)} %collective-permute-done.16, bf16[128,4096]{1,0:T(8,128)(2,1)} %collective-permute-done.12), kind=kOutput, calls=%fused_computation.13 | convolution fusion | flops 4300210176 | bytes 19922944 | tf_op jit(solution)/shard_map/dot_general | solution.py:92
  147.5 13.6 %tail_sums.6.sums_in = f32[128,512]{1,0:T(8,128)} custom-call(f32[512,512]{1,0:T(8,128)} %convert_add_fusion.losses, f32[64,512]{1,0:T(8,128)} %dynamic-slice_multiply_fusion.levels, bf16[8,512]{1,0:T(8,128)(2,1)} %broadcast_in_dim.42.weights, f32[128,512]{1,0:T(8,128)} %tail_sums.5.sums_in), custom_call_target="tpu_custom_call", output_to_operand_aliasing={{}: (3, {})} | custom-call | flops 1024 | bytes 1024 | tf_op jit(solution)/shard_map/tail_sums/pallas_call | solution.py:57
  164.1 2.3 convert_add_fusion.2.losses
  168.9 11.7 %tail_sums.7.sums_in = f32[128,512]{1,0:T(8,128)} custom-call(f32[416,512]{1,0:T(8,128)} %convert_add_fusion.2.losses, f32[64,512]{1,0:T(8,128)} %dynamic-slice_multiply_fusion.levels, bf16[8,416]{1,0:T(8,128)(2,1)} %broadcast_in_dim.44.weights, f32[128,512]{1,0:T(8,128)} %tail_sums.6.sums_in), custom_call_target="tpu_custom_call", output_to_operand_aliasing={{}: (3, {})} | custom-call | flops 1024 | bytes 1024 | tf_op jit(solution)/shard_map/tail_sums/pallas_call | solution.py:57
  180.7 7.5 %collective-permute-done.18 = f16[352,512]{1,0:T(8,128)(2,1)} collective-permute-done((f16[352,512]{1,0:T(8,128)(2,1)}, f16[352,512]{1,0:T(8,128)(2,1)}, u32[]{:S(2)}, u32[]{:S(2)}) %collective-permute-start.18) | collective-permute-done | bytes 360480 | tf_op jit(solution)/shard_map/ppermute | solution.py:86
  189.2 2.1 convert_add_fusion.3.losses
  192.6 10.6 %tail_sums.8.sums_in = f32[128,512]{1,0:T(8,128)} custom-call(f32[352,512]{1,0:T(8,128)} %convert_add_fusion.3.losses, f32[64,512]{1,0:T(8,128)} %dynamic-slice_multiply_fusion.levels, bf16[8,352]{1,0:T(8,128)(2,1)} %broadcast_in_dim.46.weights, f32[128,512]{1,0:T(8,128)} %tail_sums.7.sums_in), custom_call_target="tpu_custom_call", output_to_operand_aliasing={{}: (3, {})} | custom-call | flops 1024 | bytes 1024 | tf_op jit(solution)/shard_map/tail_sums/pallas_call | solution.py:57
  203.2 1.9 convert_add_fusion.4.losses
  205.7 8.6 %tail_sums.9 = f32[128,512]{1,0:T(8,128)} custom-call(f32[256,512]{1,0:T(8,128)} %convert_add_fusion.4.losses, f32[64,512]{1,0:T(8,128)} %dynamic-slice_multiply_fusion.levels, bf16[8,256]{1,0:T(8,128)(2,1)} %broadcast_in_dim.48.weights, f32[128,512]{1,0:T(8,128)} %tail_sums.8.sums_in), custom_call_target="tpu_custom_call", output_to_operand_aliasing={{}: (3, {})} | custom-call | flops 1024 | bytes 1024 | tf_op jit(solution)/shard_map/tail_sums/pallas_call | solution.py:57
  216.4 5.1 %collective-permute-done.20 = f32[128,512]{1,0:T(8,128)S(1)} collective-permute-done((f32[128,512]{1,0:T(8,128)}, f32[128,512]{1,0:T(8,128)S(1)}, u32[]{:S(2)}, u32[]{:S(2)}) %collective-permute-start.20) | collective-permute-done | bytes 262176 | tf_op jit(solution)/shard_map/ppermute | solution.py:86
  222.6 2.4 collective-permute-start.21
  226.5 7.4 %collective-permute-done.21 = f32[128,512]{1,0:T(8,128)S(1)} collective-permute-done((f32[128,512]{1,0:T(8,128)S(1)}, f32[128,512]{1,0:T(8,128)S(1)}, u32[]{:S(2)}, u32[]{:S(2)}) %collective-permute-start.21) | collective-permute-done | bytes 262176 | tf_op jit(solution)/shard_map/ppermute | solution.py:86
  233.9 9.0 %collective-permute-done.22 = f32[128,512]{1,0:T(8,128)S(1)} collective-permute-done((f32[128,512]{1,0:T(8,128)S(1)}, f32[128,512]{1,0:T(8,128)S(1)}, u32[]{:S(2)}, u32[]{:S(2)}) %collective-permute-start.22) | collective-permute-done | bytes 262176 | tf_op jit(solution)/shard_map/ppermute | solution.py:86
  242.9 4.6 %collective-permute-done.23 = f32[128,512]{1,0:T(8,128)S(1)} collective-permute-done((f32[128,512]{1,0:T(8,128)S(1)}, f32[128,512]{1,0:T(8,128)S(1)}, u32[]{:S(2)}, u32[]{:S(2)}) %collective-permute-start.23) | collective-permute-done | bytes 262176 | tf_op jit(solution)/shard_map/ppermute | solution.py:86
  (83 shorter events, 33.3 us)
Async XLA Ops:
  0.6 4.5 %copy-start.7 = (bf16[512]{0:T(512)(128)(2,1)S(1)}, bf16[512]{0:T(512)(128)(2,1)}, u32[]{:S(2)}) copy-start(bf16[512]{0:T(512)(128)(2,1)} %param.7) | copy-start | bytes 3076
  0.6 22.4 %collective-permute-start = (bf16[512,4096]{1,0:T(8,128)(2,1)}, bf16[512,4096]{1,0:T(8,128)(2,1)}, u32[]{:S(2)}, u32[]{:S(2)}) collective-permute-start(bf16[512,4096]{1,0:T(8,128)(2,1)} %param.4), channel_id=1, source_target_pairs={{0,8},{8,0},{16,24},{24,16},{1,9},{9,1},{17,25},{25,17},{2,10},{10... | collective-permute-start | bytes 12582920 | tf_op jit(solution)/shard_map/ppermute | solution.py:86
  3.6 39.9 %collective-permute-start.2 = (bf16[208,4096]{1,0:T(8,128)(2,1)}, bf16[208,4096]{1,0:T(8,128)(2,1)}, u32[]{:S(2)}, u32[]{:S(2)}) collective-permute-start(bf16[208,4096]{1,0:T(8,128)(2,1)} %slice.36), channel_id=1, source_target_pairs={{0,16},{8,24},{16,0},{24,8},{1,17},{9,25},{17,1},{25,9},{2,18},{10... | collective-permute-start | bytes 5111816 | tf_op jit(solution)/shard_map/ppermute | solution.py:86
  5.1 18.0 %collective-permute-start.3 = (bf16[512]{0:T(512)(128)(2,1)S(1)}, bf16[512]{0:T(512)(128)(2,1)S(1)}, u32[]{:S(2)}, u32[]{:S(2)}) collective-permute-start(bf16[512]{0:T(512)(128)(2,1)S(1)} %copy-done.7), channel_id=1, source_target_pairs={{0,8},{8,0},{16,24},{24,16},{1,9},{9,1},{17,25},{25,17},{2,10},{10... | collective-permute-start | bytes 3080 | tf_op jit(solution)/shard_map/ppermute | solution.py:86
  18.9 1.3 copy-start.1
  23.1 14.4 %copy-start = (bf16[512,4096]{1,0:T(8,128)(2,1)S(1)}, bf16[512,4096]{1,0:T(8,128)(2,1)}, u32[]{:S(2)}) copy-start(bf16[512,4096]{1,0:T(8,128)(2,1)} %param.4) | copy-start | bytes 12582916
  23.1 25.6 %collective-permute-start.1 = (f16[512,1024]{1,0:T(8,128)(2,1)}, f16[512,1024]{1,0:T(8,128)(2,1)S(1)}, u32[]{:S(2)}, u32[]{:S(2)}) collective-permute-start(f16[512,1024]{1,0:T(8,128)(2,1)} %constant_dynamic-slice_fusion.4), channel_id=1, source_target_pairs={{0,2},{2,0},{4,6},{6,4},{1,3},{3,1},{5,7},{7,5},{8,10},{10,8},{12,... | collective-permute-start | bytes 3145736 | tf_op jit(solution)/shard_map/ppermute | solution.py:86
  48.7 1.4 copy-start.5
  52.2 5.1 %collective-permute-start.6 = (bf16[208,4096]{1,0:T(8,128)(2,1)}, bf16[208,4096]{1,0:T(8,128)(2,1)}, u32[]{:S(2)}, u32[]{:S(2)}) collective-permute-start(bf16[208,4096]{1,0:T(8,128)(2,1)} %collective-permute-done.2), channel_id=1, source_target_pairs={{0,8},{8,0},{16,24},{24,16},{1,9},{9,1},{17,25},{25,17},{2,10},{10... | collective-permute-start | bytes 5111816 | tf_op jit(solution)/shard_map/ppermute | solution.py:86
  52.2 39.3 %copy-start.6 = (f16[512,1024]{1,0:T(8,128)(2,1)S(1)}, f16[512,1024]{1,0:T(8,128)(2,1)}, u32[]{:S(2)}) copy-start(f16[512,1024]{1,0:T(8,128)(2,1)} %copy-done.5) | copy-start | bytes 3145732
  52.2 38.0 %collective-permute-start.4 = (f16[512,1024]{1,0:T(8,128)(2,1)}, f16[512,1024]{1,0:T(8,128)(2,1)S(1)}, u32[]{:S(2)}, u32[]{:S(2)}) collective-permute-start(f16[512,1024]{1,0:T(8,128)(2,1)} %constant_dynamic-slice_fusion.3), channel_id=1, source_target_pairs={{0,2},{2,0},{4,6},{6,4},{1,3},{3,1},{5,7},{7,5},{8,10},{10,8},{12,... | collective-permute-start | bytes 3145736 | tf_op jit(solution)/shard_map/ppermute | solution.py:86
  52.7 37.6 %collective-permute-start.5 = (f16[512,512]{1,0:T(8,128)(2,1)}, f16[512,512]{1,0:T(8,128)(2,1)S(1)}, u32[]{:S(2)}, u32[]{:S(2)}) collective-permute-start(f16[512,512]{1,0:T(8,128)(2,1)} %add_convert_fusion.1), channel_id=1, source_target_pairs={{0,4},{2,6},{4,0},{6,2},{1,5},{3,7},{5,1},{7,3},{8,12},{10,14},{12... | collective-permute-start | bytes 1572872 | tf_op jit(solution)/shard_map/ppermute | solution.py:86
  55.2 35.0 %collective-permute-start.7 = (bf16[176,4096]{1,0:T(8,128)(2,1)S(1)}, bf16[176,4096]{1,0:T(8,128)(2,1)}, u32[]{:S(2)}, u32[]{:S(2)}) collective-permute-start(bf16[176,4096]{1,0:T(8,128)(2,1)S(1)} %slice.37), channel_id=1, source_target_pairs={{0,16},{8,24},{16,0},{24,8},{1,17},{9,25},{17,1},{25,9},{2,18},{10... | collective-permute-start | bytes 4325384 | tf_op jit(solution)/shard_map/ppermute | solution.py:86
  55.8 33.0 %collective-permute-start.8 = (bf16[2,512]{1,0:T(2,128)(2,1)S(1)}, bf16[2,512]{1,0:T(2,128)(2,1)S(1)}, u32[]{:S(2)}, u32[]{:S(2)}) collective-permute-start(bf16[2,512]{1,0:T(2,128)(2,1)S(1)} %pad_maximum_fusion.2), channel_id=1, source_target_pairs={{0,16},{8,24},{16,0},{24,8},{1,17},{9,25},{17,1},{25,9},{2,18},{10... | collective-permute-start | bytes 6152 | tf_op jit(solution)/shard_map/ppermute | solution.py:86
  69.0 25.3 %copy-start.2 = (f16[416,2048]{1,0:T(8,128)(2,1)}, f16[416,2048]{1,0:T(8,128)(2,1)S(1)}, u32[]{:S(2)}) copy-start(f16[416,2048]{1,0:T(8,128)(2,1)S(1)} %multiply_convert_fusion.2) | copy-start | bytes 5111812
  90.2 4.1 %copy-start.3 = (f16[512,1024]{1,0:T(8,128)(2,1)}, f16[512,1024]{1,0:T(8,128)(2,1)S(1)}, u32[]{:S(2)}) copy-start(f16[512,1024]{1,0:T(8,128)(2,1)S(1)} %collective-permute-done.4) | copy-start | bytes 3145732
  94.3 7.9 %collective-permute-start.11 = (bf16[176,4096]{1,0:T(8,128)(2,1)}, bf16[176,4096]{1,0:T(8,128)(2,1)}, u32[]{:S(2)}, u32[]{:S(2)}) collective-permute-start(bf16[176,4096]{1,0:T(8,128)(2,1)} %collective-permute-done.7), channel_id=1, source_target_pairs={{0,8},{8,0},{16,24},{24,16},{1,9},{9,1},{17,25},{25,17},{2,10},{10... | collective-permute-start | bytes 4325384 | tf_op jit(solution)/shard_map/ppermute | solution.py:86
  94.9 32.8 %collective-permute-start.9 = (f16[416,1024]{1,0:T(8,128)(2,1)}, f16[416,1024]{1,0:T(8,128)(2,1)}, u32[]{:S(2)}, u32[]{:S(2)}) collective-permute-start(f16[416,1024]{1,0:T(8,128)(2,1)} %constant_dynamic-slice_fusion.2), channel_id=1, source_target_pairs={{0,2},{2,0},{4,6},{6,4},{1,3},{3,1},{5,7},{7,5},{8,10},{10,8},{12,... | collective-permute-start | bytes 2555912 | tf_op jit(solution)/shard_map/ppermute | solution.py:86
  95.2 32.6 %collective-permute-start.10 = (f16[512,512]{1,0:T(8,128)(2,1)}, f16[512,512]{1,0:T(8,128)(2,1)}, u32[]{:S(2)}, u32[]{:S(2)}) collective-permute-start(f16[512,512]{1,0:T(8,128)(2,1)} %get-tuple-element.105), channel_id=1, source_target_pairs={{0,4},{2,6},{4,0},{6,2},{1,5},{3,7},{5,1},{7,3},{8,12},{10,14},{12... | collective-permute-start | bytes 1572872 | tf_op jit(solution)/shard_map/ppermute | solution.py:86
  96.9 30.9 %collective-permute-start.12 = (bf16[128,4096]{1,0:T(8,128)(2,1)}, bf16[128,4096]{1,0:T(8,128)(2,1)}, u32[]{:S(2)}, u32[]{:S(2)}) collective-permute-start(bf16[128,4096]{1,0:T(8,128)(2,1)} %slice.38), channel_id=1, source_target_pairs={{0,16},{8,24},{16,0},{24,8},{1,17},{9,25},{17,1},{25,9},{2,18},{10... | collective-permute-start | bytes 3145736 | tf_op jit(solution)/shard_map/ppermute | solution.py:86
  99.3 28.3 %collective-permute-start.13 = (f32[]{:T(128)}, f32[]{:T(128)}, u32[]{:S(2)}, u32[]{:S(2)}) collective-permute-start(f32[]{:T(128)} %add.122), channel_id=1, source_target_pairs={{0,1},{1,0},{2,3},{3,2},{4,5},{5,4},{6,7},{7,6},{8,9},{9,8},{10,11... | collective-permute-start | bytes 20 | tf_op jit(solution)/shard_map/ppermute | solution.py:86
  127.6 3.2 %copy-start.4 = (f16[512,1024]{1,0:T(8,128)(2,1)S(1)}, f16[512,1024]{1,0:T(8,128)(2,1)}, u32[]{:S(2)}) copy-start(f16[512,1024]{1,0:T(8,128)(2,1)} %copy-done.3) | copy-start | bytes 3145732
  133.2 3.2 %collective-permute-start.16 = (bf16[128,4096]{1,0:T(8,128)(2,1)}, bf16[128,4096]{1,0:T(8,128)(2,1)S(1)}, u32[]{:S(2)}, u32[]{:S(2)}) collective-permute-start(bf16[128,4096]{1,0:T(8,128)(2,1)} %collective-permute-done.12), channel_id=1, source_target_pairs={{0,8},{8,0},{16,24},{24,16},{1,9},{9,1},{17,25},{25,17},{2,10},{10... | collective-permute-start | bytes 3145736 | tf_op jit(solution)/shard_map/ppermute | solution.py:86
  133.2 29.1 %collective-permute-start.14 = (f16[352,1024]{1,0:T(8,128)(2,1)}, f16[352,1024]{1,0:T(8,128)(2,1)S(1)}, u32[]{:S(2)}, u32[]{:S(2)}) collective-permute-start(f16[352,1024]{1,0:T(8,128)(2,1)} %constant_dynamic-slice_fusion.1), channel_id=1, source_target_pairs={{0,2},{2,0},{4,6},{6,4},{1,3},{3,1},{5,7},{7,5},{8,10},{10,8},{12,... | collective-permute-start | bytes 2162696 | tf_op jit(solution)/shard_map/ppermute | solution.py:86
  134.8 27.5 %collective-permute-start.15 = (f16[416,512]{1,0:T(8,128)(2,1)}, f16[416,512]{1,0:T(8,128)(2,1)}, u32[]{:S(2)}, u32[]{:S(2)}) collective-permute-start(f16[416,512]{1,0:T(8,128)(2,1)} %add_convert_fusion.2), channel_id=1, source_target_pairs={{0,4},{2,6},{4,0},{6,2},{1,5},{3,7},{5,1},{7,3},{8,12},{10,14},{12... | collective-permute-start | bytes 1277960 | tf_op jit(solution)/shard_map/ppermute | solution.py:86
  166.4 21.7 %collective-permute-start.17 = (f16[256,1024]{1,0:T(8,128)(2,1)}, f16[256,1024]{1,0:T(8,128)(2,1)}, u32[]{:S(2)}, u32[]{:S(2)}) collective-permute-start(f16[256,1024]{1,0:T(8,128)(2,1)} %constant_dynamic-slice_fusion), channel_id=1, source_target_pairs={{0,2},{2,0},{4,6},{6,4},{1,3},{3,1},{5,7},{7,5},{8,10},{10,8},{12,... | collective-permute-start | bytes 1572872 | tf_op jit(solution)/shard_map/ppermute | solution.py:86
  166.8 21.3 %collective-permute-start.18 = (f16[352,512]{1,0:T(8,128)(2,1)}, f16[352,512]{1,0:T(8,128)(2,1)}, u32[]{:S(2)}, u32[]{:S(2)}) collective-permute-start(f16[352,512]{1,0:T(8,128)(2,1)} %add_convert_fusion.3), channel_id=1, source_target_pairs={{0,4},{2,6},{4,0},{6,2},{1,5},{3,7},{5,1},{7,3},{8,12},{10,14},{12... | collective-permute-start | bytes 1081352 | tf_op jit(solution)/shard_map/ppermute | solution.py:86
  191.3 12.0 %collective-permute-start.19 = (f16[256,512]{1,0:T(8,128)(2,1)S(1)}, f16[256,512]{1,0:T(8,128)(2,1)S(1)}, u32[]{:S(2)}, u32[]{:S(2)}) collective-permute-start(f16[256,512]{1,0:T(8,128)(2,1)S(1)} %add_convert_fusion.4), channel_id=1, source_target_pairs={{0,4},{2,6},{4,0},{6,2},{1,5},{3,7},{5,1},{7,3},{8,12},{10,14},{12... | collective-permute-start | bytes 786440 | tf_op jit(solution)/shard_map/ppermute | solution.py:86
  214.3 7.2 %collective-permute-start.20 = (f32[128,512]{1,0:T(8,128)}, f32[128,512]{1,0:T(8,128)S(1)}, u32[]{:S(2)}, u32[]{:S(2)}) collective-permute-start(f32[128,512]{1,0:T(8,128)} %tail_sums.9), channel_id=1, source_target_pairs={{0,1},{1,0},{2,3},{3,2},{4,5},{5,4},{6,7},{7,6},{8,9},{9,8},{10,11... | collective-permute-start | bytes 786440 | tf_op jit(solution)/shard_map/ppermute | solution.py:86
  222.6 11.3 %collective-permute-start.21 = (f32[128,512]{1,0:T(8,128)S(1)}, f32[128,512]{1,0:T(8,128)S(1)}, u32[]{:S(2)}, u32[]{:S(2)}) collective-permute-start(f32[128,512]{1,0:T(8,128)S(1)} %pad_maximum_fusion.1), channel_id=1, source_target_pairs={{0,2},{2,0},{4,6},{6,4},{1,3},{3,1},{5,7},{7,5},{8,10},{10,8},{12,... | collective-permute-start | bytes 786440 | tf_op jit(solution)/shard_map/ppermute | solution.py:86
  224.9 17.9 %collective-permute-start.22 = (f32[128,512]{1,0:T(8,128)S(1)}, f32[128,512]{1,0:T(8,128)S(1)}, u32[]{:S(2)}, u32[]{:S(2)}) collective-permute-start(f32[128,512]{1,0:T(8,128)S(1)} %pad_maximum_fusion.1), channel_id=1, source_target_pairs={{0,4},{2,6},{4,0},{6,2},{1,5},{3,7},{5,1},{7,3},{8,12},{10,14},{12... | collective-permute-start | bytes 786440 | tf_op jit(solution)/shard_map/ppermute | solution.py:86
  225.4 22.0 %collective-permute-start.23 = (f32[128,512]{1,0:T(8,128)S(1)}, f32[128,512]{1,0:T(8,128)S(1)}, u32[]{:S(2)}, u32[]{:S(2)}) collective-permute-start(f32[128,512]{1,0:T(8,128)S(1)} %pad_maximum_fusion.1), channel_id=1, source_target_pairs={{0,6},{2,4},{4,2},{6,0},{1,7},{3,5},{5,3},{7,1},{8,14},{10,12},{12... | collective-permute-start | bytes 786440 | tf_op jit(solution)/shard_map/ppermute | solution.py:86

commit v4 on v3

--- a/solution.py
+++ b/solution.py
@@ -13,7 +13,7 @@
 level_group = 8
 
 
-def tail_body(losses, levels, weights, sums_in, sums_out):
+def tail_body(first, losses, levels, weights, sums_in, sums_out):
     rows = losses.shape[0]
     row_block = rows if rows <= 512 else 32
     depth = levels.shape[0]
@@ -27,7 +27,7 @@
         count = sums_in[span, :]
         excess = sums_in[second, :]
         for start in range(0, rows, row_block):
-            row_weights = weights[:, pl.ds(start, row_block)]
+            row_weights = weights[:, pl.ds(first + start, row_block)]
             for level in range(level_group):
                 picked = jnp.where(which == level, row_weights, jnp.zeros_like(row_weights))
                 limit = jnp.broadcast_to(limits[level : level + 1, :], (32, lane_block))
@@ -47,21 +47,22 @@
         sums_out[second, :] = excess
         return carry
 
-    lax.fori_loop(0, depth // level_group, group, 0)
-
-
-def tail_sums(losses, levels, weights, sums):
+    sums_out[pl.ds(2 * depth, 8), :] = sums_in[pl.ds(2 * depth, 8), :]
+    lax.fori_loop(0, depth // level_group, group, 0, unroll=4)
+
+
+def tail_sums(losses, levels, weights, first, sums):
     rows, width = losses.shape
     depth = levels.shape[0]
-    both = pl.BlockSpec((2 * depth, lane_block), lambda i: (0, i))
+    both = pl.BlockSpec((2 * depth + 8, lane_block), lambda i: (0, i))
     return pl.pallas_call(
-        tail_body,
-        out_shape=jax.ShapeDtypeStruct((2 * depth, width), jnp.float32),
+        functools.partial(tail_body, first),
+        out_shape=jax.ShapeDtypeStruct((2 * depth + 8, width), jnp.float32),
         grid=(width // lane_block,),
         in_specs=[
             pl.BlockSpec((rows, lane_block), lambda i: (0, i)),
             pl.BlockSpec((depth, lane_block), lambda i: (0, i)),
-            pl.BlockSpec((8, rows), lambda i: (0, 0)),
+            pl.BlockSpec(weights.shape, lambda i: (0, 0)),
             both,
         ],
         out_specs=both,
@@ -106,14 +107,14 @@
             + last.astype(f32)
         )
 
-    cuts = [0] + [rows * c // 32 for c in (13, 24)] + [rows]
+    cuts = [0] + [rows * c // 32 for c in (13, 25)] + [rows]
     pieces = [slice(i, j) for i, j in zip(cuts, cuts[1:])]
-    limits = columns(thresholds, 2 * low + high, quarter) * half_inverse
-    depth = limits.shape[0]
+    depth = thresholds.shape[0]
 
     blocks = 2 + len(pieces)
     partial, got, last = {}, {}, {}
-    sums = jnp.zeros((2 * depth, quarter), f32)
+    starts = [0, rows] + [2 * rows + 2 * cut for cut in cuts[:-1]]
+    sums = None
     coming = swap(shocks[pieces[0]], "port", 2)
     sibling = swap(shocks, "port", 1)
     first = product(shocks)
@@ -134,31 +135,35 @@
         elif step + 1 < blocks:
             partial[step + 1] = product(jnp.concatenate([coming, swap(coming, "port", 1)], 0))
         if step > 1:
+            k = step - 2
+            summed = (partial[k], got[k], last[k], pair, far_weights)
             if step + 1 < blocks:
-                done = together(done, partial[step + 1])[0]
-            sums = tail_sums(done, limits, block_weights[step - 2], sums)
+                summed = together(summed, partial[step + 1])[0]
+            *summed, pair, far_weights = summed
+            if sums is None:
+                group_total = jnp.sum(pair.astype(f32)) + jnp.sum(far_weights.astype(f32))
+                parts = [pair.reshape(-1)]
+                parts += [far_weights[:, piece].reshape(-1) for piece in pieces]
+                row_weights = jnp.broadcast_to(jnp.concatenate(parts)[None], (8, 4 * rows))
+                sums = jnp.concatenate(
+                    [jnp.zeros((2 * depth, quarter), f32), jnp.full((8, quarter), group_total)], 0
+                )
+            sums = tail_sums(finish(*summed), limits, row_weights, starts[k], sums)
         if step == 0:
             nearest = coming
-            pair = jnp.stack([weights, swap(weights, "port", 1)])
-            small = (pair, limits)
+            pair = small = jnp.stack([weights, swap(weights, "port", 1)])
         elif step == 1:
-            small = swap(pair, "port", 2)
-        elif step == 2:
-            small = swap(group_total, "scen", 1)
+            limits = columns(together(thresholds, partial[2])[0], 2 * low + high, quarter)
+            small = (swap(pair, "port", 2), limits * half_inverse)
         else:
             small = None
         got, last, partial, nearest, sums, to_fars, small = together(
             got, last, partial, nearest, sums, to_fars, small
         )
         if step == 0:
-            pair, limits = small
+            pair = small
         elif step == 1:
-            group_total = jnp.sum(pair.astype(f32)) + jnp.sum(small.astype(f32))
-            block_weights = [pair[0], pair[1]]
-            block_weights += [small[:, piece].reshape(-1) for piece in pieces]
-            block_weights = [jnp.broadcast_to(w[None], (8, w.shape[0])) for w in block_weights]
-        elif step == 2:
-            total = group_total + small
+            far_weights, limits = small
         coming = nearest
         if step < blocks:
             to_b = send_b(partial[step], got[step])
@@ -168,15 +173,14 @@
             to_far = to_fars[step + 1]
         else:
             to_far = None
-        if step > 0:
-            done = finish(partial[step - 1], got[step - 1], last[step - 1])
-        else:
-            done = None
-        to_a, to_b, to_far, coming, done, sums = together(to_a, to_b, to_far, coming, done, sums)
-    sums = tail_sums(done, limits, block_weights[blocks - 1], sums)
+        to_a, to_b, to_far, coming = together(to_a, to_b, to_far, coming)
+    k = blocks - 1
+    done = finish(partial[k], got[k], last[k])
+    sums = tail_sums(done, limits, row_weights, starts[blocks - 1], sums)
 
     sums = sums + swap(sums, "scen", 1)
-    count, excess = sums[:depth] * 0.5, sums[depth:] * (0.5 / half_inverse)
+    count, excess = sums[:depth] * 0.5, sums[depth : 2 * depth] * (0.5 / half_inverse)
+    total = sums[2 * depth : 2 * depth + 1]
     result = jnp.concatenate([excess / jnp.maximum(count, 1.0), count / total], 0)
     parts = [result] + [swap(result, "fac", flip) for flip in (1, 2, 3)]
 

time: 250 us -> 238 us (0.952)
  Pallas kernels: 58.1 us -> 51.1 us
  waiting for transfers between devices: 66.1 us -> 62.6 us
    pallas_call x5, Pallas kernels: 58.1 us -> 51.1 us  [tail_sums(): pl.pallas_call(functools.partial(tail_body, first), out_shape=jax.ShapeDt...]
    ppermute x24 -> x23, waiting for transfers between devices: 66.1 us -> 62.6 us  [swap(): lax.ppermute(v, axis, [(i, i ^ flip) for i in range(lax.axis_size(axis))])]
    broadcast_in_dim x9 -> x2, local copies, waits for them, and re-layouts: 3.91 us -> 0.62 us  [the longest x1 0.62 us: pipelined(): row_weights = jnp.broadcast_to(jnp.concatenate(parts)[None], (8, 4 * rows))]
    convert_element_type x4 -> x5, other arithmetic: 6.01 us -> 8.14 us  [send_b(): (columns(partial, at, quarter).astype(f32) + columns(got, 1 - high, quart...]
    ppermute x24 -> x23, starting transfers between devices: 23.7 us -> 22.1 us  [swap(): lax.ppermute(v, axis, [(i, i ^ flip) for i in range(lax.axis_size(axis))])]
  transfers between devices with their start and end apart: 24 -> 23, of which waited for: 11 -> 11; matrix products, arithmetic and copies ran while one was open for 29% -> 34% of each run, Pallas kernels for 20% -> 19%
where the time goes in v4:
time: 238 us; the launch traced here: 237 us
  waiting for transfers between devices  62.6 us (26%)
  matrix products  62.2 us (26%)
  Pallas kernels  51.1 us (21%)
  other arithmetic  23.1 us (10%)
  starting transfers between devices  22.1 us (9%)
  local copies, waits for them, and re-layouts  14.2 us (6%)
    ppermute x23, waiting for transfers between devices, swap(): lax.ppermute(v, axis, [(i, i ^ flip) for i in range(lax.axis_size(axis))])  62.6 us
    dot_general x5, matrix products, product(): jnp.dot(block, loading, preferred_element_type=f32) * half_inverse  62.2 us
    pallas_call x5, Pallas kernels, tail_sums(): pl.pallas_call(functools.partial(tail_body, first), out_shape=jax.ShapeDt...  51.1 us
    ppermute x23, starting transfers between devices, swap(): lax.ppermute(v, axis, [(i, i ^ flip) for i in range(lax.axis_size(axis))])  22.1 us
    add x5, other arithmetic, finish(): columns(partial, at, quarter).astype(f32)  11.3 us
    convert_element_type x5, other arithmetic, send_b(): (columns(partial, at, quarter).astype(f32) + columns(got, 1 - high, quart...  8.14 us
    dynamic_slice x5, local copies, waits for them, and re-layouts, columns(): return lax.dynamic_slice_in_dim(v, k * width, width, 1)  5.83 us
  transfers between devices with their start and end apart: 23, of which 11 were waited for; matrix products, arithmetic and copies ran while one was open for 34% of the time, Pallas kernels for 19%

profile of v4, /device:TPU:8, one launch (start us, length us, event | category | flops | bytes accessed | tf_op | source)
XLA Modules:
  0.0 237.4 jit_solution(11892230468307151909)
XLA Ops:
  0.7 2.9 %slice.33 = bf16[208,4096]{1,0:T(8,128)(2,1)} slice(bf16[512,4096]{1,0:T(8,128)(2,1)} %param.4), slice={[0:208], [0:4096]} | slice | bytes 3407872 | tf_op jit(solution)/shard_map/slice | solution.py:118
  5.3 13.6 %multiply_convert_fusion.1 = f16[512,2048]{1,0:T(8,128)(2,1)S(1)} fusion(bf16[512,4096]{1,0:T(8,128)(2,1)} %param.4, bf16[4096,2048]{1,0:T(8,128)(2,1)} %param.5), kind=kOutput, calls=%fused_computation.1 | convolution fusion | flops 8592031744 | bytes 23068672 | tf_op jit(solution)/shard_map/dot_general | solution.py:93
  19.9 13.9 %multiply_convert_fusion = f16[512,2048]{1,0:T(8,128)(2,1)S(1)} fusion(bf16[512,4096]{1,0:T(8,128)(2,1)} %collective-permute-done, bf16[4096,2048]{1,0:T(8,128)(2,1)} %param.5), kind=kOutput, calls=%fused_computation | convolution fusion | flops 8592031744 | bytes 23068672 | tf_op jit(solution)/shard_map/dot_general | solution.py:93
  36.1 7.4 %collective-permute-done.2 = bf16[208,4096]{1,0:T(8,128)(2,1)} collective-permute-done((bf16[208,4096]{1,0:T(8,128)(2,1)}, bf16[208,4096]{1,0:T(8,128)(2,1)}, u32[]{:S(2)}, u32[]{:S(2)}) %collective-permute-start.2) | collective-permute-done | bytes 1703968 | tf_op jit(solution)/shard_map/ppermute | solution.py:87
  46.9 2.8 %collective-permute-start.5 = (f16[512,512]{1,0:T(8,128)(2,1)}, f16[512,512]{1,0:T(8,128)(2,1)S(1)}, u32[]{:S(2)}, u32[]{:S(2)}) collective-permute-start(f16[512,512]{1,0:T(8,128)(2,1)} %add_convert_fusion.1), channel_id=1, source_target_pairs={{0,4},{2,6},{4,0},{6,2},{1,5},{3,7},{5,1},{7,3},{8,12},{10,14},{12... | collective-permute-start | bytes 1572872 | tf_op jit(solution)/shard_map/ppermute | solution.py:87
  51.2 11.7 %multiply_convert_fusion.2 = f16[416,2048]{1,0:T(8,128)(2,1)S(1)} fusion(bf16[4096,2048]{1,0:T(8,128)(2,1)} %param.5, bf16[208,4096]{1,0:T(8,128)(2,1)} %collective-permute-done.6, bf16[208,4096]{1,0:T(8,128)(2,1)} %collective-permute-done.2), kind=kOutput, calls=%fused_computation.6 | convolution fusion | flops 6987841536 | bytes 21889024 | tf_op jit(solution)/shard_map/dot_general | solution.py:93
  62.9 1.7 dynamic-slice_multiply_fusion.levels
  64.7 18.6 %collective-permute-done.8 = bf16[2,512]{1,0:T(2,128)(2,1)S(1)} collective-permute-done((bf16[2,512]{1,0:T(2,128)(2,1)S(1)}, bf16[2,512]{1,0:T(2,128)(2,1)S(1)}, u32[]{:S(2)}, u32[]{:S(2)}) %collective-permute-start.8) | collective-permute-done | bytes 2080 | tf_op jit(solution)/shard_map/ppermute | solution.py:87
  85.5 2.1 add_convert_fusion
  89.1 1.9 collective-permute-start.10
  91.3 12.0 %multiply_convert_fusion.3 = f16[384,2048]{1,0:T(8,128)(2,1)} fusion(bf16[4096,2048]{1,0:T(8,128)(2,1)} %param.5, bf16[192,4096]{1,0:T(8,128)(2,1)} %collective-permute-done.11, bf16[192,4096]{1,0:T(8,128)(2,1)} %collective-permute-done.7), kind=kOutput, calls=%fused_computation.11 | convolution fusion | flops 6450315264 | bytes 21495808 | tf_op jit(solution)/shard_map/dot_general | solution.py:93
  105.8 2.3 convert_add_fusion.1.losses
  109.6 12.2 %tail_sums.5.sums_in = f32[136,512]{1,0:T(8,128)} custom-call(f32[512,512]{1,0:T(8,128)} %convert_add_fusion.1.losses, f32[64,512]{1,0:T(8,128)} %dynamic-slice_multiply_fusion.levels, bf16[8,2048]{1,0:T(8,128)(2,1)} %broadcast_in_dim.4.weights, f32[136,512]{1,0:T(8,128)} %concatenate.27.sums_in), custom_call_target="tpu_custom_call", output_to_operand_aliasing={{}: (3, {})} | custom-call | flops 1024 | bytes 1024 | tf_op jit(solution)/shard_map/tail_sums/pallas_call | solution.py:58
  121.8 2.2 constant_dynamic-slice_fusion.1
  123.9 2.0 add_convert_fusion.2
  128.7 11.0 %fusion.12 = f16[224,2048]{1,0:T(8,128)(2,1)} fusion(bf16[4096,2048]{1,0:T(8,128)(2,1)} %param.5, bf16[112,4096]{1,0:T(8,128)(2,1)S(1)} %collective-permute-done.15, bf16[112,4096]{1,0:T(8,128)(2,1)} %collective-permute-done.12), kind=kOutput, calls=%fused_computation.13 | convolution fusion | flops 3762683904 | bytes 19529728 | tf_op jit(solution)/shard_map/dot_general | solution.py:93
  139.7 2.6 %convert_add_fusion.losses = f32[512,512]{1,0:T(8,128)} fusion(f16[512,512]{1,0:T(8,128)(2,1)} %collective-permute-done.10, f16[512,1024]{1,0:T(8,128)(2,1)S(1)} %copy-done.6, s32[]{:T(128)S(6)} %select_n.110, f16[512,2048]{1,0:T(8,128)(2,1)} %copy-done.1, s32[]{:T(128)S(6)} %select_n.109), kind=kLoop, calls=%fused_computation.18 | loop fusion | flops 1310720 | bytes 2621448 | tf_op jit(solution)/shard_map/add | solution.py:105
  142.3 12.2 %tail_sums.6.sums_in = f32[136,512]{1,0:T(8,128)} custom-call(f32[512,512]{1,0:T(8,128)} %convert_add_fusion.losses, f32[64,512]{1,0:T(8,128)} %dynamic-slice_multiply_fusion.levels, bf16[8,2048]{1,0:T(8,128)(2,1)} %broadcast_in_dim.4.weights, f32[136,512]{1,0:T(8,128)} %tail_sums.5.sums_in), custom_call_target="tpu_custom_call", output_to_operand_aliasing={{}: (3, {})} | custom-call | flops 1024 | bytes 1024 | tf_op jit(solution)/shard_map/tail_sums/pallas_call | solution.py:58
  156.1 1.9 constant_dynamic-slice_fusion
  157.9 1.9 add_convert_fusion.3
  162.0 2.3 convert_add_fusion.2.losses
  164.2 10.3 %tail_sums.7.sums_in = f32[136,512]{1,0:T(8,128)} custom-call(f32[416,512]{1,0:T(8,128)} %convert_add_fusion.2.losses, f32[64,512]{1,0:T(8,128)} %dynamic-slice_multiply_fusion.levels, bf16[8,2048]{1,0:T(8,128)(2,1)} %broadcast_in_dim.4.weights, f32[136,512]{1,0:T(8,128)} %tail_sums.6.sums_in), custom_call_target="tpu_custom_call", output_to_operand_aliasing={{}: (3, {})} | custom-call | flops 1024 | bytes 1024 | tf_op jit(solution)/shard_map/tail_sums/pallas_call | solution.py:58
  174.5 6.1 %collective-permute-done.17 = f16[384,512]{1,0:T(8,128)(2,1)} collective-permute-done((f16[384,512]{1,0:T(8,128)(2,1)}, f16[384,512]{1,0:T(8,128)(2,1)}, u32[]{:S(2)}, u32[]{:S(2)}) %collective-permute-start.17) | collective-permute-done | bytes 393248 | tf_op jit(solution)/shard_map/ppermute | solution.py:87
  182.6 2.2 convert_add_fusion.3.losses
  184.8 9.7 %tail_sums.8.sums_in = f32[136,512]{1,0:T(8,128)} custom-call(f32[384,512]{1,0:T(8,128)} %convert_add_fusion.3.losses, f32[64,512]{1,0:T(8,128)} %dynamic-slice_multiply_fusion.levels, bf16[8,2048]{1,0:T(8,128)(2,1)} %broadcast_in_dim.4.weights, f32[136,512]{1,0:T(8,128)} %tail_sums.7.sums_in), custom_call_target="tpu_custom_call", output_to_operand_aliasing={{}: (3, {})} | custom-call | flops 1024 | bytes 1024 | tf_op jit(solution)/shard_map/tail_sums/pallas_call | solution.py:58
  194.6 1.9 convert_add_fusion.4.losses
  196.5 6.7 %tail_sums.9 = f32[136,512]{1,0:T(8,128)} custom-call(f32[224,512]{1,0:T(8,128)} %convert_add_fusion.4.losses, f32[64,512]{1,0:T(8,128)} %dynamic-slice_multiply_fusion.levels, bf16[8,2048]{1,0:T(8,128)(2,1)} %broadcast_in_dim.4.weights, f32[136,512]{1,0:T(8,128)} %tail_sums.8.sums_in), custom_call_target="tpu_custom_call", output_to_operand_aliasing={{}: (3, {})} | custom-call | flops 1024 | bytes 1024 | tf_op jit(solution)/shard_map/tail_sums/pallas_call | solution.py:58
  204.7 5.6 %collective-permute-done.19 = f32[136,512]{1,0:T(8,128)S(1)} collective-permute-done((f32[136,512]{1,0:T(8,128)}, f32[136,512]{1,0:T(8,128)S(1)}, u32[]{:S(2)}, u32[]{:S(2)}) %collective-permute-start.19) | collective-permute-done | bytes 278560 | tf_op jit(solution)/shard_map/ppermute | solution.py:87
  211.4 2.5 %collective-permute-start.20 = (f32[128,512]{1,0:T(8,128)S(1)}, f32[128,512]{1,0:T(8,128)S(1)}, u32[]{:S(2)}, u32[]{:S(2)}) collective-permute-start(f32[128,512]{1,0:T(8,128)S(1)} %pad_maximum_fusion.1), channel_id=1, source_target_pairs={{0,2},{2,0},{4,6},{6,4},{1,3},{3,1},{5,7},{7,5},{8,10},{10,8},{12,... | collective-permute-start | bytes 786440 | tf_op jit(solution)/shard_map/ppermute | solution.py:87
  215.4 7.3 %collective-permute-done.20 = f32[128,512]{1,0:T(8,128)S(1)} collective-permute-done((f32[128,512]{1,0:T(8,128)S(1)}, f32[128,512]{1,0:T(8,128)S(1)}, u32[]{:S(2)}, u32[]{:S(2)}) %collective-permute-start.20) | collective-permute-done | bytes 262176 | tf_op jit(solution)/shard_map/ppermute | solution.py:87
  222.7 8.9 %collective-permute-done.21 = f32[128,512]{1,0:T(8,128)S(1)} collective-permute-done((f32[128,512]{1,0:T(8,128)S(1)}, f32[128,512]{1,0:T(8,128)S(1)}, u32[]{:S(2)}, u32[]{:S(2)}) %collective-permute-start.21) | collective-permute-done | bytes 262176 | tf_op jit(solution)/shard_map/ppermute | solution.py:87
  231.6 4.5 %collective-permute-done.22 = f32[128,512]{1,0:T(8,128)S(1)} collective-permute-done((f32[128,512]{1,0:T(8,128)S(1)}, f32[128,512]{1,0:T(8,128)S(1)}, u32[]{:S(2)}, u32[]{:S(2)}) %collective-permute-start.22) | collective-permute-done | bytes 262176 | tf_op jit(solution)/shard_map/ppermute | solution.py:87
  (88 shorter events, 30.4 us)
Async XLA Ops:
  0.6 4.5 %copy-start.10 = (bf16[512]{0:T(512)(128)(2,1)S(1)}, bf16[512]{0:T(512)(128)(2,1)}, u32[]{:S(2)}) copy-start(bf16[512]{0:T(512)(128)(2,1)} %param.7) | copy-start | bytes 3076
  0.6 18.7 %collective-permute-start = (bf16[512,4096]{1,0:T(8,128)(2,1)}, bf16[512,4096]{1,0:T(8,128)(2,1)}, u32[]{:S(2)}, u32[]{:S(2)}) collective-permute-start(bf16[512,4096]{1,0:T(8,128)(2,1)} %param.4), channel_id=1, source_target_pairs={{0,8},{8,0},{16,24},{24,16},{1,9},{9,1},{17,25},{25,17},{2,10},{10... | collective-permute-start | bytes 12582920 | tf_op jit(solution)/shard_map/ppermute | solution.py:87
  3.6 39.9 %collective-permute-start.2 = (bf16[208,4096]{1,0:T(8,128)(2,1)}, bf16[208,4096]{1,0:T(8,128)(2,1)}, u32[]{:S(2)}, u32[]{:S(2)}) collective-permute-start(bf16[208,4096]{1,0:T(8,128)(2,1)} %slice.33), channel_id=1, source_target_pairs={{0,16},{8,24},{16,0},{24,8},{1,17},{9,25},{17,1},{25,9},{2,18},{10... | collective-permute-start | bytes 5111816 | tf_op jit(solution)/shard_map/ppermute | solution.py:87
  5.1 14.2 %collective-permute-start.3 = (bf16[512]{0:T(512)(128)(2,1)S(1)}, bf16[512]{0:T(512)(128)(2,1)S(1)}, u32[]{:S(2)}, u32[]{:S(2)}) collective-permute-start(bf16[512]{0:T(512)(128)(2,1)S(1)} %copy-done.10), channel_id=1, source_target_pairs={{0,8},{8,0},{16,24},{24,16},{1,9},{9,1},{17,25},{25,17},{2,10},{10... | collective-permute-start | bytes 3080 | tf_op jit(solution)/shard_map/ppermute | solution.py:87
  19.3 14.4 %copy-start = (bf16[512,4096]{1,0:T(8,128)(2,1)S(1)}, bf16[512,4096]{1,0:T(8,128)(2,1)}, u32[]{:S(2)}) copy-start(bf16[512,4096]{1,0:T(8,128)(2,1)} %param.4) | copy-start | bytes 12582916
  19.3 25.4 %collective-permute-start.1 = (f16[512,1024]{1,0:T(8,128)(2,1)S(1)}, f16[512,1024]{1,0:T(8,128)(2,1)S(1)}, u32[]{:S(2)}, u32[]{:S(2)}) collective-permute-start(f16[512,1024]{1,0:T(8,128)(2,1)S(1)} %constant_dynamic-slice_fusion.4), channel_id=1, source_target_pairs={{0,2},{2,0},{4,6},{6,4},{1,3},{3,1},{5,7},{7,5},{8,10},{10,8},{12,... | collective-permute-start | bytes 3145736 | tf_op jit(solution)/shard_map/ppermute | solution.py:87
  33.7 11.3 %copy-start.1 = (f16[512,2048]{1,0:T(8,128)(2,1)}, f16[512,2048]{1,0:T(8,128)(2,1)S(1)}, u32[]{:S(2)}) copy-start(f16[512,2048]{1,0:T(8,128)(2,1)S(1)} %multiply_convert_fusion) | copy-start | bytes 6291460
  46.1 5.1 %collective-permute-start.6 = (bf16[208,4096]{1,0:T(8,128)(2,1)}, bf16[208,4096]{1,0:T(8,128)(2,1)}, u32[]{:S(2)}, u32[]{:S(2)}) collective-permute-start(bf16[208,4096]{1,0:T(8,128)(2,1)} %collective-permute-done.2), channel_id=1, source_target_pairs={{0,8},{8,0},{16,24},{24,16},{1,9},{9,1},{17,25},{25,17},{2,10},{10... | collective-permute-start | bytes 5111816 | tf_op jit(solution)/shard_map/ppermute | solution.py:87
  46.1 38.1 %collective-permute-start.7 = (bf16[192,4096]{1,0:T(8,128)(2,1)}, bf16[192,4096]{1,0:T(8,128)(2,1)}, u32[]{:S(2)}, u32[]{:S(2)}) collective-permute-start(bf16[192,4096]{1,0:T(8,128)(2,1)} %slice.34), channel_id=1, source_target_pairs={{0,16},{8,24},{16,0},{24,8},{1,17},{9,25},{17,1},{25,9},{2,18},{10... | collective-permute-start | bytes 4718600 | tf_op jit(solution)/shard_map/ppermute | solution.py:87
  46.7 37.5 %collective-permute-start.4 = (f16[512,1024]{1,0:T(8,128)(2,1)S(1)}, f16[512,1024]{1,0:T(8,128)(2,1)S(1)}, u32[]{:S(2)}, u32[]{:S(2)}) collective-permute-start(f16[512,1024]{1,0:T(8,128)(2,1)S(1)} %constant_dynamic-slice_fusion.3), channel_id=1, source_target_pairs={{0,2},{2,0},{4,6},{6,4},{1,3},{3,1},{5,7},{7,5},{8,10},{10,8},{12,... | collective-permute-start | bytes 3145736 | tf_op jit(solution)/shard_map/ppermute | solution.py:87
  46.9 37.3 %collective-permute-start.5 = (f16[512,512]{1,0:T(8,128)(2,1)}, f16[512,512]{1,0:T(8,128)(2,1)S(1)}, u32[]{:S(2)}, u32[]{:S(2)}) collective-permute-start(f16[512,512]{1,0:T(8,128)(2,1)} %add_convert_fusion.1), channel_id=1, source_target_pairs={{0,4},{2,6},{4,0},{6,2},{1,5},{3,7},{5,1},{7,3},{8,12},{10,14},{12... | collective-permute-start | bytes 1572872 | tf_op jit(solution)/shard_map/ppermute | solution.py:87
  49.7 33.6 %collective-permute-start.8 = (bf16[2,512]{1,0:T(2,128)(2,1)S(1)}, bf16[2,512]{1,0:T(2,128)(2,1)S(1)}, u32[]{:S(2)}, u32[]{:S(2)}) collective-permute-start(bf16[2,512]{1,0:T(2,128)(2,1)S(1)} %pad_maximum_fusion.2), channel_id=1, source_target_pairs={{0,16},{8,24},{16,0},{24,8},{1,17},{9,25},{17,1},{25,9},{2,18},{10... | collective-permute-start | bytes 6152 | tf_op jit(solution)/shard_map/ppermute | solution.py:87
  62.9 21.3 %copy-start.2 = (f16[416,2048]{1,0:T(8,128)(2,1)}, f16[416,2048]{1,0:T(8,128)(2,1)S(1)}, u32[]{:S(2)}) copy-start(f16[416,2048]{1,0:T(8,128)(2,1)S(1)} %multiply_convert_fusion.2) | copy-start | bytes 5111812
  84.2 3.4 %copy-start.9 = (f16[512,512]{1,0:T(8,128)(2,1)}, f16[512,512]{1,0:T(8,128)(2,1)S(1)}, u32[]{:S(2)}) copy-start(f16[512,512]{1,0:T(8,128)(2,1)S(1)} %collective-permute-done.5) | copy-start | bytes 1572868
  87.6 3.8 %collective-permute-start.11 = (bf16[192,4096]{1,0:T(8,128)(2,1)}, bf16[192,4096]{1,0:T(8,128)(2,1)}, u32[]{:S(2)}, u32[]{:S(2)}) collective-permute-start(bf16[192,4096]{1,0:T(8,128)(2,1)} %collective-permute-done.7), channel_id=1, source_target_pairs={{0,8},{8,0},{16,24},{24,16},{1,9},{9,1},{17,25},{25,17},{2,10},{10... | collective-permute-start | bytes 4718600 | tf_op jit(solution)/shard_map/ppermute | solution.py:87
  87.6 18.2 %copy-start.8 = (f16[512,1024]{1,0:T(8,128)(2,1)S(1)}, f16[512,1024]{1,0:T(8,128)(2,1)}, u32[]{:S(2)}) copy-start(f16[512,1024]{1,0:T(8,128)(2,1)} %copy-done.7) | copy-start | bytes 3145732
  87.6 34.2 %collective-permute-start.12 = (bf16[112,4096]{1,0:T(8,128)(2,1)}, bf16[112,4096]{1,0:T(8,128)(2,1)}, u32[]{:S(2)}, u32[]{:S(2)}) collective-permute-start(bf16[112,4096]{1,0:T(8,128)(2,1)} %slice.35), channel_id=1, source_target_pairs={{0,16},{8,24},{16,0},{24,8},{1,17},{9,25},{17,1},{25,9},{2,18},{10... | collective-permute-start | bytes 2752520 | tf_op jit(solution)/shard_map/ppermute | solution.py:87
  89.1 32.6 %collective-permute-start.9 = (f16[416,1024]{1,0:T(8,128)(2,1)}, f16[416,1024]{1,0:T(8,128)(2,1)}, u32[]{:S(2)}, u32[]{:S(2)}) collective-permute-start(f16[416,1024]{1,0:T(8,128)(2,1)} %constant_dynamic-slice_fusion.2), channel_id=1, source_target_pairs={{0,2},{2,0},{4,6},{6,4},{1,3},{3,1},{5,7},{7,5},{8,10},{10,8},{12,... | collective-permute-start | bytes 2555912 | tf_op jit(solution)/shard_map/ppermute | solution.py:87
  89.1 32.6 %collective-permute-start.10 = (f16[512,512]{1,0:T(8,128)(2,1)}, f16[512,512]{1,0:T(8,128)(2,1)}, u32[]{:S(2)}, u32[]{:S(2)}) collective-permute-start(f16[512,512]{1,0:T(8,128)(2,1)} %add_convert_fusion), channel_id=1, source_target_pairs={{0,4},{2,6},{4,0},{6,2},{1,5},{3,7},{5,1},{7,3},{8,12},{10,14},{12... | collective-permute-start | bytes 1572872 | tf_op jit(solution)/shard_map/ppermute | solution.py:87
  108.1 15.8 %copy-start.3 = (f16[416,2048]{1,0:T(8,128)(2,1)S(1)}, f16[416,2048]{1,0:T(8,128)(2,1)}, u32[]{:S(2)}) copy-start(f16[416,2048]{1,0:T(8,128)(2,1)} %copy-done.2) | copy-start | bytes 5111812
  125.9 13.8 %copy-start.6 = (f16[512,1024]{1,0:T(8,128)(2,1)S(1)}, f16[512,1024]{1,0:T(8,128)(2,1)}, u32[]{:S(2)}) copy-start(f16[512,1024]{1,0:T(8,128)(2,1)} %copy-done.5) | copy-start | bytes 3145732
  125.9 2.8 %collective-permute-start.15 = (bf16[112,4096]{1,0:T(8,128)(2,1)}, bf16[112,4096]{1,0:T(8,128)(2,1)S(1)}, u32[]{:S(2)}, u32[]{:S(2)}) collective-permute-start(bf16[112,4096]{1,0:T(8,128)(2,1)} %collective-permute-done.12), channel_id=1, source_target_pairs={{0,8},{8,0},{16,24},{24,16},{1,9},{9,1},{17,25},{25,17},{2,10},{10... | collective-permute-start | bytes 2752520 | tf_op jit(solution)/shard_map/ppermute | solution.py:87
  126.0 30.0 %collective-permute-start.13 = (f16[384,1024]{1,0:T(8,128)(2,1)}, f16[384,1024]{1,0:T(8,128)(2,1)}, u32[]{:S(2)}, u32[]{:S(2)}) collective-permute-start(f16[384,1024]{1,0:T(8,128)(2,1)} %constant_dynamic-slice_fusion.1), channel_id=1, source_target_pairs={{0,2},{2,0},{4,6},{6,4},{1,3},{3,1},{5,7},{7,5},{8,10},{10,8},{12,... | collective-permute-start | bytes 2359304 | tf_op jit(solution)/shard_map/ppermute | solution.py:87
  127.3 28.8 %collective-permute-start.14 = (f16[416,512]{1,0:T(8,128)(2,1)}, f16[416,512]{1,0:T(8,128)(2,1)}, u32[]{:S(2)}, u32[]{:S(2)}) collective-permute-start(f16[416,512]{1,0:T(8,128)(2,1)} %add_convert_fusion.2), channel_id=1, source_target_pairs={{0,4},{2,6},{4,0},{6,2},{1,5},{3,7},{5,1},{7,3},{8,12},{10,14},{12... | collective-permute-start | bytes 1277960 | tf_op jit(solution)/shard_map/ppermute | solution.py:87
  139.7 18.2 %copy-start.4 = (f16[384,2048]{1,0:T(8,128)(2,1)S(1)}, f16[384,2048]{1,0:T(8,128)(2,1)}, u32[]{:S(2)}) copy-start(f16[384,2048]{1,0:T(8,128)(2,1)} %multiply_convert_fusion.3) | copy-start | bytes 4718596
  159.9 20.8 %collective-permute-start.16 = (f16[224,1024]{1,0:T(8,128)(2,1)}, f16[224,1024]{1,0:T(8,128)(2,1)}, u32[]{:S(2)}, u32[]{:S(2)}) collective-permute-start(f16[224,1024]{1,0:T(8,128)(2,1)} %constant_dynamic-slice_fusion), channel_id=1, source_target_pairs={{0,2},{2,0},{4,6},{6,4},{1,3},{3,1},{5,7},{7,5},{8,10},{10,8},{12,... | collective-permute-start | bytes 1376264 | tf_op jit(solution)/shard_map/ppermute | solution.py:87
  160.4 20.2 %collective-permute-start.17 = (f16[384,512]{1,0:T(8,128)(2,1)}, f16[384,512]{1,0:T(8,128)(2,1)}, u32[]{:S(2)}, u32[]{:S(2)}) collective-permute-start(f16[384,512]{1,0:T(8,128)(2,1)} %add_convert_fusion.3), channel_id=1, source_target_pairs={{0,4},{2,6},{4,0},{6,2},{1,5},{3,7},{5,1},{7,3},{8,12},{10,14},{12... | collective-permute-start | bytes 1179656 | tf_op jit(solution)/shard_map/ppermute | solution.py:87
  181.8 12.8 %collective-permute-start.18 = (f16[224,512]{1,0:T(8,128)(2,1)S(1)}, f16[224,512]{1,0:T(8,128)(2,1)S(1)}, u32[]{:S(2)}, u32[]{:S(2)}) collective-permute-start(f16[224,512]{1,0:T(8,128)(2,1)S(1)} %add_convert_fusion.4), channel_id=1, source_target_pairs={{0,4},{2,6},{4,0},{6,2},{1,5},{3,7},{5,1},{7,3},{8,12},{10,14},{12... | collective-permute-start | bytes 688136 | tf_op jit(solution)/shard_map/ppermute | solution.py:87
  203.1 7.1 %collective-permute-start.19 = (f32[136,512]{1,0:T(8,128)}, f32[136,512]{1,0:T(8,128)S(1)}, u32[]{:S(2)}, u32[]{:S(2)}) collective-permute-start(f32[136,512]{1,0:T(8,128)} %tail_sums.9), channel_id=1, source_target_pairs={{0,1},{1,0},{2,3},{3,2},{4,5},{5,4},{6,7},{7,6},{8,9},{9,8},{10,11... | collective-permute-start | bytes 835592 | tf_op jit(solution)/shard_map/ppermute | solution.py:87
  211.4 11.4 %collective-permute-start.20 = (f32[128,512]{1,0:T(8,128)S(1)}, f32[128,512]{1,0:T(8,128)S(1)}, u32[]{:S(2)}, u32[]{:S(2)}) collective-permute-start(f32[128,512]{1,0:T(8,128)S(1)} %pad_maximum_fusion.1), channel_id=1, source_target_pairs={{0,2},{2,0},{4,6},{6,4},{1,3},{3,1},{5,7},{7,5},{8,10},{10,8},{12,... | collective-permute-start | bytes 786440 | tf_op jit(solution)/shard_map/ppermute | solution.py:87
  213.9 17.7 %collective-permute-start.21 = (f32[128,512]{1,0:T(8,128)S(1)}, f32[128,512]{1,0:T(8,128)S(1)}, u32[]{:S(2)}, u32[]{:S(2)}) collective-permute-start(f32[128,512]{1,0:T(8,128)S(1)} %pad_maximum_fusion.1), channel_id=1, source_target_pairs={{0,4},{2,6},{4,0},{6,2},{1,5},{3,7},{5,1},{7,3},{8,12},{10,14},{12... | collective-permute-start | bytes 786440 | tf_op jit(solution)/shard_map/ppermute | solution.py:87
  214.5 21.6 %collective-permute-start.22 = (f32[128,512]{1,0:T(8,128)S(1)}, f32[128,512]{1,0:T(8,128)S(1)}, u32[]{:S(2)}, u32[]{:S(2)}) collective-permute-start(f32[128,512]{1,0:T(8,128)S(1)} %pad_maximum_fusion.1), channel_id=1, source_target_pairs={{0,6},{2,4},{4,2},{6,0},{1,7},{3,5},{5,3},{7,1},{8,14},{10,12},{12... | collective-permute-start | bytes 786440 | tf_op jit(solution)/shard_map/ppermute | solution.py:87
  (2 other events, 2.6 us)

commit v5 on v4

--- a/solution.py
+++ b/solution.py
@@ -89,25 +89,28 @@
     def columns(v, k, width):
         return lax.dynamic_slice_in_dim(v, k * width, width, 1)
 
-    def product(block):
-        return (jnp.dot(block, loading, preferred_element_type=f32) * half_inverse).astype(link)
+    def product(block, factors=loading):
+        return (jnp.dot(block, factors, preferred_element_type=f32) * half_inverse).astype(link)
+
+    def kept(partial, k):
+        if isinstance(partial, tuple):
+            return columns(partial[0], k, quarter)
+        return columns(partial, 2 * low + k, quarter)
 
     def send_a(partial):
         return columns(partial, 1 - low, 2 * quarter)
 
     def send_b(partial, got):
-        at = 2 * low + 1 - high
-        return (columns(partial, at, quarter).astype(f32) + columns(got, 1 - high, quarter).astype(f32)).astype(link)
+        return (kept(partial, 1 - high).astype(f32) + columns(got, 1 - high, quarter).astype(f32)).astype(link)
 
     def finish(partial, got, last):
-        at = 2 * low + high
         return (
-            columns(partial, at, quarter).astype(f32)
+            kept(partial, high).astype(f32)
             + columns(got, high, quarter).astype(f32)
             + last.astype(f32)
         )
 
-    cuts = [0] + [rows * c // 32 for c in (13, 25)] + [rows]
+    cuts = [0] + [rows * c // 32 for c in (12, 24)] + [rows]
     pieces = [slice(i, j) for i, j in zip(cuts, cuts[1:])]
     depth = thresholds.shape[0]
 
@@ -117,8 +120,8 @@
     sums = None
     coming = swap(shocks[pieces[0]], "port", 2)
     sibling = swap(shocks, "port", 1)
-    first = product(shocks)
-    to_a, sibling, partial[0] = together(send_a(first), sibling, first)
+    first = product(shocks, columns(loading, 1 - low, 2 * quarter))
+    to_a, sibling = together(first, sibling)
 
     for step in range(blocks + 1):
         if step < blocks:
@@ -129,9 +132,9 @@
         if 1 <= step < len(pieces):
             nearest = swap(to_far, "port", 2)
         if step == 0:
-            partial[1] = product(sibling)
-            later = together(shocks, partial[1])[0]
-            to_fars = {k: later[piece] for k, piece in enumerate(pieces) if k}
+            partial[0] = (product(shocks, columns(together(loading, to_a)[0], low, 2 * quarter)),)
+            partial[1] = product(together(sibling, partial[0][0])[0])
+            to_fars = {1: together(shocks, partial[1])[0][pieces[1]]}
         elif step + 1 < blocks:
             partial[step + 1] = product(jnp.concatenate([coming, swap(coming, "port", 1)], 0))
         if step > 1:
@@ -153,6 +156,8 @@
             nearest = coming
             pair = small = jnp.stack([weights, swap(weights, "port", 1)])
         elif step == 1:
+            later = together(shocks, partial[2])[0]
+            to_fars = {k: later[piece] for k, piece in enumerate(pieces) if k > 1}
             limits = columns(together(thresholds, partial[2])[0], 2 * low + high, quarter)
             small = (swap(pair, "port", 2), limits * half_inverse)
         else:

time: 238 us -> 231 us (0.971)
  waiting for transfers between devices: 62.6 us -> 57 us
  other arithmetic: 23.1 us -> 19.3 us
    ppermute x23, waiting for transfers between devices: 62.6 us -> 57 us  [swap(): lax.ppermute(v, axis, [(i, i ^ flip) for i in range(lax.axis_size(axis))])]
    convert_element_type x5, other arithmetic: 8.14 us -> 5.45 us  [send_b(): (kept(partial, 1 - high).astype(f32) + columns(got, 1 - high, quarter).as...]
    slice x2, local copies, waits for them, and re-layouts: 2.36 us -> 5 us  [the longest x1 2.71 us: pipelined(): to_fars = {1: together(shocks, partial[1])[0][pieces[1]]}]
    dynamic_slice x5 -> x4, local copies, waits for them, and re-layouts: 5.83 us -> 3.64 us  [columns(): return lax.dynamic_slice_in_dim(v, k * width, width, 1)]
    dot_general x5 -> x6, matrix products: 62.2 us -> 63.6 us  [product(): jnp.dot(block, factors, preferred_element_type=f32) * half_inverse]
  transfers between devices with their start and end apart: 23 -> 23, of which waited for: 11 -> 11; matrix products, arithmetic and copies ran while one was open for 34% -> 37% of each run, Pallas kernels for 19% -> 19%
where the time goes in v5:
time: 231 us; the launch traced here: 229 us
  matrix products  63.6 us (28%)
  waiting for transfers between devices  57 us (25%)
  Pallas kernels  50.9 us (22%)
  starting transfers between devices  21.1 us (9%)
  other arithmetic  19.3 us (8%)
  local copies, waits for them, and re-layouts  14.9 us (6%)
    dot_general x6, matrix products, product(): jnp.dot(block, factors, preferred_element_type=f32) * half_inverse  63.6 us
    ppermute x23, waiting for transfers between devices, swap(): lax.ppermute(v, axis, [(i, i ^ flip) for i in range(lax.axis_size(axis))])  57 us
    pallas_call x5, Pallas kernels, tail_sums(): pl.pallas_call(functools.partial(tail_body, first), out_shape=jax.ShapeDt...  50.9 us
    ppermute x23, starting transfers between devices, swap(): lax.ppermute(v, axis, [(i, i ^ flip) for i in range(lax.axis_size(axis))])  21.1 us
    add x5, other arithmetic, finish(): kept(partial, high).astype(f32) + columns(got, high, quarter).astype(f32)  10.2 us
    convert_element_type x5, other arithmetic, send_b(): (kept(partial, 1 - high).astype(f32) + columns(got, 1 - high, quarter).as...  5.45 us
  transfers between devices with their start and end apart: 23, of which 11 were waited for; matrix products, arithmetic and copies ran while one was open for 37% of the time, Pallas kernels for 19%

profile of v5, /device:TPU:8, one launch (start us, length us, event | category | flops | bytes accessed | tf_op | source)
XLA Modules:
  0.0 229.2 jit_solution(12225028113614145891)
XLA Ops:
  0.7 2.7 %slice.33 = bf16[192,4096]{1,0:T(8,128)(2,1)} slice(bf16[512,4096]{1,0:T(8,128)(2,1)} %param.4), slice={[0:192], [0:4096]} | slice | bytes 3145728 | tf_op jit(solution)/shard_map/slice | solution.py:121
  5.2 9.1 %fusion.24 = f16[512,1024]{1,0:T(8,128)(2,1)S(1)} fusion(bf16[512,4096]{1,0:T(8,128)(2,1)} %param.4, bf16[4096,2048]{1,0:T(8,128)(2,1)} %param.5, s32[]{:T(128)S(6)} %select_n.108), kind=kOutput, calls=%fused_computation.22 | convolution fusion | flops 4296015872 | bytes 13631492 | tf_op jit(solution)/shard_map/dot_general | solution.py:93
  15.0 9.4 %fusion.27 = f16[512,1024]{1,0:T(8,128)(2,1)S(1)} fusion(bf16[512,4096]{1,0:T(8,128)(2,1)} %param.4, bf16[4096,2048]{1,0:T(8,128)(2,1)} %param.5, s32[]{:T(128)S(6)} %select_n.109), kind=kOutput, calls=%fused_computation.23 | convolution fusion | flops 4296015872 | bytes 13631492 | tf_op jit(solution)/shard_map/dot_general | solution.py:93
  24.5 11.4 %multiply_convert_fusion = f16[512,2048]{1,0:T(8,128)(2,1)S(1)} fusion(bf16[512,4096]{1,0:T(8,128)(2,1)} %collective-permute-done, bf16[4096,2048]{1,0:T(8,128)(2,1)S(1)} %bitcast.20), kind=kOutput, calls=%fused_computation.4 | convolution fusion | flops 8592031744 | bytes 23068672 | tf_op jit(solution)/shard_map/dot_general | solution.py:93
  35.8 2.7 %slice.34 = bf16[192,4096]{1,0:T(8,128)(2,1)} slice(bf16[512,4096]{1,0:T(8,128)(2,1)} %param.4), slice={[192:384], [0:4096]} | slice | bytes 3145728 | tf_op jit(solution)/shard_map/slice | solution.py:137
  38.6 2.0 collective-permute-done.2
  44.5 2.6 %collective-permute-start.5 = (f16[512,512]{1,0:T(8,128)(2,1)}, f16[512,512]{1,0:T(8,128)(2,1)S(1)}, u32[]{:S(2)}, u32[]{:S(2)}) collective-permute-start(f16[512,512]{1,0:T(8,128)(2,1)} %add_convert_fusion.1), channel_id=1, source_target_pairs={{0,4},{2,6},{4,0},{6,2},{1,5},{3,7},{5,1},{7,3},{8,12},{10,14},{12... | collective-permute-start | bytes 1572872 | tf_op jit(solution)/shard_map/ppermute | solution.py:87
  47.7 11.1 %multiply_convert_fusion.2 = f16[384,2048]{1,0:T(8,128)(2,1)S(1)} fusion(bf16[4096,2048]{1,0:T(8,128)(2,1)} %param.5, bf16[192,4096]{1,0:T(8,128)(2,1)} %collective-permute-done.6, bf16[192,4096]{1,0:T(8,128)(2,1)} %collective-permute-done.2), kind=kOutput, calls=%fused_computation.14 | convolution fusion | flops 6450315264 | bytes 21495808 | tf_op jit(solution)/shard_map/dot_general | solution.py:93
  58.8 1.8 dynamic-slice_multiply_fusion.levels
  60.5 2.3 slice.35
  62.8 16.9 %collective-permute-done.8 = bf16[2,512]{1,0:T(2,128)(2,1)S(1)} collective-permute-done((bf16[2,512]{1,0:T(2,128)(2,1)S(1)}, bf16[2,512]{1,0:T(2,128)(2,1)S(1)}, u32[]{:S(2)}, u32[]{:S(2)}) %collective-permute-start.8) | collective-permute-done | bytes 2080 | tf_op jit(solution)/shard_map/ppermute | solution.py:87
  79.7 1.9 collective-permute-done.5
  84.5 2.1 collective-permute-start.10
  87.7 12.0 %multiply_convert_fusion.1 = f16[384,2048]{1,0:T(8,128)(2,1)} fusion(bf16[4096,2048]{1,0:T(8,128)(2,1)} %param.5, bf16[192,4096]{1,0:T(8,128)(2,1)} %collective-permute-done.11, bf16[192,4096]{1,0:T(8,128)(2,1)} %collective-permute-done.7), kind=kOutput, calls=%fused_computation.13 | convolution fusion | flops 6450315264 | bytes 21495808 | tf_op jit(solution)/shard_map/dot_general | solution.py:93
  101.8 2.6 %convert_add_fusion.1.losses = f32[512,512]{1,0:T(8,128)} fusion(f16[512,512]{1,0:T(8,128)(2,1)} %copy-done.6, f16[512,1024]{1,0:T(8,128)(2,1)} %copy-done.4, s32[]{:T(128)S(6)} %select_n.114, f16[512,1024]{1,0:T(8,128)(2,1)} %copy-done.5), kind=kLoop, calls=%fused_computation.26 | loop fusion | flops 1310720 | bytes 2621444 | tf_op jit(solution)/shard_map/add | solution.py:108
  105.8 12.2 %tail_sums.5.sums_in = f32[136,512]{1,0:T(8,128)} custom-call(f32[512,512]{1,0:T(8,128)} %convert_add_fusion.1.losses, f32[64,512]{1,0:T(8,128)} %dynamic-slice_multiply_fusion.levels, bf16[8,2048]{1,0:T(8,128)(2,1)} %broadcast_in_dim.4.weights, f32[136,512]{1,0:T(8,128)} %concatenate.27.sums_in), custom_call_target="tpu_custom_call", output_to_operand_aliasing={{}: (3, {})} | custom-call | flops 1024 | bytes 1024 | tf_op jit(solution)/shard_map/tail_sums/pallas_call | solution.py:58
  118.0 2.2 constant_dynamic-slice_fusion.1
  120.2 2.0 add_convert_fusion.3
  125.0 10.6 %fusion.16 = f16[256,2048]{1,0:T(8,128)(2,1)S(1)} fusion(bf16[4096,2048]{1,0:T(8,128)(2,1)} %param.5, bf16[128,4096]{1,0:T(8,128)(2,1)S(1)} %collective-permute-done.15, bf16[128,4096]{1,0:T(8,128)(2,1)} %collective-permute-done.12), kind=kOutput, calls=%fused_computation.16 | convolution fusion | flops 4300210176 | bytes 19922944 | tf_op jit(solution)/shard_map/dot_general | solution.py:93
  135.6 2.3 %convert_add_fusion.losses = f32[512,512]{1,0:T(8,128)} fusion(f16[512,512]{1,0:T(8,128)(2,1)} %collective-permute-done.10, f16[512,1024]{1,0:T(8,128)(2,1)S(1)} %copy-done.2, s32[]{:T(128)S(6)} %select_n.114, f16[512,2048]{1,0:T(8,128)(2,1)S(1)} %multiply_convert_fusion, s32[]{:T(128)S(6)} %select_n.112), kind=kLoop, calls=%fused_computation.25 | loop fusion | flops 1310720 | bytes 2621448 | tf_op jit(solution)/shard_map/add | solution.py:108
  138.0 12.2 %tail_sums.6.sums_in = f32[136,512]{1,0:T(8,128)} custom-call(f32[512,512]{1,0:T(8,128)} %convert_add_fusion.losses, f32[64,512]{1,0:T(8,128)} %dynamic-slice_multiply_fusion.levels, bf16[8,2048]{1,0:T(8,128)(2,1)} %broadcast_in_dim.4.weights, f32[136,512]{1,0:T(8,128)} %tail_sums.5.sums_in), custom_call_target="tpu_custom_call", output_to_operand_aliasing={{}: (3, {})} | custom-call | flops 1024 | bytes 1024 | tf_op jit(solution)/shard_map/tail_sums/pallas_call | solution.py:58
  152.8 2.3 collective-permute-start.17
  155.1 2.2 convert_add_fusion.3.losses
  157.3 9.6 %tail_sums.7.sums_in = f32[136,512]{1,0:T(8,128)} custom-call(f32[384,512]{1,0:T(8,128)} %convert_add_fusion.3.losses, f32[64,512]{1,0:T(8,128)} %dynamic-slice_multiply_fusion.levels, bf16[8,2048]{1,0:T(8,128)(2,1)} %broadcast_in_dim.4.weights, f32[136,512]{1,0:T(8,128)} %tail_sums.6.sums_in), custom_call_target="tpu_custom_call", output_to_operand_aliasing={{}: (3, {})} | custom-call | flops 1024 | bytes 1024 | tf_op jit(solution)/shard_map/tail_sums/pallas_call | solution.py:58
  166.9 8.0 %collective-permute-done.17 = f16[384,512]{1,0:T(8,128)(2,1)S(1)} collective-permute-done((f16[384,512]{1,0:T(8,128)(2,1)S(1)}, f16[384,512]{1,0:T(8,128)(2,1)S(1)}, u32[]{:S(2)}, u32[]{:S(2)}) %collective-permute-start.17) | collective-permute-done | bytes 393248 | tf_op jit(solution)/shard_map/ppermute | solution.py:87
  175.8 2.2 convert_add_fusion.2.losses
  178.0 9.6 %tail_sums.8.sums_in = f32[136,512]{1,0:T(8,128)} custom-call(f32[384,512]{1,0:T(8,128)} %convert_add_fusion.2.losses, f32[64,512]{1,0:T(8,128)} %dynamic-slice_multiply_fusion.levels, bf16[8,2048]{1,0:T(8,128)(2,1)} %broadcast_in_dim.4.weights, f32[136,512]{1,0:T(8,128)} %tail_sums.7.sums_in), custom_call_target="tpu_custom_call", output_to_operand_aliasing={{}: (3, {})} | custom-call | flops 1024 | bytes 1024 | tf_op jit(solution)/shard_map/tail_sums/pallas_call | solution.py:58
  188.6 7.2 %tail_sums.9 = f32[136,512]{1,0:T(8,128)} custom-call(f32[256,512]{1,0:T(8,128)} %convert_add_fusion.4.losses, f32[64,512]{1,0:T(8,128)} %dynamic-slice_multiply_fusion.levels, bf16[8,2048]{1,0:T(8,128)(2,1)} %broadcast_in_dim.4.weights, f32[136,512]{1,0:T(8,128)} %tail_sums.8.sums_in), custom_call_target="tpu_custom_call", output_to_operand_aliasing={{}: (3, {})} | custom-call | flops 1024 | bytes 1024 | tf_op jit(solution)/shard_map/tail_sums/pallas_call | solution.py:58
  197.4 5.6 %collective-permute-done.19 = f32[136,512]{1,0:T(8,128)S(1)} collective-permute-done((f32[136,512]{1,0:T(8,128)}, f32[136,512]{1,0:T(8,128)S(1)}, u32[]{:S(2)}, u32[]{:S(2)}) %collective-permute-start.19) | collective-permute-done | bytes 278560 | tf_op jit(solution)/shard_map/ppermute | solution.py:87
  207.6 5.9 %collective-permute-done.20 = f32[128,512]{1,0:T(8,128)S(1)} collective-permute-done((f32[128,512]{1,0:T(8,128)S(1)}, f32[128,512]{1,0:T(8,128)S(1)}, u32[]{:S(2)}, u32[]{:S(2)}) %collective-permute-start.20) | collective-permute-done | bytes 262176 | tf_op jit(solution)/shard_map/ppermute | solution.py:87
  213.5 9.8 %collective-permute-done.21 = f32[128,512]{1,0:T(8,128)S(1)} collective-permute-done((f32[128,512]{1,0:T(8,128)S(1)}, f32[128,512]{1,0:T(8,128)S(1)}, u32[]{:S(2)}, u32[]{:S(2)}) %collective-permute-start.21) | collective-permute-done | bytes 262176 | tf_op jit(solution)/shard_map/ppermute | solution.py:87
  223.3 4.6 %collective-permute-done.22 = f32[128,512]{1,0:T(8,128)S(1)} collective-permute-done((f32[128,512]{1,0:T(8,128)S(1)}, f32[128,512]{1,0:T(8,128)S(1)}, u32[]{:S(2)}, u32[]{:S(2)}) %collective-permute-start.22) | collective-permute-done | bytes 262176 | tf_op jit(solution)/shard_map/ppermute | solution.py:87
  (89 shorter events, 27.9 us)
Async XLA Ops:
  0.6 4.3 %copy-start.7 = (bf16[512]{0:T(512)(128)(2,1)S(1)}, bf16[512]{0:T(512)(128)(2,1)}, u32[]{:S(2)}) copy-start(bf16[512]{0:T(512)(128)(2,1)} %param.7) | copy-start | bytes 3076
  0.6 13.8 %collective-permute-start = (bf16[512,4096]{1,0:T(8,128)(2,1)}, bf16[512,4096]{1,0:T(8,128)(2,1)}, u32[]{:S(2)}, u32[]{:S(2)}) collective-permute-start(bf16[512,4096]{1,0:T(8,128)(2,1)} %param.4), channel_id=1, source_target_pairs={{0,8},{8,0},{16,24},{24,16},{1,9},{9,1},{17,25},{25,17},{2,10},{10... | collective-permute-start | bytes 12582920 | tf_op jit(solution)/shard_map/ppermute | solution.py:87
  3.5 37.1 %collective-permute-start.2 = (bf16[192,4096]{1,0:T(8,128)(2,1)}, bf16[192,4096]{1,0:T(8,128)(2,1)}, u32[]{:S(2)}, u32[]{:S(2)}) collective-permute-start(bf16[192,4096]{1,0:T(8,128)(2,1)} %slice.33), channel_id=1, source_target_pairs={{0,16},{8,24},{16,0},{24,8},{1,17},{9,25},{17,1},{25,9},{2,18},{10... | collective-permute-start | bytes 4718600 | tf_op jit(solution)/shard_map/ppermute | solution.py:87
  4.9 9.4 %collective-permute-start.3 = (bf16[512]{0:T(512)(128)(2,1)S(1)}, bf16[512]{0:T(512)(128)(2,1)S(1)}, u32[]{:S(2)}, u32[]{:S(2)}) collective-permute-start(bf16[512]{0:T(512)(128)(2,1)S(1)} %copy-done.7), channel_id=1, source_target_pairs={{0,8},{8,0},{16,24},{24,16},{1,9},{9,1},{17,25},{25,17},{2,10},{10... | collective-permute-start | bytes 3080 | tf_op jit(solution)/shard_map/ppermute | solution.py:87
  14.4 10.0 %slice-start = ((s8[16777216]{0:T(1024)(128)(4,1)}), s8[4194304]{0:T(1024)(128)(4,1)S(1)}, s32[]{:S(2)}) async-start(s8[16777216]{0:T(1024)(128)(4,1)} %bitcast.19), calls=%async_computation | async-start | bytes 8388608
  14.4 10.0 %slice-start.1 = ((s8[16777216]{0:T(1024)(128)(4,1)}), s8[4194304]{0:T(1024)(128)(4,1)S(1)}, s32[]{:S(2)}) async-start(s8[16777216]{0:T(1024)(128)(4,1)} %bitcast.19), calls=%async_computation.1 | async-start | bytes 8388608
  14.4 10.0 %slice-start.2 = ((s8[16777216]{0:T(1024)(128)(4,1)}), s8[4194304]{0:T(1024)(128)(4,1)S(1)}, s32[]{:S(2)}) async-start(s8[16777216]{0:T(1024)(128)(4,1)} %bitcast.19), calls=%async_computation.2 | async-start | bytes 8388608
  14.4 10.0 %slice-start.3 = ((s8[16777216]{0:T(1024)(128)(4,1)}), s8[4194304]{0:T(1024)(128)(4,1)S(1)}, s32[]{:S(2)}) async-start(s8[16777216]{0:T(1024)(128)(4,1)} %bitcast.19), calls=%async_computation.3 | async-start | bytes 8388608
  14.5 26.1 %collective-permute-start.1 = (f16[512,1024]{1,0:T(8,128)(2,1)S(1)}, f16[512,1024]{1,0:T(8,128)(2,1)S(1)}, u32[]{:S(2)}, u32[]{:S(2)}) collective-permute-start(f16[512,1024]{1,0:T(8,128)(2,1)S(1)} %fusion.24), channel_id=1, source_target_pairs={{0,2},{2,0},{4,6},{6,4},{1,3},{3,1},{5,7},{7,5},{8,10},{10,8},{12,... | collective-permute-start | bytes 3145736 | tf_op jit(solution)/shard_map/ppermute | solution.py:87
  24.4 16.4 %copy-start.5 = (f16[512,1024]{1,0:T(8,128)(2,1)}, f16[512,1024]{1,0:T(8,128)(2,1)S(1)}, u32[]{:S(2)}) copy-start(f16[512,1024]{1,0:T(8,128)(2,1)S(1)} %fusion.27) | copy-start | bytes 3145732
  42.6 5.1 %collective-permute-start.6 = (bf16[192,4096]{1,0:T(8,128)(2,1)}, bf16[192,4096]{1,0:T(8,128)(2,1)}, u32[]{:S(2)}, u32[]{:S(2)}) collective-permute-start(bf16[192,4096]{1,0:T(8,128)(2,1)} %collective-permute-done.2), channel_id=1, source_target_pairs={{0,8},{8,0},{16,24},{24,16},{1,9},{9,1},{17,25},{25,17},{2,10},{10... | collective-permute-start | bytes 4718600 | tf_op jit(solution)/shard_map/ppermute | solution.py:87
  42.6 39.0 %collective-permute-start.7 = (bf16[192,4096]{1,0:T(8,128)(2,1)}, bf16[192,4096]{1,0:T(8,128)(2,1)}, u32[]{:S(2)}, u32[]{:S(2)}) collective-permute-start(bf16[192,4096]{1,0:T(8,128)(2,1)} %slice.34), channel_id=1, source_target_pairs={{0,16},{8,24},{16,0},{24,8},{1,17},{9,25},{17,1},{25,9},{2,18},{10... | collective-permute-start | bytes 4718600 | tf_op jit(solution)/shard_map/ppermute | solution.py:87
  44.1 37.5 %collective-permute-start.4 = (f16[512,1024]{1,0:T(8,128)(2,1)S(1)}, f16[512,1024]{1,0:T(8,128)(2,1)S(1)}, u32[]{:S(2)}, u32[]{:S(2)}) collective-permute-start(f16[512,1024]{1,0:T(8,128)(2,1)S(1)} %constant_dynamic-slice_fusion.3), channel_id=1, source_target_pairs={{0,2},{2,0},{4,6},{6,4},{1,3},{3,1},{5,7},{7,5},{8,10},{10,8},{12,... | collective-permute-start | bytes 3145736 | tf_op jit(solution)/shard_map/ppermute | solution.py:87
  44.5 37.1 %collective-permute-start.5 = (f16[512,512]{1,0:T(8,128)(2,1)}, f16[512,512]{1,0:T(8,128)(2,1)S(1)}, u32[]{:S(2)}, u32[]{:S(2)}) collective-permute-start(f16[512,512]{1,0:T(8,128)(2,1)} %add_convert_fusion.1), channel_id=1, source_target_pairs={{0,4},{2,6},{4,0},{6,2},{1,5},{3,7},{5,1},{7,3},{8,12},{10,14},{12... | collective-permute-start | bytes 1572872 | tf_op jit(solution)/shard_map/ppermute | solution.py:87
  47.1 32.6 %collective-permute-start.8 = (bf16[2,512]{1,0:T(2,128)(2,1)S(1)}, bf16[2,512]{1,0:T(2,128)(2,1)S(1)}, u32[]{:S(2)}, u32[]{:S(2)}) collective-permute-start(bf16[2,512]{1,0:T(2,128)(2,1)S(1)} %pad_maximum_fusion.3), channel_id=1, source_target_pairs={{0,16},{8,24},{16,0},{24,8},{1,17},{9,25},{17,1},{25,9},{2,18},{10... | collective-permute-start | bytes 6152 | tf_op jit(solution)/shard_map/ppermute | solution.py:87
  58.8 22.9 %copy-start = (f16[384,2048]{1,0:T(8,128)(2,1)}, f16[384,2048]{1,0:T(8,128)(2,1)S(1)}, u32[]{:S(2)}) copy-start(f16[384,2048]{1,0:T(8,128)(2,1)S(1)} %multiply_convert_fusion.2) | copy-start | bytes 4718596
  81.6 2.3 %copy-start.6 = (f16[512,512]{1,0:T(8,128)(2,1)}, f16[512,512]{1,0:T(8,128)(2,1)S(1)}, u32[]{:S(2)}) copy-start(f16[512,512]{1,0:T(8,128)(2,1)S(1)} %collective-permute-done.5) | copy-start | bytes 1572868
  83.9 3.8 %collective-permute-start.11 = (bf16[192,4096]{1,0:T(8,128)(2,1)}, bf16[192,4096]{1,0:T(8,128)(2,1)}, u32[]{:S(2)}, u32[]{:S(2)}) collective-permute-start(bf16[192,4096]{1,0:T(8,128)(2,1)} %collective-permute-done.7), channel_id=1, source_target_pairs={{0,8},{8,0},{16,24},{24,16},{1,9},{9,1},{17,25},{25,17},{2,10},{10... | collective-permute-start | bytes 4718600 | tf_op jit(solution)/shard_map/ppermute | solution.py:87
  83.9 34.1 %collective-permute-start.12 = (bf16[128,4096]{1,0:T(8,128)(2,1)S(1)}, bf16[128,4096]{1,0:T(8,128)(2,1)}, u32[]{:S(2)}, u32[]{:S(2)}) collective-permute-start(bf16[128,4096]{1,0:T(8,128)(2,1)S(1)} %copy-done.3), channel_id=1, source_target_pairs={{0,16},{8,24},{16,0},{24,8},{1,17},{9,25},{17,1},{25,9},{2,18},{10... | collective-permute-start | bytes 3145736 | tf_op jit(solution)/shard_map/ppermute | solution.py:87
  84.5 33.5 %collective-permute-start.9 = (f16[384,1024]{1,0:T(8,128)(2,1)}, f16[384,1024]{1,0:T(8,128)(2,1)}, u32[]{:S(2)}, u32[]{:S(2)}) collective-permute-start(f16[384,1024]{1,0:T(8,128)(2,1)} %constant_dynamic-slice_fusion.2), channel_id=1, source_target_pairs={{0,2},{2,0},{4,6},{6,4},{1,3},{3,1},{5,7},{7,5},{8,10},{10,8},{12,... | collective-permute-start | bytes 2359304 | tf_op jit(solution)/shard_map/ppermute | solution.py:87
  84.5 33.5 %collective-permute-start.10 = (f16[512,512]{1,0:T(8,128)(2,1)}, f16[512,512]{1,0:T(8,128)(2,1)}, u32[]{:S(2)}, u32[]{:S(2)}) collective-permute-start(f16[512,512]{1,0:T(8,128)(2,1)} %add_convert_fusion), channel_id=1, source_target_pairs={{0,4},{2,6},{4,0},{6,2},{1,5},{3,7},{5,1},{7,3},{8,12},{10,14},{12... | collective-permute-start | bytes 1572872 | tf_op jit(solution)/shard_map/ppermute | solution.py:87
  122.2 13.5 %copy-start.2 = (f16[512,1024]{1,0:T(8,128)(2,1)S(1)}, f16[512,1024]{1,0:T(8,128)(2,1)}, u32[]{:S(2)}) copy-start(f16[512,1024]{1,0:T(8,128)(2,1)} %copy-done.1) | copy-start | bytes 3145732
  122.2 2.9 %collective-permute-start.15 = (bf16[128,4096]{1,0:T(8,128)(2,1)}, bf16[128,4096]{1,0:T(8,128)(2,1)S(1)}, u32[]{:S(2)}, u32[]{:S(2)}) collective-permute-start(bf16[128,4096]{1,0:T(8,128)(2,1)} %collective-permute-done.12), channel_id=1, source_target_pairs={{0,8},{8,0},{16,24},{24,16},{1,9},{9,1},{17,25},{25,17},{2,10},{10... | collective-permute-start | bytes 3145736 | tf_op jit(solution)/shard_map/ppermute | solution.py:87
  122.3 28.3 %collective-permute-start.13 = (f16[384,1024]{1,0:T(8,128)(2,1)}, f16[384,1024]{1,0:T(8,128)(2,1)}, u32[]{:S(2)}, u32[]{:S(2)}) collective-permute-start(f16[384,1024]{1,0:T(8,128)(2,1)} %constant_dynamic-slice_fusion.1), channel_id=1, source_target_pairs={{0,2},{2,0},{4,6},{6,4},{1,3},{3,1},{5,7},{7,5},{8,10},{10,8},{12,... | collective-permute-start | bytes 2359304 | tf_op jit(solution)/shard_map/ppermute | solution.py:87
  122.7 27.9 %collective-permute-start.14 = (f16[384,512]{1,0:T(8,128)(2,1)}, f16[384,512]{1,0:T(8,128)(2,1)S(1)}, u32[]{:S(2)}, u32[]{:S(2)}) collective-permute-start(f16[384,512]{1,0:T(8,128)(2,1)} %add_convert_fusion.3), channel_id=1, source_target_pairs={{0,4},{2,6},{4,0},{6,2},{1,5},{3,7},{5,1},{7,3},{8,12},{10,14},{12... | collective-permute-start | bytes 1179656 | tf_op jit(solution)/shard_map/ppermute | solution.py:87
  152.0 22.9 %collective-permute-start.16 = (f16[256,1024]{1,0:T(8,128)(2,1)S(1)}, f16[256,1024]{1,0:T(8,128)(2,1)S(1)}, u32[]{:S(2)}, u32[]{:S(2)}) collective-permute-start(f16[256,1024]{1,0:T(8,128)(2,1)S(1)} %constant_dynamic-slice_fusion), channel_id=1, source_target_pairs={{0,2},{2,0},{4,6},{6,4},{1,3},{3,1},{5,7},{7,5},{8,10},{10,8},{12,... | collective-permute-start | bytes 1572872 | tf_op jit(solution)/shard_map/ppermute | solution.py:87
  152.8 22.1 %collective-permute-start.17 = (f16[384,512]{1,0:T(8,128)(2,1)S(1)}, f16[384,512]{1,0:T(8,128)(2,1)S(1)}, u32[]{:S(2)}, u32[]{:S(2)}) collective-permute-start(f16[384,512]{1,0:T(8,128)(2,1)S(1)} %add_convert_fusion.2), channel_id=1, source_target_pairs={{0,4},{2,6},{4,0},{6,2},{1,5},{3,7},{5,1},{7,3},{8,12},{10,14},{12... | collective-permute-start | bytes 1179656 | tf_op jit(solution)/shard_map/ppermute | solution.py:87
  175.0 12.6 %collective-permute-start.18 = (f16[256,512]{1,0:T(8,128)(2,1)S(1)}, f16[256,512]{1,0:T(8,128)(2,1)S(1)}, u32[]{:S(2)}, u32[]{:S(2)}) collective-permute-start(f16[256,512]{1,0:T(8,128)(2,1)S(1)} %add_convert_fusion.4), channel_id=1, source_target_pairs={{0,4},{2,6},{4,0},{6,2},{1,5},{3,7},{5,1},{7,3},{8,12},{10,14},{12... | collective-permute-start | bytes 786440 | tf_op jit(solution)/shard_map/ppermute | solution.py:87
  195.8 7.1 %collective-permute-start.19 = (f32[136,512]{1,0:T(8,128)}, f32[136,512]{1,0:T(8,128)S(1)}, u32[]{:S(2)}, u32[]{:S(2)}) collective-permute-start(f32[136,512]{1,0:T(8,128)} %tail_sums.9), channel_id=1, source_target_pairs={{0,1},{1,0},{2,3},{3,2},{4,5},{5,4},{6,7},{7,6},{8,9},{9,8},{10,11... | collective-permute-start | bytes 835592 | tf_op jit(solution)/shard_map/ppermute | solution.py:87
  204.1 9.5 %collective-permute-start.20 = (f32[128,512]{1,0:T(8,128)S(1)}, f32[128,512]{1,0:T(8,128)S(1)}, u32[]{:S(2)}, u32[]{:S(2)}) collective-permute-start(f32[128,512]{1,0:T(8,128)S(1)} %pad_maximum_fusion.1), channel_id=1, source_target_pairs={{0,2},{2,0},{4,6},{6,4},{1,3},{3,1},{5,7},{7,5},{8,10},{10,8},{12,... | collective-permute-start | bytes 786440 | tf_op jit(solution)/shard_map/ppermute | solution.py:87
  205.5 17.8 %collective-permute-start.21 = (f32[128,512]{1,0:T(8,128)S(1)}, f32[128,512]{1,0:T(8,128)S(1)}, u32[]{:S(2)}, u32[]{:S(2)}) collective-permute-start(f32[128,512]{1,0:T(8,128)S(1)} %pad_maximum_fusion.1), channel_id=1, source_target_pairs={{0,4},{2,6},{4,0},{6,2},{1,5},{3,7},{5,1},{7,3},{8,12},{10,14},{12... | collective-permute-start | bytes 786440 | tf_op jit(solution)/shard_map/ppermute | solution.py:87
  206.5 21.3 %collective-permute-start.22 = (f32[128,512]{1,0:T(8,128)S(1)}, f32[128,512]{1,0:T(8,128)S(1)}, u32[]{:S(2)}, u32[]{:S(2)}) collective-permute-start(f32[128,512]{1,0:T(8,128)S(1)} %pad_maximum_fusion.1), channel_id=1, source_target_pairs={{0,6},{2,4},{4,2},{6,0},{1,7},{3,5},{5,3},{7,1},{8,14},{10,12},{12... | collective-permute-start | bytes 786440 | tf_op jit(solution)/shard_map/ppermute | solution.py:87
  (3 other events, 4.5 us)

commit v6 on v5

--- a/solution.py
+++ b/solution.py
@@ -110,7 +110,7 @@
             + last.astype(f32)
         )
 
-    cuts = [0] + [rows * c // 32 for c in (12, 24)] + [rows]
+    cuts = [0] + [rows * c // 32 for c in (12, 23)] + [rows]
     pieces = [slice(i, j) for i, j in zip(cuts, cuts[1:])]
     depth = thresholds.shape[0]
 

time: 231 us -> 243 us (1.052)
  local copies, waits for them, and re-layouts: 14.9 us -> 21.4 us
  waiting for transfers between devices: 57 us -> 61.2 us
    ppermute x23, waiting for transfers between devices: 57 us -> 61.2 us  [swap(): lax.ppermute(v, axis, [(i, i ^ flip) for i in range(lax.axis_size(axis))])]
    reshape x3, local copies, waits for them, and re-layouts: 0.17 us -> 3.28 us  [pipelined(): parts += [far_weights[:, piece].reshape(-1) for piece in pieces]]
  transfers between devices with their start and end apart: 23 -> 23, of which waited for: 11 -> 13; matrix products, arithmetic and copies ran while one was open for 37% -> 37% of each run, Pallas kernels for 19% -> 18%
where the time goes in v6:
time: 243 us; the launch traced here: 242 us
  matrix products  62.3 us (26%)
  waiting for transfers between devices  61.2 us (25%)
  Pallas kernels  52.2 us (21%)
  starting transfers between devices  22.3 us (9%)
  local copies, waits for them, and re-layouts  21.4 us (9%)
  other arithmetic  20.8 us (9%)
    dot_general x6, matrix products, product(): jnp.dot(block, factors, preferred_element_type=f32) * half_inverse  62.3 us
    ppermute x23, waiting for transfers between devices, swap(): lax.ppermute(v, axis, [(i, i ^ flip) for i in range(lax.axis_size(axis))])  61.2 us
    pallas_call x5, Pallas kernels, tail_sums(): pl.pallas_call(functools.partial(tail_body, first), out_shape=jax.ShapeDt...  52.2 us
    ppermute x23, starting transfers between devices, swap(): lax.ppermute(v, axis, [(i, i ^ flip) for i in range(lax.axis_size(axis))])  22.3 us
    add x5, other arithmetic, finish(): kept(partial, high).astype(f32) + columns(got, high, quarter).astype(f32)  10.4 us
    convert_element_type x5, other arithmetic, send_b(): (kept(partial, 1 - high).astype(f32) + columns(got, 1 - high, quarter).as...  6.82 us
    dynamic_slice x4, local copies, waits for them, and re-layouts, columns(): return lax.dynamic_slice_in_dim(v, k * width, width, 1)  5.7 us
  transfers between devices with their start and end apart: 23, of which 13 were waited for; matrix products, arithmetic and copies ran while one was open for 37% of the time, Pallas kernels for 18%

profile of v6, /device:TPU:8, one launch (start us, length us, event | category | flops | bytes accessed | tf_op | source)
XLA Modules:
  0.0 242.2 jit_solution(1513175747161124651)
XLA Ops:
  0.7 2.8 %slice.33 = bf16[192,4096]{1,0:T(8,128)(2,1)} slice(bf16[512,4096]{1,0:T(8,128)(2,1)} %param.4), slice={[0:192], [0:4096]} | slice | bytes 3145728 | tf_op jit(solution)/shard_map/slice | solution.py:121
  5.2 10.1 %fusion.24 = f16[512,1024]{1,0:T(8,128)(2,1)} fusion(bf16[512,4096]{1,0:T(8,128)(2,1)} %param.4, bf16[4096,2048]{1,0:T(8,128)(2,1)} %param.5, s32[]{:T(128)S(6)} %select_n.108), kind=kOutput, calls=%fused_computation.22 | convolution fusion | flops 4296015872 | bytes 13631492 | tf_op jit(solution)/shard_map/dot_general | solution.py:93
  16.0 9.4 %fusion.27 = f16[512,1024]{1,0:T(8,128)(2,1)S(1)} fusion(bf16[512,4096]{1,0:T(8,128)(2,1)} %param.4, bf16[4096,2048]{1,0:T(8,128)(2,1)} %param.5, s32[]{:T(128)S(6)} %select_n.109), kind=kOutput, calls=%fused_computation.23 | convolution fusion | flops 4296015872 | bytes 13631492 | tf_op jit(solution)/shard_map/dot_general | solution.py:93
  25.5 11.4 %multiply_convert_fusion = f16[512,2048]{1,0:T(8,128)(2,1)S(1)} fusion(bf16[512,4096]{1,0:T(8,128)(2,1)} %collective-permute-done, bf16[4096,2048]{1,0:T(8,128)(2,1)S(1)} %bitcast.18), kind=kOutput, calls=%fused_computation.4 | convolution fusion | flops 8592031744 | bytes 23068672 | tf_op jit(solution)/shard_map/dot_general | solution.py:93
  38.3 2.3 collective-permute-done.2
  45.0 2.6 %collective-permute-start.5 = (f16[512,512]{1,0:T(8,128)(2,1)}, f16[512,512]{1,0:T(8,128)(2,1)S(1)}, u32[]{:S(2)}, u32[]{:S(2)}) collective-permute-start(f16[512,512]{1,0:T(8,128)(2,1)} %add_convert_fusion.1), channel_id=1, source_target_pairs={{0,4},{2,6},{4,0},{6,2},{1,5},{3,7},{5,1},{7,3},{8,12},{10,14},{12... | collective-permute-start | bytes 1572872 | tf_op jit(solution)/shard_map/ppermute | solution.py:87
  48.6 11.1 %multiply_convert_fusion.1 = f16[384,2048]{1,0:T(8,128)(2,1)S(1)} fusion(bf16[4096,2048]{1,0:T(8,128)(2,1)} %param.5, bf16[192,4096]{1,0:T(8,128)(2,1)} %collective-permute-done.6, bf16[192,4096]{1,0:T(8,128)(2,1)} %collective-permute-done.2), kind=kOutput, calls=%fused_computation.9 | convolution fusion | flops 6450315264 | bytes 21495808 | tf_op jit(solution)/shard_map/dot_general | solution.py:93
  59.7 1.7 dynamic-slice_multiply_fusion.levels
  61.4 2.4 slice.35
  63.8 13.8 %collective-permute-done.8 = bf16[2,512]{1,0:T(2,128)(2,1)S(1)} collective-permute-done((bf16[2,512]{1,0:T(2,128)(2,1)S(1)}, bf16[2,512]{1,0:T(2,128)(2,1)S(1)}, u32[]{:S(2)}, u32[]{:S(2)}) %collective-permute-start.8) | collective-permute-done | bytes 2080 | tf_op jit(solution)/shard_map/ppermute | solution.py:87
  77.6 4.6 %collective-permute-done.5 = f16[512,512]{1,0:T(8,128)(2,1)S(1)} collective-permute-done((f16[512,512]{1,0:T(8,128)(2,1)}, f16[512,512]{1,0:T(8,128)(2,1)S(1)}, u32[]{:S(2)}, u32[]{:S(2)}) %collective-permute-start.5) | collective-permute-done | bytes 524320 | tf_op jit(solution)/shard_map/ppermute | solution.py:87
  85.7 1.9 collective-permute-start.10
  88.1 10.5 %fusion.13 = f16[352,2048]{1,0:T(8,128)(2,1)S(1)} fusion(bf16[4096,2048]{1,0:T(8,128)(2,1)} %param.5, bf16[176,4096]{1,0:T(8,128)(2,1)} %collective-permute-done.11, bf16[176,4096]{1,0:T(8,128)(2,1)} %collective-permute-done.7), kind=kOutput, calls=%fused_computation.15 | convolution fusion | flops 5912788992 | bytes 21102592 | tf_op jit(solution)/shard_map/dot_general | solution.py:93
  106.9 2.6 %convert_add_fusion.1.losses = f32[512,512]{1,0:T(8,128)} fusion(f16[512,512]{1,0:T(8,128)(2,1)} %copy-done.6, f16[512,1024]{1,0:T(8,128)(2,1)} %copy-done.4, s32[]{:T(128)S(6)} %select_n.114, f16[512,1024]{1,0:T(8,128)(2,1)} %copy-done.5), kind=kLoop, calls=%fused_computation.26 | loop fusion | flops 1310720 | bytes 2621444 | tf_op jit(solution)/shard_map/add | solution.py:108
  110.8 12.2 %tail_sums.5.sums_in = f32[136,512]{1,0:T(8,128)} custom-call(f32[512,512]{1,0:T(8,128)} %convert_add_fusion.1.losses, f32[64,512]{1,0:T(8,128)} %dynamic-slice_multiply_fusion.levels, bf16[8,2048]{1,0:T(8,128)(2,1)} %broadcast_in_dim.4.weights, f32[136,512]{1,0:T(8,128)} %concatenate.27.sums_in), custom_call_target="tpu_custom_call", output_to_operand_aliasing={{}: (3, {})} | custom-call | flops 1024 | bytes 1024 | tf_op jit(solution)/shard_map/tail_sums/pallas_call | solution.py:58
  124.1 2.0 add_convert_fusion.2
  129.2 9.8 %fusion.16 = f16[288,2048]{1,0:T(8,128)(2,1)} fusion(bf16[4096,2048]{1,0:T(8,128)(2,1)} %param.5, bf16[144,4096]{1,0:T(8,128)(2,1)S(1)} %collective-permute-done.15, bf16[144,4096]{1,0:T(8,128)(2,1)} %collective-permute-done.12), kind=kOutput, calls=%fused_computation.16 | convolution fusion | flops 4837736448 | bytes 20316160 | tf_op jit(solution)/shard_map/dot_general | solution.py:93
  138.9 2.4 %convert_add_fusion.losses = f32[512,512]{1,0:T(8,128)} fusion(f16[512,512]{1,0:T(8,128)(2,1)} %collective-permute-done.10, f16[512,1024]{1,0:T(8,128)(2,1)S(1)} %copy-done.3, s32[]{:T(128)S(6)} %select_n.114, f16[512,2048]{1,0:T(8,128)(2,1)S(1)} %multiply_convert_fusion, s32[]{:T(128)S(6)} %select_n.112), kind=kLoop, calls=%fused_computation.25 | loop fusion | flops 1310720 | bytes 2621448 | tf_op jit(solution)/shard_map/add | solution.py:108
  141.4 12.2 %tail_sums.6.sums_in = f32[136,512]{1,0:T(8,128)} custom-call(f32[512,512]{1,0:T(8,128)} %convert_add_fusion.losses, f32[64,512]{1,0:T(8,128)} %dynamic-slice_multiply_fusion.levels, bf16[8,2048]{1,0:T(8,128)(2,1)} %broadcast_in_dim.4.weights, f32[136,512]{1,0:T(8,128)} %tail_sums.5.sums_in), custom_call_target="tpu_custom_call", output_to_operand_aliasing={{}: (3, {})} | custom-call | flops 1024 | bytes 1024 | tf_op jit(solution)/shard_map/tail_sums/pallas_call | solution.py:58
  153.8 2.1 constant_dynamic-slice_fusion
  155.9 1.9 add_convert_fusion.3
  160.3 2.3 convert_add_fusion.2.losses
  162.5 9.6 %tail_sums.7.sums_in = f32[136,512]{1,0:T(8,128)} custom-call(f32[384,512]{1,0:T(8,128)} %convert_add_fusion.2.losses, f32[64,512]{1,0:T(8,128)} %dynamic-slice_multiply_fusion.levels, bf16[8,2048]{1,0:T(8,128)(2,1)} %broadcast_in_dim.4.weights, f32[136,512]{1,0:T(8,128)} %tail_sums.6.sums_in), custom_call_target="tpu_custom_call", output_to_operand_aliasing={{}: (3, {})} | custom-call | flops 1024 | bytes 1024 | tf_op jit(solution)/shard_map/tail_sums/pallas_call | solution.py:58
  172.2 9.2 %collective-permute-done.17 = f16[352,512]{1,0:T(8,128)(2,1)} collective-permute-done((f16[352,512]{1,0:T(8,128)(2,1)}, f16[352,512]{1,0:T(8,128)(2,1)}, u32[]{:S(2)}, u32[]{:S(2)}) %collective-permute-start.17) | collective-permute-done | bytes 360480 | tf_op jit(solution)/shard_map/ppermute | solution.py:87
  183.4 2.1 convert_add_fusion.3.losses
  185.5 9.2 %tail_sums.8.sums_in = f32[136,512]{1,0:T(8,128)} custom-call(f32[352,512]{1,0:T(8,128)} %convert_add_fusion.3.losses, f32[64,512]{1,0:T(8,128)} %dynamic-slice_multiply_fusion.levels, bf16[8,2048]{1,0:T(8,128)(2,1)} %broadcast_in_dim.4.weights, f32[136,512]{1,0:T(8,128)} %tail_sums.7.sums_in), custom_call_target="tpu_custom_call", output_to_operand_aliasing={{}: (3, {})} | custom-call | flops 1024 | bytes 1024 | tf_op jit(solution)/shard_map/tail_sums/pallas_call | solution.py:58
  196.7 9.0 %tail_sums.9 = f32[136,512]{1,0:T(8,128)} custom-call(f32[288,512]{1,0:T(8,128)} %convert_add_fusion.4.losses, f32[64,512]{1,0:T(8,128)} %dynamic-slice_multiply_fusion.levels, bf16[8,2048]{1,0:T(8,128)(2,1)} %broadcast_in_dim.4.weights, f32[136,512]{1,0:T(8,128)} %tail_sums.8.sums_in), custom_call_target="tpu_custom_call", output_to_operand_aliasing={{}: (3, {})} | custom-call | flops 1024 | bytes 1024 | tf_op jit(solution)/shard_map/tail_sums/pallas_call | solution.py:58
  207.2 6.6 %collective-permute-done.19 = f32[136,512]{1,0:T(8,128)S(1)} collective-permute-done((f32[136,512]{1,0:T(8,128)}, f32[136,512]{1,0:T(8,128)S(1)}, u32[]{:S(2)}, u32[]{:S(2)}) %collective-permute-start.19) | collective-permute-done | bytes 278560 | tf_op jit(solution)/shard_map/ppermute | solution.py:87
  214.9 2.9 %collective-permute-start.20 = (f32[128,512]{1,0:T(8,128)S(1)}, f32[128,512]{1,0:T(8,128)S(1)}, u32[]{:S(2)}, u32[]{:S(2)}) collective-permute-start(f32[128,512]{1,0:T(8,128)S(1)} %pad_maximum_fusion.1), channel_id=1, source_target_pairs={{0,2},{2,0},{4,6},{6,4},{1,3},{3,1},{5,7},{7,5},{8,10},{10,8},{12,... | collective-permute-start | bytes 786440 | tf_op jit(solution)/shard_map/ppermute | solution.py:87
  219.4 6.9 %collective-permute-done.20 = f32[128,512]{1,0:T(8,128)S(1)} collective-permute-done((f32[128,512]{1,0:T(8,128)S(1)}, f32[128,512]{1,0:T(8,128)S(1)}, u32[]{:S(2)}, u32[]{:S(2)}) %collective-permute-start.20) | collective-permute-done | bytes 262176 | tf_op jit(solution)/shard_map/ppermute | solution.py:87
  226.2 10.1 %collective-permute-done.21 = f32[128,512]{1,0:T(8,128)S(1)} collective-permute-done((f32[128,512]{1,0:T(8,128)S(1)}, f32[128,512]{1,0:T(8,128)S(1)}, u32[]{:S(2)}, u32[]{:S(2)}) %collective-permute-start.21) | collective-permute-done | bytes 262176 | tf_op jit(solution)/shard_map/ppermute | solution.py:87
  236.4 4.6 %collective-permute-done.22 = f32[128,512]{1,0:T(8,128)S(1)} collective-permute-done((f32[128,512]{1,0:T(8,128)S(1)}, f32[128,512]{1,0:T(8,128)S(1)}, u32[]{:S(2)}, u32[]{:S(2)}) %collective-permute-start.22) | collective-permute-done | bytes 262176 | tf_op jit(solution)/shard_map/ppermute | solution.py:87
  (91 shorter events, 37.8 us)
Async XLA Ops:
  0.6 4.4 %copy-start.7 = (bf16[512]{0:T(512)(128)(2,1)S(1)}, bf16[512]{0:T(512)(128)(2,1)}, u32[]{:S(2)}) copy-start(bf16[512]{0:T(512)(128)(2,1)} %param.7) | copy-start | bytes 3076
  0.6 14.8 %collective-permute-start = (bf16[512,4096]{1,0:T(8,128)(2,1)}, bf16[512,4096]{1,0:T(8,128)(2,1)}, u32[]{:S(2)}, u32[]{:S(2)}) collective-permute-start(bf16[512,4096]{1,0:T(8,128)(2,1)} %param.4), channel_id=1, source_target_pairs={{0,8},{8,0},{16,24},{24,16},{1,9},{9,1},{17,25},{25,17},{2,10},{10... | collective-permute-start | bytes 12582920 | tf_op jit(solution)/shard_map/ppermute | solution.py:87
  3.5 37.1 %collective-permute-start.2 = (bf16[192,4096]{1,0:T(8,128)(2,1)}, bf16[192,4096]{1,0:T(8,128)(2,1)}, u32[]{:S(2)}, u32[]{:S(2)}) collective-permute-start(bf16[192,4096]{1,0:T(8,128)(2,1)} %slice.33), channel_id=1, source_target_pairs={{0,16},{8,24},{16,0},{24,8},{1,17},{9,25},{17,1},{25,9},{2,18},{10... | collective-permute-start | bytes 4718600 | tf_op jit(solution)/shard_map/ppermute | solution.py:87
  5.0 10.4 %collective-permute-start.3 = (bf16[512]{0:T(512)(128)(2,1)S(1)}, bf16[512]{0:T(512)(128)(2,1)S(1)}, u32[]{:S(2)}, u32[]{:S(2)}) collective-permute-start(bf16[512]{0:T(512)(128)(2,1)S(1)} %copy-done.7), channel_id=1, source_target_pairs={{0,8},{8,0},{16,24},{24,16},{1,9},{9,1},{17,25},{25,17},{2,10},{10... | collective-permute-start | bytes 3080 | tf_op jit(solution)/shard_map/ppermute | solution.py:87
  15.4 10.0 %slice-start = ((s8[16777216]{0:T(1024)(128)(4,1)}), s8[4194304]{0:T(1024)(128)(4,1)S(1)}, s32[]{:S(2)}) async-start(s8[16777216]{0:T(1024)(128)(4,1)} %bitcast.17), calls=%async_computation | async-start | bytes 8388608
  15.4 10.0 %slice-start.1 = ((s8[16777216]{0:T(1024)(128)(4,1)}), s8[4194304]{0:T(1024)(128)(4,1)S(1)}, s32[]{:S(2)}) async-start(s8[16777216]{0:T(1024)(128)(4,1)} %bitcast.17), calls=%async_computation.1 | async-start | bytes 8388608
  15.4 10.0 %slice-start.2 = ((s8[16777216]{0:T(1024)(128)(4,1)}), s8[4194304]{0:T(1024)(128)(4,1)S(1)}, s32[]{:S(2)}) async-start(s8[16777216]{0:T(1024)(128)(4,1)} %bitcast.17), calls=%async_computation.2 | async-start | bytes 8388608
  15.5 10.0 %slice-start.3 = ((s8[16777216]{0:T(1024)(128)(4,1)}), s8[4194304]{0:T(1024)(128)(4,1)S(1)}, s32[]{:S(2)}) async-start(s8[16777216]{0:T(1024)(128)(4,1)} %bitcast.17), calls=%async_computation.3 | async-start | bytes 8388608
  15.5 25.6 %collective-permute-start.1 = (f16[512,1024]{1,0:T(8,128)(2,1)}, f16[512,1024]{1,0:T(8,128)(2,1)S(1)}, u32[]{:S(2)}, u32[]{:S(2)}) collective-permute-start(f16[512,1024]{1,0:T(8,128)(2,1)} %fusion.24), channel_id=1, source_target_pairs={{0,2},{2,0},{4,6},{6,4},{1,3},{3,1},{5,7},{7,5},{8,10},{10,8},{12,... | collective-permute-start | bytes 3145736 | tf_op jit(solution)/shard_map/ppermute | solution.py:87
  25.5 17.0 %copy-start.5 = (f16[512,1024]{1,0:T(8,128)(2,1)}, f16[512,1024]{1,0:T(8,128)(2,1)S(1)}, u32[]{:S(2)}) copy-start(f16[512,1024]{1,0:T(8,128)(2,1)S(1)} %fusion.27) | copy-start | bytes 3145732
  43.5 5.1 %collective-permute-start.6 = (bf16[192,4096]{1,0:T(8,128)(2,1)}, bf16[192,4096]{1,0:T(8,128)(2,1)}, u32[]{:S(2)}, u32[]{:S(2)}) collective-permute-start(bf16[192,4096]{1,0:T(8,128)(2,1)} %collective-permute-done.2), channel_id=1, source_target_pairs={{0,8},{8,0},{16,24},{24,16},{1,9},{9,1},{17,25},{25,17},{2,10},{10... | collective-permute-start | bytes 4718600 | tf_op jit(solution)/shard_map/ppermute | solution.py:87
  43.5 38.8 %collective-permute-start.7 = (bf16[176,4096]{1,0:T(8,128)(2,1)S(1)}, bf16[176,4096]{1,0:T(8,128)(2,1)}, u32[]{:S(2)}, u32[]{:S(2)}) collective-permute-start(bf16[176,4096]{1,0:T(8,128)(2,1)S(1)} %slice.34), channel_id=1, source_target_pairs={{0,16},{8,24},{16,0},{24,8},{1,17},{9,25},{17,1},{25,9},{2,18},{10... | collective-permute-start | bytes 4325384 | tf_op jit(solution)/shard_map/ppermute | solution.py:87
  44.5 37.8 %collective-permute-start.4 = (f16[512,1024]{1,0:T(8,128)(2,1)}, f16[512,1024]{1,0:T(8,128)(2,1)S(1)}, u32[]{:S(2)}, u32[]{:S(2)}) collective-permute-start(f16[512,1024]{1,0:T(8,128)(2,1)} %constant_dynamic-slice_fusion.3), channel_id=1, source_target_pairs={{0,2},{2,0},{4,6},{6,4},{1,3},{3,1},{5,7},{7,5},{8,10},{10,8},{12,... | collective-permute-start | bytes 3145736 | tf_op jit(solution)/shard_map/ppermute | solution.py:87
  45.0 37.3 %collective-permute-start.5 = (f16[512,512]{1,0:T(8,128)(2,1)}, f16[512,512]{1,0:T(8,128)(2,1)S(1)}, u32[]{:S(2)}, u32[]{:S(2)}) collective-permute-start(f16[512,512]{1,0:T(8,128)(2,1)} %add_convert_fusion.1), channel_id=1, source_target_pairs={{0,4},{2,6},{4,0},{6,2},{1,5},{3,7},{5,1},{7,3},{8,12},{10,14},{12... | collective-permute-start | bytes 1572872 | tf_op jit(solution)/shard_map/ppermute | solution.py:87
  47.6 30.1 %collective-permute-start.8 = (bf16[2,512]{1,0:T(2,128)(2,1)S(1)}, bf16[2,512]{1,0:T(2,128)(2,1)S(1)}, u32[]{:S(2)}, u32[]{:S(2)}) collective-permute-start(bf16[2,512]{1,0:T(2,128)(2,1)S(1)} %pad_maximum_fusion.2), channel_id=1, source_target_pairs={{0,16},{8,24},{16,0},{24,8},{1,17},{9,25},{17,1},{25,9},{2,18},{10... | collective-permute-start | bytes 6152 | tf_op jit(solution)/shard_map/ppermute | solution.py:87
  59.7 24.9 %copy-start = (f16[384,2048]{1,0:T(8,128)(2,1)}, f16[384,2048]{1,0:T(8,128)(2,1)S(1)}, u32[]{:S(2)}) copy-start(f16[384,2048]{1,0:T(8,128)(2,1)S(1)} %multiply_convert_fusion.1) | copy-start | bytes 4718596
  84.6 3.6 %collective-permute-start.11 = (bf16[176,4096]{1,0:T(8,128)(2,1)}, bf16[176,4096]{1,0:T(8,128)(2,1)}, u32[]{:S(2)}, u32[]{:S(2)}) collective-permute-start(bf16[176,4096]{1,0:T(8,128)(2,1)} %collective-permute-done.7), channel_id=1, source_target_pairs={{0,8},{8,0},{16,24},{24,16},{1,9},{9,1},{17,25},{25,17},{2,10},{10... | collective-permute-start | bytes 4325384 | tf_op jit(solution)/shard_map/ppermute | solution.py:87
  84.6 38.5 %collective-permute-start.12 = (bf16[144,4096]{1,0:T(8,128)(2,1)}, bf16[144,4096]{1,0:T(8,128)(2,1)}, u32[]{:S(2)}, u32[]{:S(2)}) collective-permute-start(bf16[144,4096]{1,0:T(8,128)(2,1)} %slice.35), channel_id=1, source_target_pairs={{0,16},{8,24},{16,0},{24,8},{1,17},{9,25},{17,1},{25,9},{2,18},{10... | collective-permute-start | bytes 3538952 | tf_op jit(solution)/shard_map/ppermute | solution.py:87
  85.7 37.4 %collective-permute-start.9 = (f16[384,1024]{1,0:T(8,128)(2,1)}, f16[384,1024]{1,0:T(8,128)(2,1)}, u32[]{:S(2)}, u32[]{:S(2)}) collective-permute-start(f16[384,1024]{1,0:T(8,128)(2,1)} %constant_dynamic-slice_fusion.2), channel_id=1, source_target_pairs={{0,2},{2,0},{4,6},{6,4},{1,3},{3,1},{5,7},{7,5},{8,10},{10,8},{12,... | collective-permute-start | bytes 2359304 | tf_op jit(solution)/shard_map/ppermute | solution.py:87
  85.7 37.4 %collective-permute-start.10 = (f16[512,512]{1,0:T(8,128)(2,1)}, f16[512,512]{1,0:T(8,128)(2,1)}, u32[]{:S(2)}, u32[]{:S(2)}) collective-permute-start(f16[512,512]{1,0:T(8,128)(2,1)} %add_convert_fusion), channel_id=1, source_target_pairs={{0,4},{2,6},{4,0},{6,2},{1,5},{3,7},{5,1},{7,3},{8,12},{10,14},{12... | collective-permute-start | bytes 1572872 | tf_op jit(solution)/shard_map/ppermute | solution.py:87
  126.1 12.8 %copy-start.3 = (f16[512,1024]{1,0:T(8,128)(2,1)S(1)}, f16[512,1024]{1,0:T(8,128)(2,1)}, u32[]{:S(2)}) copy-start(f16[512,1024]{1,0:T(8,128)(2,1)} %copy-done.2) | copy-start | bytes 3145732
  126.1 3.1 %collective-permute-start.15 = (bf16[144,4096]{1,0:T(8,128)(2,1)}, bf16[144,4096]{1,0:T(8,128)(2,1)S(1)}, u32[]{:S(2)}, u32[]{:S(2)}) collective-permute-start(bf16[144,4096]{1,0:T(8,128)(2,1)} %collective-permute-done.12), channel_id=1, source_target_pairs={{0,8},{8,0},{16,24},{24,16},{1,9},{9,1},{17,25},{25,17},{2,10},{10... | collective-permute-start | bytes 3538952 | tf_op jit(solution)/shard_map/ppermute | solution.py:87
  126.2 27.6 %collective-permute-start.13 = (f16[352,1024]{1,0:T(8,128)(2,1)}, f16[352,1024]{1,0:T(8,128)(2,1)}, u32[]{:S(2)}, u32[]{:S(2)}) collective-permute-start(f16[352,1024]{1,0:T(8,128)(2,1)} %constant_dynamic-slice_fusion.1), channel_id=1, source_target_pairs={{0,2},{2,0},{4,6},{6,4},{1,3},{3,1},{5,7},{7,5},{8,10},{10,8},{12,... | collective-permute-start | bytes 2162696 | tf_op jit(solution)/shard_map/ppermute | solution.py:87
  127.3 26.6 %collective-permute-start.14 = (f16[384,512]{1,0:T(8,128)(2,1)}, f16[384,512]{1,0:T(8,128)(2,1)}, u32[]{:S(2)}, u32[]{:S(2)}) collective-permute-start(f16[384,512]{1,0:T(8,128)(2,1)} %add_convert_fusion.2), channel_id=1, source_target_pairs={{0,4},{2,6},{4,0},{6,2},{1,5},{3,7},{5,1},{7,3},{8,12},{10,14},{12... | collective-permute-start | bytes 1179656 | tf_op jit(solution)/shard_map/ppermute | solution.py:87
  153.6 27.8 %copy-start.1 = (f16[288,2048]{1,0:T(8,128)(2,1)S(1)}, f16[288,2048]{1,0:T(8,128)(2,1)}, u32[]{:S(2)}) copy-start(f16[288,2048]{1,0:T(8,128)(2,1)} %fusion.16) | copy-start | bytes 3538948
  157.8 23.6 %collective-permute-start.16 = (f16[288,1024]{1,0:T(8,128)(2,1)}, f16[288,1024]{1,0:T(8,128)(2,1)S(1)}, u32[]{:S(2)}, u32[]{:S(2)}) collective-permute-start(f16[288,1024]{1,0:T(8,128)(2,1)} %constant_dynamic-slice_fusion), channel_id=1, source_target_pairs={{0,2},{2,0},{4,6},{6,4},{1,3},{3,1},{5,7},{7,5},{8,10},{10,8},{12,... | collective-permute-start | bytes 1769480 | tf_op jit(solution)/shard_map/ppermute | solution.py:87
  158.8 22.7 %collective-permute-start.17 = (f16[352,512]{1,0:T(8,128)(2,1)}, f16[352,512]{1,0:T(8,128)(2,1)}, u32[]{:S(2)}, u32[]{:S(2)}) collective-permute-start(f16[352,512]{1,0:T(8,128)(2,1)} %add_convert_fusion.3), channel_id=1, source_target_pairs={{0,4},{2,6},{4,0},{6,2},{1,5},{3,7},{5,1},{7,3},{8,12},{10,14},{12... | collective-permute-start | bytes 1081352 | tf_op jit(solution)/shard_map/ppermute | solution.py:87
  182.3 13.4 %collective-permute-start.18 = (f16[288,512]{1,0:T(8,128)(2,1)}, f16[288,512]{1,0:T(8,128)(2,1)S(1)}, u32[]{:S(2)}, u32[]{:S(2)}) collective-permute-start(f16[288,512]{1,0:T(8,128)(2,1)} %add_convert_fusion.4), channel_id=1, source_target_pairs={{0,4},{2,6},{4,0},{6,2},{1,5},{3,7},{5,1},{7,3},{8,12},{10,14},{12... | collective-permute-start | bytes 884744 | tf_op jit(solution)/shard_map/ppermute | solution.py:87
  205.7 8.1 %collective-permute-start.19 = (f32[136,512]{1,0:T(8,128)}, f32[136,512]{1,0:T(8,128)S(1)}, u32[]{:S(2)}, u32[]{:S(2)}) collective-permute-start(f32[136,512]{1,0:T(8,128)} %tail_sums.9), channel_id=1, source_target_pairs={{0,1},{1,0},{2,3},{3,2},{4,5},{5,4},{6,7},{7,6},{8,9},{9,8},{10,11... | collective-permute-start | bytes 835592 | tf_op jit(solution)/shard_map/ppermute | solution.py:87
  214.9 11.3 %collective-permute-start.20 = (f32[128,512]{1,0:T(8,128)S(1)}, f32[128,512]{1,0:T(8,128)S(1)}, u32[]{:S(2)}, u32[]{:S(2)}) collective-permute-start(f32[128,512]{1,0:T(8,128)S(1)} %pad_maximum_fusion.1), channel_id=1, source_target_pairs={{0,2},{2,0},{4,6},{6,4},{1,3},{3,1},{5,7},{7,5},{8,10},{10,8},{12,... | collective-permute-start | bytes 786440 | tf_op jit(solution)/shard_map/ppermute | solution.py:87
  217.8 18.5 %collective-permute-start.21 = (f32[128,512]{1,0:T(8,128)S(1)}, f32[128,512]{1,0:T(8,128)S(1)}, u32[]{:S(2)}, u32[]{:S(2)}) collective-permute-start(f32[128,512]{1,0:T(8,128)S(1)} %pad_maximum_fusion.1), channel_id=1, source_target_pairs={{0,4},{2,6},{4,0},{6,2},{1,5},{3,7},{5,1},{7,3},{8,12},{10,14},{12... | collective-permute-start | bytes 786440 | tf_op jit(solution)/shard_map/ppermute | solution.py:87
  218.4 22.5 %collective-permute-start.22 = (f32[128,512]{1,0:T(8,128)S(1)}, f32[128,512]{1,0:T(8,128)S(1)}, u32[]{:S(2)}, u32[]{:S(2)}) collective-permute-start(f32[128,512]{1,0:T(8,128)S(1)} %pad_maximum_fusion.1), channel_id=1, source_target_pairs={{0,6},{2,4},{4,2},{6,0},{1,7},{3,5},{5,3},{7,1},{8,14},{10,12},{12... | collective-permute-start | bytes 786440 | tf_op jit(solution)/shard_map/ppermute | solution.py:87
  (3 other events, 4.9 us)
